TPU v7x, 32 devices: a whole 2x2x4 slice. The times are simulated.
32 devices in a mesh: grp: 2 (over core), tm: 16 (over z, y, x).
Axes of the slice: x: 2, y: 2, z: 4, core: 2. Of those that a mesh axis runs over, the one named last changes fastest.
Arguments:
- x_start: float32 [512, 128], P(('grp', 'tm')), may hold values from -3 to 3
- y_start: float32 [512, 128], P('tm'), may hold values from 0 to 1
- cost: float32 [512, 128], P(('grp', 'tm')), may hold values from -6 to 6
- rhs: float32 [512, 128], P('tm'), may hold values from -6 to 6
- tiles: float32 [2048, 128, 128], P(('grp', 'tm')), may hold values from -0.375 to 0.375
- tile_rows: int32 [2048], P(('grp', 'tm')), may hold values from 0 to 511, as said below
- tile_cols: int32 [2048], P(('grp', 'tm')), may hold values from 0 to 511, as said below
- tile_count: int32 [32], P(('grp', 'tm')), may hold values from 1 to 64, as said below
- var_class: int32 [512, 128], P(('grp', 'tm')), may hold values from 0 to 7
- lower_table: float32 [8], replicated, may hold values from -1 to -0.2
- upper_table: float32 [8], replicated, may hold values from 0.2 to 1
Outputs:
- primal: float32 [512, 128], P(('grp', 'tm'))
- dual: float32 [512, 128], P('tm')
- primal_mean: float32 [512, 128], P(('grp', 'tm'))
- dual_mean: float32 [512, 128], P('tm')
Inputs may be any that keep to these rules, and one draw needn't show every extreme that they name: `tile_cols`: the tile slots of device d (slots d * 64 to (d + 1) * 64 - 1) name only that device's own column blocks d * 16 to (d + 1) * 16 - 1. `tile_rows`: the tile slots of device d = g * 16 + t name only row blocks of time blocks t - 1, t and t + 1 (rows k * 32 to (k + 1) * 32 - 1 belong to time block k). Only the first tile_count[d] slots of device d are live; some device has all 64 slots live.
All inputs are finite; a program needn't handle non-finite values.
Results may differ from a plain program's by a relative error of at most 0.0001.
Values sent between devices are 32-bit elements; how exact they have to be, the bound alone decides.
No kernel may reach another device: no remote copies, remote signals or barrier semaphores. Data moves between devices by JAX's collectives and lax.ppermute only.
A program may use at most 64 MiB of HBM per device.

v0:
```python
import jax
import jax.numpy as jnp
from jax import lax
from jax.sharding import PartitionSpec as P

ITERS = 2


primal_step = 0.6
dual_step = 0.6


def with_halo(block, sides, width):
    for axis, dim in sides:
        count = lax.axis_size(axis)
        forward = [(i, i + 1) for i in range(count - 1)]
        backward = [(target, source) for source, target in forward]
        low = lax.ppermute(
            lax.slice_in_dim(block, block.shape[dim] - width, None, axis=dim), axis, forward
        )
        high = lax.ppermute(lax.slice_in_dim(block, 0, width, axis=dim), axis, backward)
        block = jnp.concatenate([low, block, high], axis=dim)
    return block


def shifted(block, axis, distance):
    devices = range(lax.axis_size(axis))
    route = [(i - distance, i) for i in devices if i - distance in devices]
    return lax.ppermute(block, axis, route)


def dual_update(dual_part, rhs_part, image_part):
    return jnp.maximum(dual_part + dual_step * (rhs_part - image_part), 0.0)


def body(
    x_start,
    y_start,
    cost,
    rhs,
    tiles,
    tile_rows,
    tile_cols,
    tile_count,
    var_class,
    lower_table,
    upper_table,
):
    tile_total = tiles.shape[0]
    col_blocks = x_start.shape[0]
    row_blocks = y_start.shape[0]
    time_devices = lax.axis_size("tm")
    time_index = lax.axis_index("tm")
    device_index = lax.axis_index("grp") * time_devices + time_index
    local_cols = tile_cols - device_index * col_blocks
    live_mask = (jnp.arange(tile_total) < tile_count[0]).astype(jnp.float32)[:, None]
    col_select = (local_cols[:, None] == jnp.arange(col_blocks)[None, :]).astype(jnp.float32)
    lower_bound = jnp.zeros(x_start.shape, jnp.float32)
    upper_bound = jnp.zeros(x_start.shape, jnp.float32)
    for class_id in range(lower_table.shape[0]):
        lower_bound = jnp.where(var_class == class_id, lower_table[class_id], lower_bound)
        upper_bound = jnp.where(var_class == class_id, upper_table[class_id], upper_bound)
    window_first = (time_index - 1) * row_blocks
    row_select = (
        (tile_rows - window_first)[:, None] == jnp.arange(3 * row_blocks)[None, :]
    ).astype(jnp.float32)
    dual_view = with_halo(y_start, (("tm", 0),), row_blocks)
    primal = x_start
    dual = y_start
    primal_total = jnp.zeros_like(x_start)
    dual_total = jnp.zeros_like(y_start)
    for iteration in range(ITERS):
        dual_picked = jnp.dot(row_select, dual_view, precision=lax.Precision.HIGHEST)
        backward = (
            jnp.einsum("nrc,nr->nc", tiles, dual_picked, precision=lax.Precision.HIGHEST)
            * live_mask
        )
        adjoint_part = jnp.dot(col_select.T, backward, precision=lax.Precision.HIGHEST)
        moved = primal - primal_step * (cost - adjoint_part)
        primal_next = jnp.minimum(jnp.maximum(moved, lower_bound), upper_bound)
        extrapolated = 2.0 * primal_next - primal
        primal_picked = jnp.dot(col_select, extrapolated, precision=lax.Precision.HIGHEST)
        forward = (
            jnp.einsum("nrc,nc->nr", tiles, primal_picked, precision=lax.Precision.HIGHEST)
            * live_mask
        )
        window_terms = jnp.dot(row_select.T, forward, precision=lax.Precision.HIGHEST)
        summed = lax.psum(window_terms, "grp")
        from_above = shifted(summed[:row_blocks], "tm", -1)
        from_below = shifted(summed[2 * row_blocks :], "tm", 1)
        image_slab = summed[row_blocks : 2 * row_blocks] + from_above + from_below
        dual_next = dual_update(dual, rhs, image_slab)
        if iteration + 1 < ITERS:
            dual_view = with_halo(dual_next, (("tm", 0),), row_blocks)
        primal_total = primal_total + primal_next
        dual_total = dual_total + dual_next
        primal = primal_next
        dual = dual_next
    return (primal, dual, primal_total / ITERS, dual_total / ITERS)


def solution(mesh):
    return jax.shard_map(
        body,
        mesh=mesh,
        in_specs=(
            P(("grp", "tm"), None),
            P("tm", None),
            P(("grp", "tm"), None),
            P("tm", None),
            P(("grp", "tm"), None, None),
            P(("grp", "tm")),
            P(("grp", "tm")),
            P(("grp", "tm")),
            P(("grp", "tm"), None),
            P(),
            P(),
        ),
        out_specs=(P(("grp", "tm"), None), P("tm", None), P(("grp", "tm"), None), P("tm", None)),
        check_vma=False,
    )
```

profile of v0, /device:TPU:16, one launch (start us, length us, event | category | flops | bytes accessed | tf_op | source)
XLA Modules:
  0.0 100.7 jit_solution(15821462959131894350)
XLA Ops:
  0.7 4.4 %collective-permute-start.1 = (f32[32,128]{1,0:T(8,128)}, f32[32,128]{1,0:T(8,128)S(1)}, u32[]{:S(2)}, u32[]{:S(2)}) collective-permute-start(f32[32,128]{1,0:T(8,128)} %param.12), channel_id=1, source_target_pairs={{1,0},{2,1},{3,2},{4,3},{5,4},{6,5},{7,6},{8,7},{9,8},{10,9},{11,1... | collective-permute-start | bytes 49160 | tf_op jit(solution)/shard_map/ppermute | solution.py:21
  5.0 1.9 %collective-permute-start = (f32[32,128]{1,0:T(8,128)}, f32[32,128]{1,0:T(8,128)S(1)}, u32[]{:S(2)}, u32[]{:S(2)}) collective-permute-start(f32[32,128]{1,0:T(8,128)} %param.12), channel_id=1, source_target_pairs={{0,1},{1,2},{2,3},{3,4},{4,5},{5,6},{6,7},{7,8},{8,9},{9,10},{10,1... | collective-permute-start | bytes 49160 | tf_op jit(solution)/shard_map/ppermute | solution.py:18
  7.6 1.6 %fusion.64 = (f32[1]{0:T(128)}, f32[1]{0:T(128)}, f32[1]{0:T(128)}, f32[1]{0:T(128)}, f32[1]{0:T(128)}, /*index=5*/f32[1]{0:T(128)}, f32[1]{0:T(128)}, f32[1]{0:T(128)}) fusion(f32[8]{0:T(128)} %param.20), kind=kLoop, calls=%fused_computation.84 | loop fusion | bytes 64 | tf_op jit(solution)/shard_map/slice | solution.py:61
  9.3 1.6 %fusion.63 = (f32[1]{0:T(128)}, f32[1]{0:T(128)}, f32[1]{0:T(128)}, f32[1]{0:T(128)}, f32[1]{0:T(128)}, /*index=5*/f32[1]{0:T(128)}, f32[1]{0:T(128)}, f32[1]{0:T(128)}) fusion(f32[8]{0:T(128)} %param.21), kind=kLoop, calls=%fused_computation.83 | loop fusion | bytes 64 | tf_op jit(solution)/shard_map/slice | solution.py:62
  11.6 0.8 broadcast_subtract_fusion.1
  12.4 0.8 broadcast_subtract_fusion
  13.3 0.9 fusion.8
  14.2 5.3 %fusion.65 = f32[64,1,128]{2,1,0:T(1,128)S(1)} fusion(f32[64,128,1]{1,2,0:T(1,128)S(1)} %bitcast.46, f32[64,128,128]{2,1,0:T(8,128)} %param.15), kind=kOutput, calls=%fused_computation.85 | convolution fusion | flops 12582912 | bytes 4259840 | tf_op jit(solution)/shard_map/nrc,nr->nc/dot_general | solution.py:75
  19.5 10.4 %fusion.7 = f32[16,128]{1,0:T(8,128)S(1)} fusion(f32[16,128]{1,0:T(8,128)S(1)} %copy-done.4, f32[16,128]{1,0:T(8,128)S(1)} %copy-done.5, f32[64,128]{1,0:T(8,128)S(1)} %bitcast.49, f32[64]{0:T(128)S(1)} %compare_convert_fusion, s32[64]{0:T(128)S(1)} %broadcast_subtract_fusion.1, pred[16,128]{1,0:T(8,128)(4,1)S(1)} %get-tuple-element.16, ...), kind=kOutput, calls=%fused_computation.9 | convolution fusion | flops 1625088 | bytes 74304 | tf_op jit(solution)/shard_map/dot_general | solution.py:78
  30.2 6.6 %fusion.66 = f32[64,1,128]{2,1,0:T(1,128)S(1)} fusion(f32[64,128,1]{1,2,0:T(1,128)S(1)} %bitcast.53, f32[64,128,128]{2,1,0:T(8,128)S(1)} %copy-done), kind=kOutput, calls=%fused_computation.86 | convolution fusion | flops 12582912 | bytes 4259840 | tf_op jit(solution)/shard_map/nrc,nc->nr/dot_general | solution.py:84
  37.1 3.5 %psum.14 = f32[96,128]{1,0:T(8,128)S(1)} all-reduce(f32[96,128]{1,0:T(8,128)S(1)} %fusion.23), channel_id=1, replica_groups=mesh['grp'=2,'tm'=16] {'grp'}, use_global_device_ids=true, to_apply=%region_0.1 | all-reduce | flops 12288 | bytes 98304 | tf_op jit(solution)/shard_map/psum | solution.py:88
  40.7 6.0 %collective-permute-start.2 = (f32[32,128]{1,0:T(8,128)S(1)}, f32[32,128]{1,0:T(8,128)S(1)}, u32[]{:S(2)}, u32[]{:S(2)}) collective-permute-start(f32[32,128]{1,0:T(8,128)S(1)} %get-tuple-element.8), channel_id=1, source_target_pairs={{1,0},{2,1},{3,2},{4,3},{5,4},{6,5},{7,6},{8,7},{9,8},{10,9},{11,1... | collective-permute-start | bytes 49160 | tf_op jit(solution)/shard_map/ppermute | solution.py:29
  46.6 1.9 %collective-permute-start.3 = (f32[32,128]{1,0:T(8,128)S(1)}, f32[32,128]{1,0:T(8,128)S(1)}, u32[]{:S(2)}, u32[]{:S(2)}) collective-permute-start(f32[32,128]{1,0:T(8,128)S(1)} %get-tuple-element.9), channel_id=1, source_target_pairs={{0,1},{1,2},{2,3},{3,4},{4,5},{5,6},{6,7},{7,8},{8,9},{9,10},{10,1... | collective-permute-start | bytes 49160 | tf_op jit(solution)/shard_map/ppermute | solution.py:29
  48.6 5.5 %collective-permute-done.3 = f32[32,128]{1,0:T(8,128)S(1)} collective-permute-done((f32[32,128]{1,0:T(8,128)S(1)}, f32[32,128]{1,0:T(8,128)S(1)}, u32[]{:S(2)}, u32[]{:S(2)}) %collective-permute-start.3) | collective-permute-done | bytes 16416 | tf_op jit(solution)/shard_map/ppermute | solution.py:29
  54.1 1.9 %collective-permute-start.5 = (f32[32,128]{1,0:T(8,128)S(1)}, f32[32,128]{1,0:T(8,128)S(1)}, u32[]{:S(2)}, u32[]{:S(2)}) collective-permute-start(f32[32,128]{1,0:T(8,128)S(1)} %fusion.37), channel_id=1, source_target_pairs={{1,0},{2,1},{3,2},{4,3},{5,4},{6,5},{7,6},{8,7},{9,8},{10,9},{11,1... | collective-permute-start | bytes 49160 | tf_op jit(solution)/shard_map/ppermute | solution.py:21
  56.0 4.1 %collective-permute-start.4 = (f32[32,128]{1,0:T(8,128)S(1)}, f32[32,128]{1,0:T(8,128)S(1)}, u32[]{:S(2)}, u32[]{:S(2)}) collective-permute-start(f32[32,128]{1,0:T(8,128)S(1)} %fusion.37), channel_id=1, source_target_pairs={{0,1},{1,2},{2,3},{3,4},{4,5},{5,6},{6,7},{7,8},{8,9},{9,10},{10,1... | collective-permute-start | bytes 49160 | tf_op jit(solution)/shard_map/ppermute | solution.py:18
  60.1 3.3 %collective-permute-done.4 = f32[32,128]{1,0:T(8,128)S(1)} collective-permute-done((f32[32,128]{1,0:T(8,128)S(1)}, f32[32,128]{1,0:T(8,128)S(1)}, u32[]{:S(2)}, u32[]{:S(2)}) %collective-permute-start.4) | collective-permute-done | bytes 16416 | tf_op jit(solution)/shard_map/ppermute | solution.py:18
  63.7 5.3 %fusion.67 = f32[64,1,128]{2,1,0:T(1,128)S(1)} fusion(f32[64,128,1]{1,2,0:T(1,128)S(1)} %bitcast.47, f32[64,128,128]{2,1,0:T(8,128)} %param.15), kind=kOutput, calls=%fused_computation.87 | convolution fusion | flops 12582912 | bytes 4259840 | tf_op jit(solution)/shard_map/nrc,nr->nc/dot_general | solution.py:75
  68.9 11.1 %add_multiply_fusion.1 = (f32[16,128]{1,0:T(8,128)}, f32[16,128]{1,0:T(8,128)S(1)}) fusion(f32[16,128]{1,0:T(8,128)S(1)} %fusion.7, pred[16,128]{1,0:T(8,128)(4,1)S(1)} %get-tuple-element.16, pred[16,128]{1,0:T(8,128)(4,1)S(1)} %get-tuple-element.15, pred[16,128]{1,0:T(8,128)(4,1)S(1)} %get-tuple-element.14, pred[16,128]{1,0:T(8,128)(4,1)S(1)} %get-tuple-element.13, ...), kind=kOutput, calls=%fused_computation.57 | convolution fusion | flops 1629184 | bytes 82496 | tf_op jit(solution)/shard_map/dot_general | solution.py:78
  80.2 6.6 %fusion.68 = f32[64,1,128]{2,1,0:T(1,128)S(1)} fusion(f32[64,128,1]{1,2,0:T(1,128)S(1)} %bitcast.51, f32[64,128,128]{2,1,0:T(8,128)S(1)} %copy-done.1), kind=kOutput, calls=%fused_computation.88 | convolution fusion | flops 12582912 | bytes 4259840 | tf_op jit(solution)/shard_map/nrc,nc->nr/dot_general | solution.py:84
  87.1 3.5 %psum.15 = f32[96,128]{1,0:T(8,128)S(1)} all-reduce(f32[96,128]{1,0:T(8,128)S(1)} %fusion.20), channel_id=1, replica_groups=mesh['grp'=2,'tm'=16] {'grp'}, use_global_device_ids=true, to_apply=%region_1.2 | all-reduce | flops 12288 | bytes 98304 | tf_op jit(solution)/shard_map/psum | solution.py:88
  90.7 1.9 %collective-permute-start.6 = (f32[32,128]{1,0:T(8,128)S(1)}, f32[32,128]{1,0:T(8,128)S(1)}, u32[]{:S(2)}, u32[]{:S(2)}) collective-permute-start(f32[32,128]{1,0:T(8,128)S(1)} %get-tuple-element.6), channel_id=1, source_target_pairs={{1,0},{2,1},{3,2},{4,3},{5,4},{6,5},{7,6},{8,7},{9,8},{10,9},{11,1... | collective-permute-start | bytes 49160 | tf_op jit(solution)/shard_map/ppermute | solution.py:29
  92.6 3.9 %collective-permute-start.7 = (f32[32,128]{1,0:T(8,128)S(1)}, f32[32,128]{1,0:T(8,128)S(1)}, u32[]{:S(2)}, u32[]{:S(2)}) collective-permute-start(f32[32,128]{1,0:T(8,128)S(1)} %get-tuple-element.7), channel_id=1, source_target_pairs={{0,1},{1,2},{2,3},{3,4},{4,5},{5,6},{6,7},{7,8},{8,9},{9,10},{10,1... | collective-permute-start | bytes 49160 | tf_op jit(solution)/shard_map/ppermute | solution.py:29
  96.6 3.5 %collective-permute-done.7 = f32[32,128]{1,0:T(8,128)S(1)} collective-permute-done((f32[32,128]{1,0:T(8,128)S(1)}, f32[32,128]{1,0:T(8,128)S(1)}, u32[]{:S(2)}, u32[]{:S(2)}) %collective-permute-start.7) | collective-permute-done | bytes 16416 | tf_op jit(solution)/shard_map/ppermute | solution.py:29
  (30 shorter events, 2.6 us)
Async XLA Ops:
  0.6 18.9 %copy-start.5 = (f32[16,128]{1,0:T(8,128)S(1)}, f32[16,128]{1,0:T(8,128)}, u32[]{:S(2)}) copy-start(f32[16,128]{1,0:T(8,128)} %param.13) | copy-start | bytes 24580
  0.6 18.9 %copy-start.4 = (f32[16,128]{1,0:T(8,128)S(1)}, f32[16,128]{1,0:T(8,128)}, u32[]{:S(2)}) copy-start(f32[16,128]{1,0:T(8,128)} %param.11) | copy-start | bytes 24580
  0.7 12.6 %collective-permute-start.1 = (f32[32,128]{1,0:T(8,128)}, f32[32,128]{1,0:T(8,128)S(1)}, u32[]{:S(2)}, u32[]{:S(2)}) collective-permute-start(f32[32,128]{1,0:T(8,128)} %param.12), channel_id=1, source_target_pairs={{1,0},{2,1},{3,2},{4,3},{5,4},{6,5},{7,6},{8,7},{9,8},{10,9},{11,1... | collective-permute-start | bytes 49160 | tf_op jit(solution)/shard_map/ppermute | solution.py:21
  5.0 8.2 %collective-permute-start = (f32[32,128]{1,0:T(8,128)}, f32[32,128]{1,0:T(8,128)S(1)}, u32[]{:S(2)}, u32[]{:S(2)}) collective-permute-start(f32[32,128]{1,0:T(8,128)} %param.12), channel_id=1, source_target_pairs={{0,1},{1,2},{2,3},{3,4},{4,5},{5,6},{6,7},{7,8},{8,9},{9,10},{10,1... | collective-permute-start | bytes 49160 | tf_op jit(solution)/shard_map/ppermute | solution.py:18
  11.6 18.6 %copy-start = (f32[64,128,128]{2,1,0:T(8,128)S(1)}, f32[64,128,128]{2,1,0:T(8,128)}, u32[]{:S(2)}) copy-start(f32[64,128,128]{2,1,0:T(8,128)} %param.15) | copy-start | bytes 12582916
  14.2 39.9 %copy-start.2 = (f32[32,128]{1,0:T(8,128)S(1)}, f32[32,128]{1,0:T(8,128)}, u32[]{:S(2)}) copy-start(f32[32,128]{1,0:T(8,128)} %param.12) | copy-start | bytes 49156
  14.2 39.9 %copy-start.3 = (f32[32,128]{1,0:T(8,128)S(1)}, f32[32,128]{1,0:T(8,128)}, u32[]{:S(2)}) copy-start(f32[32,128]{1,0:T(8,128)} %param.14) | copy-start | bytes 49156
  40.6 39.6 %copy-start.1 = (f32[64,128,128]{2,1,0:T(8,128)S(1)}, f32[64,128,128]{2,1,0:T(8,128)}, u32[]{:S(2)}) copy-start(f32[64,128,128]{2,1,0:T(8,128)} %param.15) | copy-start | bytes 12582916
  40.7 7.9 %collective-permute-start.2 = (f32[32,128]{1,0:T(8,128)S(1)}, f32[32,128]{1,0:T(8,128)S(1)}, u32[]{:S(2)}, u32[]{:S(2)}) collective-permute-start(f32[32,128]{1,0:T(8,128)S(1)} %get-tuple-element.8), channel_id=1, source_target_pairs={{1,0},{2,1},{3,2},{4,3},{5,4},{6,5},{7,6},{8,7},{9,8},{10,9},{11,1... | collective-permute-start | bytes 49160 | tf_op jit(solution)/shard_map/ppermute | solution.py:29
  46.6 7.4 %collective-permute-start.3 = (f32[32,128]{1,0:T(8,128)S(1)}, f32[32,128]{1,0:T(8,128)S(1)}, u32[]{:S(2)}, u32[]{:S(2)}) collective-permute-start(f32[32,128]{1,0:T(8,128)S(1)} %get-tuple-element.9), channel_id=1, source_target_pairs={{0,1},{1,2},{2,3},{3,4},{4,5},{5,6},{6,7},{7,8},{8,9},{9,10},{10,1... | collective-permute-start | bytes 49160 | tf_op jit(solution)/shard_map/ppermute | solution.py:29
  54.1 6.0 %collective-permute-start.5 = (f32[32,128]{1,0:T(8,128)S(1)}, f32[32,128]{1,0:T(8,128)S(1)}, u32[]{:S(2)}, u32[]{:S(2)}) collective-permute-start(f32[32,128]{1,0:T(8,128)S(1)} %fusion.37), channel_id=1, source_target_pairs={{1,0},{2,1},{3,2},{4,3},{5,4},{6,5},{7,6},{8,7},{9,8},{10,9},{11,1... | collective-permute-start | bytes 49160 | tf_op jit(solution)/shard_map/ppermute | solution.py:21
  56.0 7.4 %collective-permute-start.4 = (f32[32,128]{1,0:T(8,128)S(1)}, f32[32,128]{1,0:T(8,128)S(1)}, u32[]{:S(2)}, u32[]{:S(2)}) collective-permute-start(f32[32,128]{1,0:T(8,128)S(1)} %fusion.37), channel_id=1, source_target_pairs={{0,1},{1,2},{2,3},{3,4},{4,5},{5,6},{6,7},{7,8},{8,9},{9,10},{10,1... | collective-permute-start | bytes 49160 | tf_op jit(solution)/shard_map/ppermute | solution.py:18
  80.0 20.7 %copy-start.6 = (f32[16,128]{1,0:T(8,128)}, f32[16,128]{1,0:T(8,128)S(1)}, u32[]{:S(2)}) copy-start(f32[16,128]{1,0:T(8,128)S(1)} %get-tuple-element.35) | copy-start | bytes 24580
  90.7 5.9 %collective-permute-start.6 = (f32[32,128]{1,0:T(8,128)S(1)}, f32[32,128]{1,0:T(8,128)S(1)}, u32[]{:S(2)}, u32[]{:S(2)}) collective-permute-start(f32[32,128]{1,0:T(8,128)S(1)} %get-tuple-element.6), channel_id=1, source_target_pairs={{1,0},{2,1},{3,2},{4,3},{5,4},{6,5},{7,6},{8,7},{9,8},{10,9},{11,1... | collective-permute-start | bytes 49160 | tf_op jit(solution)/shard_map/ppermute | solution.py:29
  92.6 7.4 %collective-permute-start.7 = (f32[32,128]{1,0:T(8,128)S(1)}, f32[32,128]{1,0:T(8,128)S(1)}, u32[]{:S(2)}, u32[]{:S(2)}) collective-permute-start(f32[32,128]{1,0:T(8,128)S(1)} %get-tuple-element.7), channel_id=1, source_target_pairs={{0,1},{1,2},{2,3},{3,4},{4,5},{5,6},{6,7},{7,8},{8,9},{9,10},{10,1... | collective-permute-start | bytes 49160 | tf_op jit(solution)/shard_map/ppermute | solution.py:29
where the time goes:
time: 101 us
  matrix products  47.4 us (47%)
  starting transfers between devices  26.1 us (26%)
  waiting for transfers between devices  12.3 us (12%)
  blocking collectives  7.06 us (7%)
  local copies, waits for them, and re-layouts  3.31 us (3%)
  other arithmetic  2.99 us (3%)
  between operations  1.53 us (2%)
    dot_general x2, matrix products, body(): jnp.dot(col_select.T, backward, precision=lax.Precision.HIGHEST)  21.5 us
    ppermute x4, starting transfers between devices, shifted(): return lax.ppermute(block, axis, route)  13.7 us
    dot_general x2, matrix products, body(): jnp.einsum('nrc,nc->nr', tiles, primal_picked, precision=lax.Precision.HI...  13.2 us
    dot_general x2, matrix products, body(): jnp.einsum('nrc,nr->nc', tiles, dual_picked, precision=lax.Precision.HIGH...  10.6 us
    ppermute x4, waiting for transfers between devices, shifted(): return lax.ppermute(block, axis, route)  8.99 us
    psum x2, blocking collectives, body(): summed = lax.psum(window_terms, 'grp')  7.06 us
    ppermute x2, starting transfers between devices, with_halo(): lax.ppermute(lax.slice_in_dim(block, 0, width, axis=dim), axis, backward)  6.3 us
    ppermute x2, starting transfers between devices, with_halo(): lax.ppermute(lax.slice_in_dim(block, block.shape[dim] - width, None, axis...  6.03 us
  transfers between devices with their start and end apart: 8, of which 3 were waited for; matrix products, arithmetic and copies ran while one was open for 6% of the time, Pallas kernels for 0%

commit v1 on v0

v1 whole, which is shorter than its diff:
```python
import functools

import jax
import jax.numpy as jnp
from jax import lax
from jax.experimental import pallas as pl
from jax.experimental.pallas import tpu as pltpu
from jax.sharding import PartitionSpec as P

ITERS = 2
AXES = ("grp", "tm")
primal_step = 0.6
dual_step = 0.6
f32 = jnp.float32
bf16 = jnp.bfloat16


def split(value):
    high = value.astype(bf16)
    return high, (value - high.astype(f32)).astype(bf16)


def prep_kernel(
    chunks,
    tiles,
    rows,
    cols,
    count,
    classes,
    lower_table,
    upper_table,
    packed,
    row_pick,
    row_sum,
    col_pick,
    col_sum,
    lower,
    upper,
    held,
    sems,
):
    total, size = tiles.shape[0], tiles.shape[1]
    step = total // chunks
    copies = []
    for k in range(chunks):
        part = pl.ds(k * step, step)
        copy = pltpu.make_async_copy(tiles.at[part], held.at[part], sems.at[k])
        copy.start()
        copies.append(copy)
    time = lax.axis_index("tm")
    device = lax.axis_index("grp") * lax.axis_size("tm") + time
    slot = lax.broadcasted_iota(jnp.int32, (1, total), 1)
    live = slot < count[0]
    row_total = row_sum.shape[0]
    col_total = col_sum.shape[0]
    local_rows = rows[...] - (time - 1) * (row_total // 3)
    local_cols = cols[...] - device * col_total
    for local, total_out, pick, summed in (
        (local_rows, row_total, row_pick, row_sum),
        (local_cols, col_total, col_pick, col_sum),
    ):
        hit = lax.broadcasted_iota(jnp.int32, (total_out, total), 0) == local
        alive = jnp.where(hit & live, 1.0, 0.0).astype(f32)
        summed[...] = jnp.concatenate([alive, alive], axis=1).astype(bf16)
        pick[...] = jnp.transpose(jnp.where(hit, 1.0, 0.0).astype(f32)).astype(bf16)
    low = jnp.zeros(classes.shape, f32)
    high = jnp.zeros(classes.shape, f32)
    for k in range(lower_table.shape[0]):
        low = jnp.where(classes[...] == k, lower_table[k], low)
        high = jnp.where(classes[...] == k, upper_table[k], high)
    lower[...] = low
    upper[...] = high
    for k in range(chunks):
        copies[k].wait()
        for n in range(k * step, (k + 1) * step):
            tile_high, tile_low = split(held[n])
            lanes = pl.ds(n % 2 * size, size)
            packed[n // 2, pl.ds(0, size), lanes] = tile_high
            packed[n // 2, pl.ds(size, size), lanes] = tile_low


def products(packed, picked_high, picked_low, transposed):
    total, size = picked_high.shape
    row = lax.broadcasted_iota(jnp.int32, (8, size), 0)
    even = row % 2 == 0
    both = jnp.concatenate([even, even], axis=0)
    outs = []
    for q in range(total // 8):
        part = slice(8 * q, 8 * q + 8)
        left = jnp.concatenate([picked_high[part], picked_low[part]], axis=0)
        if transposed:
            zero = jnp.zeros_like(left)
            left = jnp.concatenate(
                [jnp.where(both, left, zero), jnp.where(both, zero, left)], axis=1
            )
        else:
            left = jnp.concatenate([left, left], axis=1)
        left = left.astype(bf16)
        result = jnp.zeros((8, size), f32)
        for j in range(4):
            out = lax.dot_general(
                left,
                packed[4 * q + j],
                (((1,), (1 if transposed else 0,)), ((), ())),
                preferred_element_type=f32,
            )
            out = out[:8] + out[8:]
            if transposed:
                term = out[:, :size] + out[:, size:]
            else:
                term = jnp.where(even, out[:, :size], out[:, size:])
            result = jnp.where(row // 2 == j, term, result)
        outs.append(result)
    return jnp.concatenate(outs, axis=0)


def pick(selector, values):
    size = values.shape[1]
    both = jnp.concatenate(split(values), axis=1)
    out = jnp.dot(selector[...], both, preferred_element_type=f32)
    return out[:, :size], out[:, size:]


def summed(selector, values):
    both = jnp.concatenate(split(values), axis=0)
    return jnp.dot(selector[...], both, preferred_element_type=f32)


def step_kernel(
    packed,
    row_pick,
    row_sum,
    col_pick,
    col_sum,
    lower,
    upper,
    cost,
    primal,
    offset,
    view,
    primal_out,
    window_out,
):
    blocks = offset.shape[0]
    high, low = pick(row_pick, view[...])
    adjoint = summed(col_sum, products(packed, high, low, False))
    moved = primal[...] - primal_step * (cost[...] - adjoint)
    primal_next = jnp.minimum(jnp.maximum(moved, lower[...]), upper[...])
    primal_out[...] = primal_next
    high, low = pick(col_pick, 2.0 * primal_next - primal[...])
    window = summed(row_sum, products(packed, high, low, True)) * (-dual_step)
    window_out[...] = window
    own = pl.ds(blocks, blocks)
    first = (lax.axis_index("grp") == 0).astype(f32)
    window_out[own] = window[blocks : 2 * blocks] + offset[...] * first


def vmem(count):
    return [pl.BlockSpec(memory_space=pltpu.VMEM)] * count


def body(
    groups,
    times,
    x_start,
    y_start,
    cost,
    rhs,
    tiles,
    tile_rows,
    tile_cols,
    tile_count,
    var_class,
    lower_table,
    upper_table,
):
    total, size = tiles.shape[0], tiles.shape[1]
    cols, rows = x_start.shape[0], y_start.shape[0]
    grp, tm = lax.axis_index("grp"), lax.axis_index("tm")
    rising = grp % 2 == 0

    def number(g, t):
        return g * times + t

    def swap(value, bit):
        route = [
            (number(g, t), number(g ^ bit, t)) for g in range(groups) for t in range(times)
        ]
        return lax.ppermute(value, AXES, route)

    def group_sum(value):
        bit = 1
        while bit < groups:
            value = value + swap(value, bit)
            bit *= 2
        return value

    def ring(distance):
        route = []
        for g in range(groups):
            for t in range(times):
                target = t + distance if g % 2 == 0 else t - distance
                if 0 <= target < times:
                    route.append((number(g, t), number(g, target)))
                else:
                    route.append((number(g, t), number(g ^ 1, t)))
        return route

    def back(distance):
        return [(target, source) for source, target in ring(distance)]

    def neighbours(rising_value, falling_value):
        forth = lax.ppermute(rising_value, AXES, ring(1))
        reverse = lax.ppermute(falling_value, AXES, back(1))
        return jnp.where(rising, forth, reverse), jnp.where(rising, reverse, forth)

    chunks = 8
    prepared = pl.pallas_call(
        functools.partial(prep_kernel, chunks),
        out_shape=(
            jax.ShapeDtypeStruct((total // 2, 2 * size, 2 * size), bf16),
            jax.ShapeDtypeStruct((total, 3 * rows), bf16),
            jax.ShapeDtypeStruct((3 * rows, 2 * total), bf16),
            jax.ShapeDtypeStruct((total, cols), bf16),
            jax.ShapeDtypeStruct((cols, 2 * total), bf16),
            jax.ShapeDtypeStruct(x_start.shape, f32),
            jax.ShapeDtypeStruct(x_start.shape, f32),
        ),
        in_specs=[pl.BlockSpec(memory_space=pl.ANY)]
        + vmem(2)
        + [pl.BlockSpec(memory_space=pltpu.SMEM)]
        + vmem(1)
        + [pl.BlockSpec(memory_space=pltpu.SMEM)] * 2,
        out_specs=tuple(vmem(7)),
        scratch_shapes=[
            pltpu.VMEM(tiles.shape, f32),
            pltpu.SemaphoreType.DMA((chunks,)),
        ],
        compiler_params=pltpu.CompilerParams(vmem_limit_bytes=24 << 20),
        cost_estimate=pl.CostEstimate(
            flops=4 * total * size * size,
            bytes_accessed=8 * total * size * size,
            transcendentals=0,
        ),
        name="prep",
    )(
        tiles,
        tile_rows[None, :],
        tile_cols[None, :],
        tile_count,
        var_class,
        lower_table,
        upper_table,
    )

    def step(primal, offset, view):
        return pl.pallas_call(
            step_kernel,
            out_shape=(
                jax.ShapeDtypeStruct(x_start.shape, f32),
                jax.ShapeDtypeStruct((3 * rows, size), f32),
            ),
            in_specs=vmem(11),
            out_specs=tuple(vmem(2)),
            compiler_params=pltpu.CompilerParams(vmem_limit_bytes=24 << 20),
            cost_estimate=pl.CostEstimate(
                flops=8 * total * size * size,
                bytes_accessed=8 * total * size * size,
                transcendentals=0,
            ),
            name="step",
        )(*prepared, cost, primal, offset, view)

    above, below = neighbours(y_start, y_start)
    view = jnp.concatenate([above, y_start, below], axis=0)
    primal = x_start
    dual = y_start
    primal_total = jnp.zeros_like(x_start)
    dual_total = jnp.zeros_like(y_start)
    for iteration in range(ITERS):
        primal, window = step(primal, dual + dual_step * rhs, view)
        window = group_sum(window)
        low, own, high = window[:rows], window[rows : 2 * rows], window[2 * rows :]
        if iteration + 1 < ITERS:
            near = jnp.where(rising, window[rows:], window[: 2 * rows])
            far = jnp.where(rising, high, low)
            near = lax.ppermute(near, AXES, ring(1))
            far = lax.ppermute(far, AXES, ring(2))
            has_near = jnp.where(rising, tm >= 1, tm + 1 < times)
            has_far = jnp.where(rising, tm >= 2, tm + 2 < times)
            part = jnp.where(rising, near[rows:], near[:rows])
            part = jnp.where(has_near, part, 0.0)
            side = jnp.where(rising, near[:rows] + low, near[rows:] + high)
            side = side + jnp.where(has_far, far, 0.0)
            side = jnp.maximum(side, 0.0)
            sent = jnp.concatenate([side, part], axis=0)
            got = swap(sent, 1)
            dual = jnp.maximum(own + (part + got[rows:]), 0.0)
            above = jnp.where(rising, side, got[:rows])
            below = jnp.where(rising, got[:rows], side)
            view = jnp.concatenate([above, dual, below], axis=0)
        else:
            above, below = neighbours(
                jnp.where(rising, high, low), jnp.where(rising, low, high)
            )
            above = jnp.where(tm >= 1, above, 0.0)
            below = jnp.where(tm + 1 < times, below, 0.0)
            dual = jnp.maximum(own + (above + below), 0.0)
        primal_total = primal_total + primal
        dual_total = dual_total + dual
    return (primal, dual, primal_total / ITERS, dual_total / ITERS)


def solution(mesh):
    groups, times = mesh.shape["grp"], mesh.shape["tm"]
    return jax.shard_map(
        functools.partial(body, groups, times),
        mesh=mesh,
        in_specs=(
            P(("grp", "tm"), None),
            P("tm", None),
            P(("grp", "tm"), None),
            P("tm", None),
            P(("grp", "tm"), None, None),
            P(("grp", "tm")),
            P(("grp", "tm")),
            P(("grp", "tm")),
            P(("grp", "tm"), None),
            P(),
            P(),
        ),
        out_specs=(P(("grp", "tm"), None), P("tm", None), P(("grp", "tm"), None), P("tm", None)),
        check_vma=False,
    )
```

time: 101 us -> 39.8 us (0.39)
  the two profiles are of different devices: /device:TPU:16 before, /device:TPU:6 now
where the time goes in v1:
time: 39.8 us; the launch traced here: 39.4 us
  waiting for transfers between devices  10.4 us (26%)
  local copies, waits for them, and re-layouts  9.63 us (24%)
  starting transfers between devices  8.78 us (22%)
  Pallas kernels  6.31 us (16%)
  other arithmetic  2.75 us (7%)
  between operations  1.46 us (4%)
    unnamed x24, local copies, waits for them, and re-layouts  9.63 us
    pallas_call x2, Pallas kernels, step(): pl.pallas_call(step_kernel, out_shape=(jax.ShapeDtypeStruct(x_start.shape...  4.58 us
    ppermute x2, waiting for transfers between devices, neighbours(): reverse = lax.ppermute(falling_value, AXES, back(1))  3.76 us
    ppermute x2, starting transfers between devices, neighbours(): forth = lax.ppermute(rising_value, AXES, ring(1))  3.57 us
    ppermute x3, waiting for transfers between devices, swap(): return lax.ppermute(value, AXES, route)  3.14 us
    ppermute x1, waiting for transfers between devices, body(): far = lax.ppermute(far, AXES, ring(2))  3.12 us
    ppermute x1, starting transfers between devices, body(): near = lax.ppermute(near, AXES, ring(1))  2.62 us
    div x2, other arithmetic, body(): return (primal, dual, primal_total / ITERS, dual_total / ITERS)  1.92 us
  transfers between devices with their start and end apart: 9, of which 6 were waited for; matrix products, arithmetic and copies ran while one was open for 5% of the time, Pallas kernels for 4%

profile of v1, /device:TPU:6, one launch (start us, length us, event | category | flops | bytes accessed | tf_op | source)
XLA Modules:
  0.0 39.4 jit_solution(15830573425295871554)
XLA Ops:
  0.7 1.5 %collective-permute-start = (f32[32,128]{1,0:T(8,128)}, f32[32,128]{1,0:T(8,128)S(1)}, u32[]{:S(2)}, u32[]{:S(2)}) collective-permute-start(f32[32,128]{1,0:T(8,128)} %param.12), channel_id=1, source_target_pairs={{0,1},{1,2},{2,3},{3,4},{4,5},{5,6},{6,7},{7,8},{8,9},{9,10},{10,1... | collective-permute-start | bytes 49160 | tf_op jit(solution)/shard_map/ppermute | solution.py:213
  2.7 0.8 %multiply_add_fusion.1.offset = f32[32,128]{1,0:T(8,128)S(1)} fusion(f32[32,128]{1,0:T(8,128)} %param.12, f32[32,128]{1,0:T(8,128)} %param.14), kind=kLoop, calls=%fused_computation.18 | loop fusion | flops 8192 | bytes 49152 | tf_op jit(solution)/shard_map/add | solution.py:281
  4.2 2.2 %copy-done.2 = f32[64,128,128]{2,1,0:T(8,128)S(1)} copy-done((f32[64,128,128]{2,1,0:T(8,128)S(1)}, f32[64,128,128]{2,1,0:T(8,128)}, u32[]{:S(2)}) %copy-start.2) | copy-done | bytes 4194328
  6.3 0.7 %copy-done.4 = s32[16,128]{1,0:T(8,128)S(1)} copy-done((s32[16,128]{1,0:T(8,128)S(1)}, s32[16,128]{1,0:T(8,128)}, u32[]{:S(2)}) %copy-start.4) | copy-done | bytes 8216
  7.0 0.7 %copy-done.6 = s32[64]{0:T(128)S(1)} copy-done((s32[64]{0:T(128)S(1)}, s32[64]{0:T(128)}, u32[]{:S(2)}) %copy-start.6) | copy-done | bytes 280
  7.7 0.7 %copy-done.7 = s32[64]{0:T(128)S(1)} copy-done((s32[64]{0:T(128)S(1)}, s32[64]{0:T(128)}, u32[]{:S(2)}) %copy-start.7) | copy-done | bytes 280
  8.4 0.7 %copy-done.8 = f32[8]{0:T(128)S(1)} copy-done((f32[8]{0:T(128)S(1)}, f32[8]{0:T(128)}, u32[]{:S(2)}) %copy-start.8) | copy-done | bytes 56
  9.0 0.7 %copy-done.9 = f32[8]{0:T(128)S(1)} copy-done((f32[8]{0:T(128)S(1)}, f32[8]{0:T(128)}, u32[]{:S(2)}) %copy-start.9) | copy-done | bytes 56
  9.7 1.7 %prep.1 = (bf16[32,256,256]{2,1,0:T(8,128)(2,1)S(1)}, bf16[64,96]{1,0:T(8,128)(2,1)S(1)}, bf16[96,128]{1,0:T(8,128)(2,1)S(1)}, bf16[64,16]{1,0:T(8,128)(2,1)S(1)...) custom-call(f32[64,128,128]{2,1,0:T(8,128)S(1)} %copy-done.2, s32[1,64]{1,0:T(1,128)S(1)} %bitcast.2, ...), custom_call_target="tpu_custom_call" | custom-call | flops 4194304 | bytes 8388608 | tf_op jit(solution)/shard_map/prep/pallas_call | solution.py:218
  11.5 2.3 %step.2 = (f32[16,128]{1,0:T(8,128)S(1)}, f32[96,128]{1,0:T(8,128)S(1)}) custom-call(bf16[32,256,256]{2,1,0:T(8,128)(2,1)S(1)} %get-tuple-element.15.packed, bf16[64,96]{1,0:T(8,128)(2,1)S(1)} %get-tuple-element.16.row_pick, bf16[96,128]{1,0:T(8,128)(2,1)S(1)} %get-tuple-element.17.row_sum, bf16[64,16]{1,0:T(8,128)(2,1)S(1)} %get-tuple-element.18.col_pick, ...), custom_call_target="tpu_custom_call" | custom-call | flops 8388608 | bytes 8388608 | tf_op jit(solution)/shard_map/step/pallas_call | solution.py:257
  13.8 1.9 %copy-done = bf16[32,256,256]{2,1,0:T(8,128)(2,1)} copy-done((bf16[32,256,256]{2,1,0:T(8,128)(2,1)}, bf16[32,256,256]{2,1,0:T(8,128)(2,1)S(1)}, u32[]{:S(2)}) %copy-start) | copy-done | bytes 4194328
  15.7 1.1 %collective-permute-start.2 = (f32[96,128]{1,0:T(8,128)S(1)}, f32[96,128]{1,0:T(8,128)S(1)}, u32[]{:S(2)}, u32[]{:S(2)}) collective-permute-start(f32[96,128]{1,0:T(8,128)S(1)} %get-tuple-element.23), channel_id=1, source_target_pairs={{0,16},{1,17},{2,18},{3,19},{4,20},{5,21},{6,22},{7,23},{8,24},{9,... | collective-permute-start | bytes 147464 | tf_op jit(solution)/shard_map/ppermute | solution.py:189
  16.8 0.9 %collective-permute-done.2 = f32[96,128]{1,0:T(8,128)S(1)} collective-permute-done((f32[96,128]{1,0:T(8,128)S(1)}, f32[96,128]{1,0:T(8,128)S(1)}, u32[]{:S(2)}, u32[]{:S(2)}) %collective-permute-start.2) | collective-permute-done | bytes 49184 | tf_op jit(solution)/shard_map/ppermute | solution.py:189
  17.7 2.6 %collective-permute-start.3 = (f32[64,128]{1,0:T(8,128)S(1)}, f32[64,128]{1,0:T(8,128)S(1)}, u32[]{:S(2)}, u32[]{:S(2)}) collective-permute-start(f32[64,128]{1,0:T(8,128)S(1)} %slice_select_fusion), channel_id=1, source_target_pairs={{0,1},{1,2},{2,3},{3,4},{4,5},{5,6},{6,7},{7,8},{8,9},{9,10},{10,1... | collective-permute-start | bytes 98312 | tf_op jit(solution)/shard_map/ppermute | solution.py:287
  20.3 0.6 %collective-permute-start.4 = (f32[32,128]{1,0:T(8,128)S(1)}, f32[32,128]{1,0:T(8,128)S(1)}, u32[]{:S(2)}, u32[]{:S(2)}) collective-permute-start(f32[32,128]{1,0:T(8,128)S(1)} %slice_select_fusion.5), channel_id=1, source_target_pairs={{0,2},{1,3},{2,4},{3,5},{4,6},{5,7},{6,8},{7,9},{8,10},{9,11},{10,... | collective-permute-start | bytes 49160 | tf_op jit(solution)/shard_map/ppermute | solution.py:288
  20.9 3.1 %collective-permute-done.4 = f32[32,128]{1,0:T(8,128)S(1)} collective-permute-done((f32[32,128]{1,0:T(8,128)S(1)}, f32[32,128]{1,0:T(8,128)S(1)}, u32[]{:S(2)}, u32[]{:S(2)}) %collective-permute-start.4) | collective-permute-done | bytes 16416 | tf_op jit(solution)/shard_map/ppermute | solution.py:288
  24.2 1.2 %collective-permute-done.5 = f32[64,128]{1,0:T(8,128)S(1)} collective-permute-done((f32[64,128]{1,0:T(8,128)S(1)}, f32[64,128]{1,0:T(8,128)S(1)}, u32[]{:S(2)}, u32[]{:S(2)}) %collective-permute-start.5) | collective-permute-done | bytes 32800 | tf_op jit(solution)/shard_map/ppermute | solution.py:189
  25.4 2.2 %copy-done.1 = bf16[32,256,256]{2,1,0:T(8,128)(2,1)S(1)} copy-done((bf16[32,256,256]{2,1,0:T(8,128)(2,1)S(1)}, bf16[32,256,256]{2,1,0:T(8,128)(2,1)}, u32[]{:S(2)}) %copy-start.1) | copy-done | bytes 4194328
  27.6 2.3 %step.3 = (f32[16,128]{1,0:T(8,128)}, f32[96,128]{1,0:T(8,128)S(1)}) custom-call(bf16[32,256,256]{2,1,0:T(8,128)(2,1)S(1)} %copy-done.1, bf16[64,96]{1,0:T(8,128)(2,1)S(1)} %get-tuple-element.16.row_pick, bf16[96,128]{1,0:T(8,128)(2,1)S(1)} %get-tuple-element.17.row_sum, bf16[64,16]{1,0:T(8,128)(2,1)S(1)} %get-tuple-element.18.col_pick, ...), custom_call_target="tpu_custom_call" | custom-call | flops 8388608 | bytes 8388608 | tf_op jit(solution)/shard_map/step/pallas_call | solution.py:257
  30.1 1.1 %collective-permute-done.6 = f32[96,128]{1,0:T(8,128)S(1)} collective-permute-done((f32[96,128]{1,0:T(8,128)S(1)}, f32[96,128]{1,0:T(8,128)S(1)}, u32[]{:S(2)}, u32[]{:S(2)}) %collective-permute-start.6) | collective-permute-done | bytes 49184 | tf_op jit(solution)/shard_map/ppermute | solution.py:189
  31.2 2.0 %collective-permute-start.7 = (f32[32,128]{1,0:T(8,128)S(1)}, f32[32,128]{1,0:T(8,128)S(1)}, u32[]{:S(2)}, u32[]{:S(2)}) collective-permute-start(f32[32,128]{1,0:T(8,128)S(1)} %get-tuple-element.30), channel_id=1, source_target_pairs={{0,1},{1,2},{2,3},{3,4},{4,5},{5,6},{6,7},{7,8},{8,9},{9,10},{10,1... | collective-permute-start | bytes 49160 | tf_op jit(solution)/shard_map/ppermute | solution.py:213
  33.3 1.3 %add_multiply_fusion.1 = f32[16,128]{1,0:T(8,128)} fusion(f32[16,128]{1,0:T(8,128)S(1)} %get-tuple-element.22.primal, f32[16,128]{1,0:T(8,128)} %get-tuple-element.11), kind=kLoop, calls=%fused_computation.19 | loop fusion | flops 4096 | bytes 24576 | tf_op jit(solution)/shard_map/div | solution.py:311
  35.0 3.8 %collective-permute-done.8 = f32[32,128]{1,0:T(8,128)S(1)} collective-permute-done((f32[32,128]{1,0:T(8,128)S(1)}, f32[32,128]{1,0:T(8,128)S(1)}, u32[]{:S(2)}, u32[]{:S(2)}) %collective-permute-start.8) | collective-permute-done | bytes 16416 | tf_op jit(solution)/shard_map/ppermute | solution.py:214
  38.8 0.6 %add_multiply_fusion = (f32[32,128]{1,0:T(8,128)}, f32[32,128]{1,0:T(8,128)}) fusion(f32[32,128]{1,0:T(8,128)S(1)} %get-tuple-element.35, f32[32,128]{1,0:T(8,128)S(1)} %collective-permute-done.8, f32[32,128]{1,0:T(8,128)S(1)} %collective-permute-done.7, pred[]{:T(512)S(6)} %lt.14, pred[]{:T(512)S(6)} %eq.5, pred[]{:T(512)S(6)} %ge.7, f32[96,128]{1,0:T(8,128)S(1)} %add.61), kind=kLoop, calls=%fused_computation.9 | loop fusion | flops 36864 | bytes 98307 | tf_op jit(solution)/shard_map/div | solution.py:311
  (35 shorter events, 1.4 us)
Async XLA Ops:
  0.6 10.8 %copy-start.11 = (f32[32,128]{1,0:T(8,128)S(1)}, f32[32,128]{1,0:T(8,128)}, u32[]{:S(2)}) copy-start(f32[32,128]{1,0:T(8,128)} %param.12) | copy-start | bytes 49156
  0.6 10.8 %copy-start.3 = (f32[16,128]{1,0:T(8,128)S(1)}, f32[16,128]{1,0:T(8,128)}, u32[]{:S(2)}) copy-start(f32[16,128]{1,0:T(8,128)} %cost.3) | copy-start | bytes 24580
  0.7 10.8 %copy-start.5 = (f32[16,128]{1,0:T(8,128)S(1)}, f32[16,128]{1,0:T(8,128)}, u32[]{:S(2)}) copy-start(f32[16,128]{1,0:T(8,128)} %primal.1) | copy-start | bytes 24580
  0.7 10.7 %collective-permute-start = (f32[32,128]{1,0:T(8,128)}, f32[32,128]{1,0:T(8,128)S(1)}, u32[]{:S(2)}, u32[]{:S(2)}) collective-permute-start(f32[32,128]{1,0:T(8,128)} %param.12), channel_id=1, source_target_pairs={{0,1},{1,2},{2,3},{3,4},{4,5},{5,6},{6,7},{7,8},{8,9},{9,10},{10,1... | collective-permute-start | bytes 49160 | tf_op jit(solution)/shard_map/ppermute | solution.py:213
  2.2 9.2 %collective-permute-start.1 = (f32[32,128]{1,0:T(8,128)}, f32[32,128]{1,0:T(8,128)S(1)}, u32[]{:S(2)}, u32[]{:S(2)}) collective-permute-start(f32[32,128]{1,0:T(8,128)} %param.12), channel_id=1, source_target_pairs={{1,0},{2,1},{3,2},{4,3},{5,4},{6,5},{7,6},{8,7},{9,8},{10,9},{11,1... | collective-permute-start | bytes 49160 | tf_op jit(solution)/shard_map/ppermute | solution.py:214
  4.2 2.2 %copy-start.2 = (f32[64,128,128]{2,1,0:T(8,128)S(1)}, f32[64,128,128]{2,1,0:T(8,128)}, u32[]{:S(2)}) copy-start(f32[64,128,128]{2,1,0:T(8,128)} %tiles.1) | copy-start | bytes 12582916
  6.3 0.7 %copy-start.4 = (s32[16,128]{1,0:T(8,128)S(1)}, s32[16,128]{1,0:T(8,128)}, u32[]{:S(2)}) copy-start(s32[16,128]{1,0:T(8,128)} %classes.1) | copy-start | bytes 24580
  7.0 0.7 %copy-start.6 = (s32[64]{0:T(128)S(1)}, s32[64]{0:T(128)}, u32[]{:S(2)}) copy-start(s32[64]{0:T(128)} %param.16) | copy-start | bytes 772
  7.7 0.7 %copy-start.7 = (s32[64]{0:T(128)S(1)}, s32[64]{0:T(128)}, u32[]{:S(2)}) copy-start(s32[64]{0:T(128)} %param.17) | copy-start | bytes 772
  8.4 0.7 %copy-start.8 = (f32[8]{0:T(128)S(1)}, f32[8]{0:T(128)}, u32[]{:S(2)}) copy-start(f32[8]{0:T(128)} %lower_table.1) | copy-start | bytes 100
  9.0 0.7 %copy-start.9 = (f32[8]{0:T(128)S(1)}, f32[8]{0:T(128)}, u32[]{:S(2)}) copy-start(f32[8]{0:T(128)} %upper_table.1) | copy-start | bytes 100
  9.7 15.7 %copy-start.10 = (f32[32,128]{1,0:T(8,128)S(1)}, f32[32,128]{1,0:T(8,128)}, u32[]{:S(2)}) copy-start(f32[32,128]{1,0:T(8,128)} %param.14) | copy-start | bytes 49156
  13.8 1.9 %copy-start = (bf16[32,256,256]{2,1,0:T(8,128)(2,1)}, bf16[32,256,256]{2,1,0:T(8,128)(2,1)S(1)}, u32[]{:S(2)}) copy-start(bf16[32,256,256]{2,1,0:T(8,128)(2,1)S(1)} %get-tuple-element.15.packed) | copy-start | bytes 12582916
  15.7 2.0 %collective-permute-start.2 = (f32[96,128]{1,0:T(8,128)S(1)}, f32[96,128]{1,0:T(8,128)S(1)}, u32[]{:S(2)}, u32[]{:S(2)}) collective-permute-start(f32[96,128]{1,0:T(8,128)S(1)} %get-tuple-element.23), channel_id=1, source_target_pairs={{0,16},{1,17},{2,18},{3,19},{4,20},{5,21},{6,22},{7,23},{8,24},{9,... | collective-permute-start | bytes 147464 | tf_op jit(solution)/shard_map/ppermute | solution.py:189
  17.7 6.4 %collective-permute-start.3 = (f32[64,128]{1,0:T(8,128)S(1)}, f32[64,128]{1,0:T(8,128)S(1)}, u32[]{:S(2)}, u32[]{:S(2)}) collective-permute-start(f32[64,128]{1,0:T(8,128)S(1)} %slice_select_fusion), channel_id=1, source_target_pairs={{0,1},{1,2},{2,3},{3,4},{4,5},{5,6},{6,7},{7,8},{8,9},{9,10},{10,1... | collective-permute-start | bytes 98312 | tf_op jit(solution)/shard_map/ppermute | solution.py:287
  20.3 3.7 %collective-permute-start.4 = (f32[32,128]{1,0:T(8,128)S(1)}, f32[32,128]{1,0:T(8,128)S(1)}, u32[]{:S(2)}, u32[]{:S(2)}) collective-permute-start(f32[32,128]{1,0:T(8,128)S(1)} %slice_select_fusion.5), channel_id=1, source_target_pairs={{0,2},{1,3},{2,4},{3,5},{4,6},{5,7},{6,8},{7,9},{8,10},{9,11},{10,... | collective-permute-start | bytes 49160 | tf_op jit(solution)/shard_map/ppermute | solution.py:288
  24.1 1.3 %collective-permute-start.5 = (f32[64,128]{1,0:T(8,128)S(1)}, f32[64,128]{1,0:T(8,128)S(1)}, u32[]{:S(2)}, u32[]{:S(2)}) collective-permute-start(f32[64,128]{1,0:T(8,128)S(1)} %pad_maximum_fusion.2), channel_id=1, source_target_pairs={{0,16},{1,17},{2,18},{3,19},{4,20},{5,21},{6,22},{7,23},{8,24},{9,... | collective-permute-start | bytes 98312 | tf_op jit(solution)/shard_map/ppermute | solution.py:189
  25.4 2.2 %copy-start.1 = (bf16[32,256,256]{2,1,0:T(8,128)(2,1)S(1)}, bf16[32,256,256]{2,1,0:T(8,128)(2,1)}, u32[]{:S(2)}) copy-start(bf16[32,256,256]{2,1,0:T(8,128)(2,1)} %copy-done) | copy-start | bytes 12582916
  29.9 1.3 %collective-permute-start.6 = (f32[96,128]{1,0:T(8,128)S(1)}, f32[96,128]{1,0:T(8,128)S(1)}, u32[]{:S(2)}, u32[]{:S(2)}) collective-permute-start(f32[96,128]{1,0:T(8,128)S(1)} %get-tuple-element.25), channel_id=1, source_target_pairs={{0,16},{1,17},{2,18},{3,19},{4,20},{5,21},{6,22},{7,23},{8,24},{9,... | collective-permute-start | bytes 147464 | tf_op jit(solution)/shard_map/ppermute | solution.py:189
  31.2 3.8 %collective-permute-start.7 = (f32[32,128]{1,0:T(8,128)S(1)}, f32[32,128]{1,0:T(8,128)S(1)}, u32[]{:S(2)}, u32[]{:S(2)}) collective-permute-start(f32[32,128]{1,0:T(8,128)S(1)} %get-tuple-element.30), channel_id=1, source_target_pairs={{0,1},{1,2},{2,3},{3,4},{4,5},{5,6},{6,7},{7,8},{8,9},{9,10},{10,1... | collective-permute-start | bytes 49160 | tf_op jit(solution)/shard_map/ppermute | solution.py:213
  33.2 5.5 %collective-permute-start.8 = (f32[32,128]{1,0:T(8,128)S(1)}, f32[32,128]{1,0:T(8,128)S(1)}, u32[]{:S(2)}, u32[]{:S(2)}) collective-permute-start(f32[32,128]{1,0:T(8,128)S(1)} %get-tuple-element.31), channel_id=1, source_target_pairs={{1,0},{2,1},{3,2},{4,3},{5,4},{6,5},{7,6},{8,7},{9,8},{10,9},{11,1... | collective-permute-start | bytes 49160 | tf_op jit(solution)/shard_map/ppermute | solution.py:214

commit v2 on v1

v2 whole, which is shorter than its diff:
```python
import functools

import jax
import jax.numpy as jnp
from jax import lax
from jax.experimental import pallas as pl
from jax.experimental.pallas import tpu as pltpu
from jax.sharding import PartitionSpec as P

ITERS = 2
AXES = ("grp", "tm")
primal_step = 0.6
dual_step = 0.6
f32 = jnp.float32
bf16 = jnp.bfloat16


def split(value):
    high = value.astype(bf16)
    return high, (value - high.astype(f32)).astype(bf16)


def prep_kernel(
    chunks,
    tiles,
    rows,
    cols,
    count,
    classes,
    lower_table,
    upper_table,
    primal,
    cost,
    dual,
    rhs,
    packed,
    row_pick,
    row_sum,
    col_pick,
    col_sum,
    lower,
    upper,
    primal_out,
    cost_out,
    dual_out,
    rhs_out,
    held,
    rows_in,
    cols_in,
    classes_in,
    lower_in,
    upper_in,
    sems,
):
    total, size = tiles.shape[0], tiles.shape[1]
    step = total // chunks
    small = []
    for source, target in (
        (rows, rows_in),
        (cols, cols_in),
        (classes, classes_in),
        (lower_table, lower_in),
        (upper_table, upper_in),
        (primal, primal_out),
        (cost, cost_out),
        (dual, dual_out),
        (rhs, rhs_out),
    ):
        copy = pltpu.make_async_copy(source, target, sems.at[chunks + len(small)])
        copy.start()
        small.append(copy)
    copies = []
    for k in range(chunks):
        part = pl.ds(k * step, step)
        copy = pltpu.make_async_copy(tiles.at[part], held.at[part], sems.at[k])
        copy.start()
        copies.append(copy)
    for copy in small:
        copy.wait()
    time = lax.axis_index("tm")
    device = lax.axis_index("grp") * lax.axis_size("tm") + time
    slot = lax.broadcasted_iota(jnp.int32, (1, total), 1)
    live = slot < count[0]
    row_total = row_sum.shape[0]
    col_total = col_sum.shape[0]
    local_rows = rows_in[...] - (time - 1) * (row_total // 3)
    local_cols = cols_in[...] - device * col_total
    for local, total_out, pick, summed in (
        (local_rows, row_total, row_pick, row_sum),
        (local_cols, col_total, col_pick, col_sum),
    ):
        hit = lax.broadcasted_iota(jnp.int32, (total_out, total), 0) == local
        alive = jnp.where(hit & live, 1.0, 0.0).astype(f32)
        summed[...] = jnp.concatenate([alive, alive], axis=1).astype(bf16)
        pick[...] = jnp.transpose(jnp.where(hit, 1.0, 0.0).astype(f32)).astype(bf16)
    low = jnp.zeros(classes.shape, f32)
    high = jnp.zeros(classes.shape, f32)
    for k in range(lower_table.shape[0]):
        low = jnp.where(classes_in[...] == k, lower_in[k], low)
        high = jnp.where(classes_in[...] == k, upper_in[k], high)
    lower[...] = low
    upper[...] = high
    for k in range(chunks):
        copies[k].wait()
        for n in range(k * step, (k + 1) * step):
            tile_high, tile_low = split(held[n])
            lanes = pl.ds(n % 2 * size, size)
            packed[n // 2, pl.ds(0, size), lanes] = tile_high
            packed[n // 2, pl.ds(size, size), lanes] = tile_low


def products(packed, picked_high, picked_low, transposed):
    total, size = picked_high.shape
    row = lax.broadcasted_iota(jnp.int32, (8, size), 0)
    even = row % 2 == 0
    both = jnp.concatenate([even, even], axis=0)
    outs = []
    for q in range(total // 8):
        part = slice(8 * q, 8 * q + 8)
        left = jnp.concatenate([picked_high[part], picked_low[part]], axis=0)
        if transposed:
            zero = jnp.zeros_like(left)
            left = jnp.concatenate(
                [jnp.where(both, left, zero), jnp.where(both, zero, left)], axis=1
            )
        else:
            left = jnp.concatenate([left, left], axis=1)
        left = left.astype(bf16)
        result = jnp.zeros((8, size), f32)
        for j in range(4):
            out = lax.dot_general(
                left,
                packed[4 * q + j],
                (((1,), (1 if transposed else 0,)), ((), ())),
                preferred_element_type=f32,
            )
            out = out[:8] + out[8:]
            if transposed:
                term = out[:, :size] + out[:, size:]
            else:
                term = jnp.where(even, out[:, :size], out[:, size:])
            result = jnp.where(row // 2 == j, term, result)
        outs.append(result)
    return jnp.concatenate(outs, axis=0)


def pick(selector, values):
    size = values.shape[1]
    both = jnp.concatenate(split(values), axis=1)
    out = jnp.dot(selector[...], both, preferred_element_type=f32)
    return out[:, :size], out[:, size:]


def summed(selector, values):
    both = jnp.concatenate(split(values), axis=0)
    return jnp.dot(selector[...], both, preferred_element_type=f32)


def iterate(state, view, primal, base):
    packed, row_pick, row_sum, col_pick, col_sum, lower, upper, cost = state
    blocks = base.shape[0]
    high, low = pick(row_pick, view)
    adjoint = summed(col_sum, products(packed, high, low, False))
    moved = primal[...] - primal_step * (cost[...] - adjoint)
    primal_next = jnp.minimum(jnp.maximum(moved, lower[...]), upper[...])
    high, low = pick(col_pick, 2.0 * primal_next - primal[...])
    window = summed(row_sum, products(packed, high, low, True)) * (-dual_step)
    first = (lax.axis_index("grp") == 0).astype(f32)
    own = window[blocks : 2 * blocks] + base * first
    window = jnp.concatenate([window[:blocks], own, window[2 * blocks :]], axis=0)
    return primal_next, window


def rises():
    return lax.rem(lax.axis_index("grp"), 2) == 0


def first_kernel(*refs):
    state, (primal, dual, rhs, forth, reverse), (primal_out, window_out) = (
        refs[:8],
        refs[8:13],
        refs[13:],
    )
    rising = rises()
    above = jnp.where(rising, forth[...], reverse[...])
    below = jnp.where(rising, reverse[...], forth[...])
    view = jnp.concatenate([above, dual[...], below], axis=0)
    primal_out[...], window_out[...] = iterate(
        state, view, primal, dual[...] + dual_step * rhs[...]
    )


def fold_kernel(window, other, summed_out, near_out, far_out):
    blocks = far_out.shape[0]
    total = window[...] + other[...]
    summed_out[...] = total
    rising = rises()
    near_out[...] = jnp.where(rising, total[blocks:], total[: 2 * blocks])
    far_out[...] = jnp.where(rising, total[2 * blocks :], total[:blocks])


def side_kernel(window, near, far, sent):
    blocks = far.shape[0]
    rising = rises()
    time, times = lax.axis_index("tm"), lax.axis_size("tm")
    rank = jnp.where(rising, time, times - 1 - time)
    above, own, below = (window[pl.ds(k * blocks, blocks)] for k in range(3))
    first, last = near[pl.ds(0, blocks)], near[pl.ds(blocks, blocks)]
    part = jnp.where(rising, last, first)
    side = jnp.where(rising, first + above, last + below)
    side = side + jnp.where(rank >= 2, far[...], 0.0)
    sent[pl.ds(0, blocks)] = jnp.maximum(side, 0.0)
    sent[pl.ds(blocks, blocks)] = jnp.where(rank >= 1, part, 0.0)


def later_kernel(*refs):
    state, (primal, rhs, total, sent, got), (primal_out, window_out, mean_out, dual_out) = (
        refs[:8],
        refs[8:13],
        refs[13:],
    )
    blocks = rhs.shape[0]
    rising = rises()
    side, part = (sent[pl.ds(k * blocks, blocks)] for k in range(2))
    other, other_part = (got[pl.ds(k * blocks, blocks)] for k in range(2))
    dual = jnp.maximum(total[pl.ds(blocks, blocks)] + (part + other_part), 0.0)
    above = jnp.where(rising, side, other)
    below = jnp.where(rising, other, side)
    view = jnp.concatenate([above, dual, below], axis=0)
    primal_next, window = iterate(state, view, primal, dual + dual_step * rhs[...])
    primal_out[...] = primal_next
    window_out[...] = window
    mean_out[...] = (primal[...] + primal_next) / ITERS
    dual_out[...] = dual


def last_fold_kernel(window, other, own_out, forth_out, reverse_out):
    blocks = own_out.shape[0]
    total = window[...] + other[...]
    own_out[...] = total[blocks : 2 * blocks]
    rising = rises()
    forth_out[...] = jnp.where(rising, total[2 * blocks :], total[:blocks])
    reverse_out[...] = jnp.where(rising, total[:blocks], total[2 * blocks :])


def vmem(count):
    return [pl.BlockSpec(memory_space=pltpu.VMEM)] * count


def body(
    groups,
    times,
    x_start,
    y_start,
    cost,
    rhs,
    tiles,
    tile_rows,
    tile_cols,
    tile_count,
    var_class,
    lower_table,
    upper_table,
):
    total, size = tiles.shape[0], tiles.shape[1]
    cols, rows = x_start.shape[0], y_start.shape[0]
    tm = lax.axis_index("tm")
    rising = lax.rem(lax.axis_index("grp"), 2) == 0

    def number(g, t):
        return g * times + t

    def swap(value, bit):
        route = [
            (number(g, t), number(g ^ bit, t)) for g in range(groups) for t in range(times)
        ]
        return lax.ppermute(value, AXES, route)

    def group_sum(value):
        bit = 1
        while 2 * bit < groups:
            value = value + swap(value, bit)
            bit *= 2
        return value, swap(value, bit)

    def ring(distance):
        route = []
        for g in range(groups):
            for t in range(times):
                target = t + distance if g % 2 == 0 else t - distance
                if 0 <= target < times:
                    route.append((number(g, t), number(g, target)))
                else:
                    route.append((number(g, t), number(g ^ 1, t)))
        return route

    def back(distance):
        return [(target, source) for source, target in ring(distance)]

    def shape(count, kind=f32, width=size):
        return jax.ShapeDtypeStruct((count, width), kind)

    def kernel(code, name, outs, args, limit=1 << 20, passes=0):
        return pl.pallas_call(
            code,
            out_shape=tuple(outs),
            in_specs=vmem(len(args)),
            out_specs=tuple(vmem(len(outs))),
            compiler_params=pltpu.CompilerParams(vmem_limit_bytes=limit),
            cost_estimate=pl.CostEstimate(
                flops=4 * passes * total * size * size,
                bytes_accessed=4 * passes * total * size * size,
                transcendentals=0,
            ),
            name=name,
        )(*args)

    chunks = 8
    inputs = (
        tiles,
        tile_rows[None, :],
        tile_cols[None, :],
        tile_count,
        var_class,
        lower_table,
        upper_table,
        x_start,
        cost,
        y_start,
        rhs,
    )
    forth = lax.ppermute(y_start, AXES, ring(1))
    reverse = lax.ppermute(y_start, AXES, back(1))
    outs = (
        jax.ShapeDtypeStruct((total // 2, 2 * size, 2 * size), bf16),
        shape(total, bf16, 3 * rows),
        shape(3 * rows, bf16, 2 * total),
        shape(total, bf16, cols),
        shape(cols, bf16, 2 * total),
        shape(cols),
        shape(cols),
        shape(cols),
        shape(cols),
        shape(rows),
        shape(rows),
    )
    *selectors, lower, upper, primal, cost, dual, rhs = pl.pallas_call(
        functools.partial(prep_kernel, chunks),
        out_shape=outs,
        in_specs=[
            pl.BlockSpec(memory_space=pltpu.SMEM if value is tile_count else pltpu.HBM)
            for value in inputs
        ],
        out_specs=tuple(vmem(len(outs))),
        scratch_shapes=[
            pltpu.VMEM(tiles.shape, f32),
            pltpu.VMEM((1, total), jnp.int32),
            pltpu.VMEM((1, total), jnp.int32),
            pltpu.VMEM(var_class.shape, jnp.int32),
            pltpu.SMEM(lower_table.shape, f32),
            pltpu.SMEM(upper_table.shape, f32),
            pltpu.SemaphoreType.DMA((chunks + 9,)),
        ],
        compiler_params=pltpu.CompilerParams(vmem_limit_bytes=16 << 20),
        cost_estimate=pl.CostEstimate(
            flops=4 * total * size * size,
            bytes_accessed=8 * total * size * size,
            transcendentals=0,
        ),
        name="prep",
    )(
        *(
            value if value is tile_count else pltpu.with_memory_space_constraint(value, pltpu.HBM)
            for value in inputs
        )
    )
    state = (*selectors, lower, upper, cost)

    primal_1, window = kernel(
        first_kernel,
        "first",
        (shape(cols), shape(3 * rows)),
        (*state, primal, dual, rhs, forth, reverse),
        limit=16 << 20,
        passes=2,
    )
    window, near, far = kernel(
        fold_kernel,
        "fold",
        (shape(3 * rows), shape(2 * rows), shape(rows)),
        group_sum(window),
    )
    near = lax.ppermute(near, AXES, ring(1))
    far = lax.ppermute(far, AXES, ring(2))
    (sent,) = kernel(side_kernel, "side", (shape(2 * rows),), (window, near, far))
    got = swap(sent, 1)
    primal_2, window, primal_mean, dual_1 = kernel(
        later_kernel,
        "later",
        (shape(cols), shape(3 * rows), shape(cols), shape(rows)),
        (*state, primal_1, rhs, window, sent, got),
        limit=16 << 20,
        passes=2,
    )
    own, forth, reverse = kernel(
        last_fold_kernel,
        "last_fold",
        (shape(rows),) * 3,
        group_sum(window),
    )
    forth = lax.ppermute(forth, AXES, ring(1))
    reverse = lax.ppermute(reverse, AXES, back(1))
    above = jnp.where(tm >= 1, jnp.where(rising, forth, reverse), 0.0)
    below = jnp.where(tm + 1 < times, jnp.where(rising, reverse, forth), 0.0)
    dual_2 = jnp.maximum(own + (above + below), 0.0)
    return primal_2, dual_2, primal_mean, (dual_1 + dual_2) / ITERS


def solution(mesh):
    groups, times = mesh.shape["grp"], mesh.shape["tm"]
    return jax.shard_map(
        functools.partial(body, groups, times),
        mesh=mesh,
        in_specs=(
            P(("grp", "tm"), None),
            P("tm", None),
            P(("grp", "tm"), None),
            P("tm", None),
            P(("grp", "tm"), None, None),
            P(("grp", "tm")),
            P(("grp", "tm")),
            P(("grp", "tm")),
            P(("grp", "tm"), None),
            P(),
            P(),
        ),
        out_specs=(P(("grp", "tm"), None), P("tm", None), P(("grp", "tm"), None), P("tm", None)),
        check_vma=False,
    )
```

time: 39.8 us -> 30.3 us (0.76)
  the two profiles are of different devices: /device:TPU:6 before, /device:TPU:16 now
where the time goes in v2:
time: 30.3 us; the launch traced here: 30.2 us
  waiting for transfers between devices  11.4 us (38%)
  starting transfers between devices  9.62 us (32%)
  Pallas kernels  7.15 us (24%)
  between operations  1.36 us (4%)
  other arithmetic  0.62 us (2%)
    pallas_call x5, Pallas kernels, kernel(): pl.pallas_call(code, out_shape=tuple(outs), in_specs=vmem(len(args)), out...  4.65 us
    ppermute x3, waiting for transfers between devices, swap(): return lax.ppermute(value, AXES, route)  3.48 us
    ppermute x1, waiting for transfers between devices, body(): forth = lax.ppermute(forth, AXES, ring(1))  3.47 us
    pallas_call x1, Pallas kernels, body(): pl.pallas_call(functools.partial(prep_kernel, chunks), out_shape=outs, in...  2.5 us
    ppermute x1, starting transfers between devices, body(): far = lax.ppermute(far, AXES, ring(2))  2.42 us
    ppermute x1, starting transfers between devices, body(): reverse = lax.ppermute(y_start, AXES, back(1))  2.33 us
    ppermute x1, waiting for transfers between devices, body(): far = lax.ppermute(far, AXES, ring(2))  2.31 us
    ppermute x1, starting transfers between devices, body(): reverse = lax.ppermute(reverse, AXES, back(1))  1.9 us
  transfers between devices with their start and end apart: 9, of which 7 were waited for; matrix products, arithmetic and copies ran while one was open for 0% of the time, Pallas kernels for 8%

profile of v2, /device:TPU:16, one launch (start us, length us, event | category | flops | bytes accessed | tf_op | source)
XLA Modules:
  0.0 30.2 jit_solution(5518756902387298330)
XLA Ops:
  0.6 1.5 %collective-permute-start = (f32[32,128]{1,0:T(8,128)}, f32[32,128]{1,0:T(8,128)S(1)}, u32[]{:S(2)}, u32[]{:S(2)}) collective-permute-start(f32[32,128]{1,0:T(8,128)} %dual.1), channel_id=1, source_target_pairs={{0,1},{1,2},{2,3},{3,4},{4,5},{5,6},{6,7},{7,8},{8,9},{9,10},{10,1... | collective-permute-start | bytes 49160 | tf_op jit(solution)/shard_map/ppermute | solution.py:332
  2.2 2.3 %collective-permute-start.1 = (f32[32,128]{1,0:T(8,128)}, f32[32,128]{1,0:T(8,128)S(1)}, u32[]{:S(2)}, u32[]{:S(2)}) collective-permute-start(f32[32,128]{1,0:T(8,128)} %dual.1), channel_id=1, source_target_pairs={{1,0},{2,1},{3,2},{4,3},{5,4},{6,5},{7,6},{8,7},{9,8},{10,9},{11,1... | collective-permute-start | bytes 49160 | tf_op jit(solution)/shard_map/ppermute | solution.py:333
  5.2 2.5 %prep.1 = (bf16[32,256,256]{2,1,0:T(8,128)(2,1)S(1)}, bf16[64,96]{1,0:T(8,128)(2,1)S(1)}, bf16[96,128]{1,0:T(8,128)(2,1)S(1)}, bf16[64,16]{1,0:T(8,128)(2,1)S(1)...) custom-call(f32[64,128,128]{2,1,0:T(8,128)} %tiles.1, ...), custom_call_target="tpu_custom_call" | custom-call | flops 4194304 | bytes 8388608 | tf_op jit(solution)/shard_map/prep/pallas_call | solution.py:347
  7.7 0.0 collective-permute-done.refs_11_
  7.7 0.0 collective-permute-done.1.refs_12_
  7.7 2.3 %first.1 = (f32[16,128]{1,0:T(8,128)S(1)}, f32[96,128]{1,0:T(8,128)S(1)}) custom-call(bf16[32,256,256]{2,1,0:T(8,128)(2,1)S(1)} %get-tuple-element.27.refs_0_, bf16[64,96]{1,0:T(8,128)(2,1)S(1)} %get-tuple-element.28.refs_1_, bf16[96,128]{1,0:T(8,128)(2,1)S(1)} %get-tuple-element.29.refs_2_, bf16[64,16]{1,0:T(8,128)(2,1)S(1)} %get-tuple-element.30.refs_3_, ...), custom_call_target="tpu_custom_call" | custom-call | flops 8388608 | bytes 8388608 | tf_op jit(solution)/shard_map/first/pallas_call | solution.py:304
  10.0 0.1 collective-permute-start.2
  10.1 1.2 %collective-permute-done.2.other = f32[96,128]{1,0:T(8,128)S(1)} collective-permute-done((f32[96,128]{1,0:T(8,128)S(1)}, f32[96,128]{1,0:T(8,128)S(1)}, u32[]{:S(2)}, u32[]{:S(2)}) %collective-permute-start.2) | collective-permute-done | bytes 49184 | tf_op jit(solution)/shard_map/ppermute | solution.py:277
  11.3 0.9 %collective-permute-start.3 = (f32[64,128]{1,0:T(8,128)S(1)}, f32[64,128]{1,0:T(8,128)S(1)}, u32[]{:S(2)}, u32[]{:S(2)}) collective-permute-start(f32[64,128]{1,0:T(8,128)S(1)} %get-tuple-element.41), channel_id=1, source_target_pairs={{0,1},{1,2},{2,3},{3,4},{4,5},{5,6},{6,7},{7,8},{8,9},{9,10},{10,1... | collective-permute-start | bytes 98312 | tf_op jit(solution)/shard_map/ppermute | solution.py:393
  12.2 2.4 %collective-permute-start.4 = (f32[32,128]{1,0:T(8,128)S(1)}, f32[32,128]{1,0:T(8,128)S(1)}, u32[]{:S(2)}, u32[]{:S(2)}) collective-permute-start(f32[32,128]{1,0:T(8,128)S(1)} %get-tuple-element.42), channel_id=1, source_target_pairs={{0,2},{1,3},{2,4},{3,5},{4,6},{5,7},{6,8},{7,9},{8,10},{9,11},{10,... | collective-permute-start | bytes 49160 | tf_op jit(solution)/shard_map/ppermute | solution.py:394
  14.6 2.3 %collective-permute-done.4.far = f32[32,128]{1,0:T(8,128)S(1)} collective-permute-done((f32[32,128]{1,0:T(8,128)S(1)}, f32[32,128]{1,0:T(8,128)S(1)}, u32[]{:S(2)}, u32[]{:S(2)}) %collective-permute-start.4) | collective-permute-done | bytes 16416 | tf_op jit(solution)/shard_map/ppermute | solution.py:394
  16.9 0.3 collective-permute-done.3.near
  17.2 0.1 collective-permute-start.5
  17.3 1.2 %collective-permute-done.5.refs_12_ = f32[64,128]{1,0:T(8,128)S(1)} collective-permute-done((f32[64,128]{1,0:T(8,128)S(1)}, f32[64,128]{1,0:T(8,128)S(1)}, u32[]{:S(2)}, u32[]{:S(2)}) %collective-permute-start.5) | collective-permute-done | bytes 32800 | tf_op jit(solution)/shard_map/ppermute | solution.py:277
  18.5 2.3 %later.1 = (f32[16,128]{1,0:T(8,128)}, f32[96,128]{1,0:T(8,128)S(1)}, f32[16,128]{1,0:T(8,128)}, f32[32,128]{1,0:T(8,128)S(1)}) custom-call(bf16[32,256,256]{2,1,0:T(8,128)(2,1)S(1)} %get-tuple-element.27.refs_0_, bf16[64,96]{1,0:T(8,128)(2,1)S(1)} %get-tuple-element.28.refs_1_, bf16[96,128]{1,0:T(8,128)(2,1)S(1)} %get-tuple-element.29.refs_2_, ...), custom_call_target="tpu_custom_call" | custom-call | flops 8388608 | bytes 8388608 | tf_op jit(solution)/shard_map/later/pallas_call | solution.py:304
  20.8 0.2 collective-permute-start.6
  21.0 1.1 %collective-permute-done.6.other = f32[96,128]{1,0:T(8,128)S(1)} collective-permute-done((f32[96,128]{1,0:T(8,128)S(1)}, f32[96,128]{1,0:T(8,128)S(1)}, u32[]{:S(2)}, u32[]{:S(2)}) %collective-permute-start.6) | collective-permute-done | bytes 49184 | tf_op jit(solution)/shard_map/ppermute | solution.py:277
  22.1 1.9 %collective-permute-start.8 = (f32[32,128]{1,0:T(8,128)S(1)}, f32[32,128]{1,0:T(8,128)S(1)}, u32[]{:S(2)}, u32[]{:S(2)}) collective-permute-start(f32[32,128]{1,0:T(8,128)S(1)} %get-tuple-element.47), channel_id=1, source_target_pairs={{1,0},{2,1},{3,2},{4,3},{5,4},{6,5},{7,6},{8,7},{9,8},{10,9},{11,1... | collective-permute-start | bytes 49160 | tf_op jit(solution)/shard_map/ppermute | solution.py:412
  24.0 0.2 collective-permute-start.7
  24.2 1.9 %collective-permute-done.8 = f32[32,128]{1,0:T(8,128)S(1)} collective-permute-done((f32[32,128]{1,0:T(8,128)S(1)}, f32[32,128]{1,0:T(8,128)S(1)}, u32[]{:S(2)}, u32[]{:S(2)}) %collective-permute-start.8) | collective-permute-done | bytes 16416 | tf_op jit(solution)/shard_map/ppermute | solution.py:412
  26.1 3.5 %collective-permute-done.7 = f32[32,128]{1,0:T(8,128)S(1)} collective-permute-done((f32[32,128]{1,0:T(8,128)S(1)}, f32[32,128]{1,0:T(8,128)S(1)}, u32[]{:S(2)}, u32[]{:S(2)}) %collective-permute-start.7) | collective-permute-done | bytes 16416 | tf_op jit(solution)/shard_map/ppermute | solution.py:411
  29.5 0.6 %add_multiply_fusion = (f32[32,128]{1,0:T(8,128)}, f32[32,128]{1,0:T(8,128)}) fusion(f32[32,128]{1,0:T(8,128)S(1)} %get-tuple-element.49, f32[32,128]{1,0:T(8,128)S(1)} %get-tuple-element.45, f32[32,128]{1,0:T(8,128)S(1)} %collective-permute-done.8, f32[32,128]{1,0:T(8,128)S(1)} %collective-permute-done.7, pred[]{:T(512)S(6)} %lt.3, pred[]{:T(512)S(6)} %eq.3, ...), kind=kLoop, calls=%fused_computation | loop fusion | flops 36864 | bytes 98307 | tf_op jit(solution)/shard_map/div | solution.py:416
  (3 shorter events, 0.0 us)
Async XLA Ops:
  0.6 7.0 %collective-permute-start = (f32[32,128]{1,0:T(8,128)}, f32[32,128]{1,0:T(8,128)S(1)}, u32[]{:S(2)}, u32[]{:S(2)}) collective-permute-start(f32[32,128]{1,0:T(8,128)} %dual.1), channel_id=1, source_target_pairs={{0,1},{1,2},{2,3},{3,4},{4,5},{5,6},{6,7},{7,8},{8,9},{9,10},{10,1... | collective-permute-start | bytes 49160 | tf_op jit(solution)/shard_map/ppermute | solution.py:332
  2.2 5.5 %collective-permute-start.1 = (f32[32,128]{1,0:T(8,128)}, f32[32,128]{1,0:T(8,128)S(1)}, u32[]{:S(2)}, u32[]{:S(2)}) collective-permute-start(f32[32,128]{1,0:T(8,128)} %dual.1), channel_id=1, source_target_pairs={{1,0},{2,1},{3,2},{4,3},{5,4},{6,5},{7,6},{8,7},{9,8},{10,9},{11,1... | collective-permute-start | bytes 49160 | tf_op jit(solution)/shard_map/ppermute | solution.py:333
  10.0 1.3 %collective-permute-start.2 = (f32[96,128]{1,0:T(8,128)S(1)}, f32[96,128]{1,0:T(8,128)S(1)}, u32[]{:S(2)}, u32[]{:S(2)}) collective-permute-start(f32[96,128]{1,0:T(8,128)S(1)} %get-tuple-element.39.window), channel_id=1, source_target_pairs={{0,16},{1,17},{2,18},{3,19},{4,20},{5,21},{6,22},{7,23},{8,24},{9,... | collective-permute-start | bytes 147464 | tf_op jit(solution)/shard_map/ppermute | solution.py:277
  11.3 5.9 %collective-permute-start.3 = (f32[64,128]{1,0:T(8,128)S(1)}, f32[64,128]{1,0:T(8,128)S(1)}, u32[]{:S(2)}, u32[]{:S(2)}) collective-permute-start(f32[64,128]{1,0:T(8,128)S(1)} %get-tuple-element.41), channel_id=1, source_target_pairs={{0,1},{1,2},{2,3},{3,4},{4,5},{5,6},{6,7},{7,8},{8,9},{9,10},{10,1... | collective-permute-start | bytes 98312 | tf_op jit(solution)/shard_map/ppermute | solution.py:393
  12.2 4.7 %collective-permute-start.4 = (f32[32,128]{1,0:T(8,128)S(1)}, f32[32,128]{1,0:T(8,128)S(1)}, u32[]{:S(2)}, u32[]{:S(2)}) collective-permute-start(f32[32,128]{1,0:T(8,128)S(1)} %get-tuple-element.42), channel_id=1, source_target_pairs={{0,2},{1,3},{2,4},{3,5},{4,6},{5,7},{6,8},{7,9},{8,10},{9,11},{10,... | collective-permute-start | bytes 49160 | tf_op jit(solution)/shard_map/ppermute | solution.py:394
  17.2 1.3 %collective-permute-start.5 = (f32[64,128]{1,0:T(8,128)S(1)}, f32[64,128]{1,0:T(8,128)S(1)}, u32[]{:S(2)}, u32[]{:S(2)}) collective-permute-start(f32[64,128]{1,0:T(8,128)S(1)} %side.1.refs_11_), channel_id=1, source_target_pairs={{0,16},{1,17},{2,18},{3,19},{4,20},{5,21},{6,22},{7,23},{8,24},{9,... | collective-permute-start | bytes 98312 | tf_op jit(solution)/shard_map/ppermute | solution.py:277
  20.8 1.3 %collective-permute-start.6 = (f32[96,128]{1,0:T(8,128)S(1)}, f32[96,128]{1,0:T(8,128)S(1)}, u32[]{:S(2)}, u32[]{:S(2)}) collective-permute-start(f32[96,128]{1,0:T(8,128)S(1)} %get-tuple-element.44.window), channel_id=1, source_target_pairs={{0,16},{1,17},{2,18},{3,19},{4,20},{5,21},{6,22},{7,23},{8,24},{9,... | collective-permute-start | bytes 147464 | tf_op jit(solution)/shard_map/ppermute | solution.py:277
  22.1 4.0 %collective-permute-start.8 = (f32[32,128]{1,0:T(8,128)S(1)}, f32[32,128]{1,0:T(8,128)S(1)}, u32[]{:S(2)}, u32[]{:S(2)}) collective-permute-start(f32[32,128]{1,0:T(8,128)S(1)} %get-tuple-element.47), channel_id=1, source_target_pairs={{1,0},{2,1},{3,2},{4,3},{5,4},{6,5},{7,6},{8,7},{9,8},{10,9},{11,1... | collective-permute-start | bytes 49160 | tf_op jit(solution)/shard_map/ppermute | solution.py:412
  24.0 5.5 %collective-permute-start.7 = (f32[32,128]{1,0:T(8,128)S(1)}, f32[32,128]{1,0:T(8,128)S(1)}, u32[]{:S(2)}, u32[]{:S(2)}) collective-permute-start(f32[32,128]{1,0:T(8,128)S(1)} %get-tuple-element.46), channel_id=1, source_target_pairs={{0,1},{1,2},{2,3},{3,4},{4,5},{5,6},{6,7},{7,8},{8,9},{9,10},{10,1... | collective-permute-start | bytes 49160 | tf_op jit(solution)/shard_map/ppermute | solution.py:411

commit v3 on v2

--- a/solution.py
+++ b/solution.py
@@ -6,6 +6,7 @@
 from jax.experimental import pallas as pl
 from jax.experimental.pallas import tpu as pltpu
 from jax.sharding import PartitionSpec as P
+
 
 ITERS = 2
 AXES = ("grp", "tm")
@@ -181,9 +182,9 @@
         refs[8:13],
         refs[13:],
     )
-    rising = rises()
-    above = jnp.where(rising, forth[...], reverse[...])
-    below = jnp.where(rising, reverse[...], forth[...])
+    even = lax.rem(lax.axis_index("tm"), 2) == 0
+    above = jnp.where(even, forth[...], reverse[...])
+    below = jnp.where(even, reverse[...], forth[...])
     view = jnp.concatenate([above, dual[...], below], axis=0)
     primal_out[...], window_out[...] = iterate(
         state, view, primal, dual[...] + dual_step * rhs[...]
@@ -204,7 +205,7 @@
     rising = rises()
     time, times = lax.axis_index("tm"), lax.axis_size("tm")
     rank = jnp.where(rising, time, times - 1 - time)
-    above, own, below = (window[pl.ds(k * blocks, blocks)] for k in range(3))
+    above, _, below = (window[pl.ds(k * blocks, blocks)] for k in range(3))
     first, last = near[pl.ds(0, blocks)], near[pl.ds(blocks, blocks)]
     part = jnp.where(rising, last, first)
     side = jnp.where(rising, first + above, last + below)
@@ -238,9 +239,9 @@
     blocks = own_out.shape[0]
     total = window[...] + other[...]
     own_out[...] = total[blocks : 2 * blocks]
-    rising = rises()
-    forth_out[...] = jnp.where(rising, total[2 * blocks :], total[:blocks])
-    reverse_out[...] = jnp.where(rising, total[:blocks], total[2 * blocks :])
+    even = lax.rem(lax.axis_index("tm"), 2) == 0
+    forth_out[...] = jnp.where(even, total[:blocks], total[2 * blocks :])
+    reverse_out[...] = jnp.where(even, total[2 * blocks :], total[:blocks])
 
 
 def vmem(count):
@@ -265,7 +266,6 @@
     total, size = tiles.shape[0], tiles.shape[1]
     cols, rows = x_start.shape[0], y_start.shape[0]
     tm = lax.axis_index("tm")
-    rising = lax.rem(lax.axis_index("grp"), 2) == 0
 
     def number(g, t):
         return g * times + t
@@ -294,13 +294,26 @@
                     route.append((number(g, t), number(g ^ 1, t)))
         return route
 
-    def back(distance):
-        return [(target, source) for source, target in ring(distance)]
+    def pairs(odd):
+        route = []
+        for g in range(groups):
+            for t in range(times):
+                target = t + 1 if (t + odd) % 2 == 0 else t - 1
+                if 0 <= target < times:
+                    route.append((number(g, t), number(g, target)))
+                else:
+                    route.append((number(g, t), number(g ^ 1, t)))
+        return route
+
+    def exchange(odd, even):
+        odd = lax.ppermute(odd, AXES, pairs(1))
+        even = lax.ppermute(even, AXES, pairs(0))
+        return odd, even
 
     def shape(count, kind=f32, width=size):
         return jax.ShapeDtypeStruct((count, width), kind)
 
-    def kernel(code, name, outs, args, limit=1 << 20, passes=0):
+    def kernel(code, outs, args, limit=1 << 20, passes=0):
         return pl.pallas_call(
             code,
             out_shape=tuple(outs),
@@ -312,7 +325,6 @@
                 bytes_accessed=4 * passes * total * size * size,
                 transcendentals=0,
             ),
-            name=name,
         )(*args)
 
     chunks = 8
@@ -329,8 +341,7 @@
         y_start,
         rhs,
     )
-    forth = lax.ppermute(y_start, AXES, ring(1))
-    reverse = lax.ppermute(y_start, AXES, back(1))
+    forth, reverse = exchange(y_start, y_start)
     outs = (
         jax.ShapeDtypeStruct((total // 2, 2 * size, 2 * size), bf16),
         shape(total, bf16, 3 * rows),
@@ -378,40 +389,32 @@
 
     primal_1, window = kernel(
         first_kernel,
-        "first",
         (shape(cols), shape(3 * rows)),
         (*state, primal, dual, rhs, forth, reverse),
         limit=16 << 20,
         passes=2,
     )
     window, near, far = kernel(
-        fold_kernel,
-        "fold",
-        (shape(3 * rows), shape(2 * rows), shape(rows)),
-        group_sum(window),
+        fold_kernel, (shape(3 * rows), shape(2 * rows), shape(rows)), group_sum(window)
     )
     near = lax.ppermute(near, AXES, ring(1))
     far = lax.ppermute(far, AXES, ring(2))
-    (sent,) = kernel(side_kernel, "side", (shape(2 * rows),), (window, near, far))
+    (sent,) = kernel(side_kernel, (shape(2 * rows),), (window, near, far))
     got = swap(sent, 1)
     primal_2, window, primal_mean, dual_1 = kernel(
         later_kernel,
-        "later",
         (shape(cols), shape(3 * rows), shape(cols), shape(rows)),
         (*state, primal_1, rhs, window, sent, got),
         limit=16 << 20,
         passes=2,
     )
     own, forth, reverse = kernel(
-        last_fold_kernel,
-        "last_fold",
-        (shape(rows),) * 3,
-        group_sum(window),
-    )
-    forth = lax.ppermute(forth, AXES, ring(1))
-    reverse = lax.ppermute(reverse, AXES, back(1))
-    above = jnp.where(tm >= 1, jnp.where(rising, forth, reverse), 0.0)
-    below = jnp.where(tm + 1 < times, jnp.where(rising, reverse, forth), 0.0)
+        last_fold_kernel, (shape(rows),) * 3, group_sum(window)
+    )
+    forth, reverse = exchange(forth, reverse)
+    even = lax.rem(tm, 2) == 0
+    above = jnp.where(tm >= 1, jnp.where(even, forth, reverse), 0.0)
+    below = jnp.where(tm + 1 < times, jnp.where(even, reverse, forth), 0.0)
     dual_2 = jnp.maximum(own + (above + below), 0.0)
     return primal_2, dual_2, primal_mean, (dual_1 + dual_2) / ITERS
 

time: 30.3 us -> 29.5 us (0.974)
  starting transfers between devices: 9.62 us -> 8.03 us
  waiting for transfers between devices: 11.4 us -> 12.2 us
    ppermute x1, starting transfers between devices: 2.42 us -> 1.22 us  [body(): far = lax.ppermute(far, AXES, ring(2))]
    ppermute x1, waiting for transfers between devices: 2.31 us -> 3.42 us  [body(): far = lax.ppermute(far, AXES, ring(2))]
    ppermute x4, starting transfers between devices: 5.96 us -> 5.13 us  [the longest x2 2.81 us: exchange(): odd = lax.ppermute(odd, AXES, pairs(1))]
    ppermute x1, starting transfers between devices: 0.87 us -> 1.32 us  [body(): near = lax.ppermute(near, AXES, ring(1))]
  transfers between devices with their start and end apart: 9 -> 9, of which waited for: 7 -> 7; matrix products, arithmetic and copies ran while one was open for 0% -> 0% of each run, Pallas kernels for 8% -> 9%
where the time goes in v3:
time: 29.5 us; the launch traced here: 29.3 us
  waiting for transfers between devices  12.2 us (41%)
  starting transfers between devices  8.03 us (27%)
  Pallas kernels  7.15 us (24%)
  between operations  1.36 us (5%)
  other arithmetic  0.62 us (2%)
    pallas_call x5, Pallas kernels, kernel(): pl.pallas_call(code, out_shape=tuple(outs), in_specs=vmem(len(args)), out...  4.65 us
    ppermute x3, waiting for transfers between devices, swap(): return lax.ppermute(value, AXES, route)  3.48 us
    ppermute x1, waiting for transfers between devices, body(): far = lax.ppermute(far, AXES, ring(2))  3.42 us
    ppermute x2, waiting for transfers between devices, exchange(): odd = lax.ppermute(odd, AXES, pairs(1))  3.41 us
    ppermute x2, starting transfers between devices, exchange(): odd = lax.ppermute(odd, AXES, pairs(1))  2.81 us
    pallas_call x1, Pallas kernels, body(): pl.pallas_call(functools.partial(prep_kernel, chunks), out_shape=outs, in...  2.5 us
    ppermute x2, starting transfers between devices, exchange(): even = lax.ppermute(even, AXES, pairs(0))  2.32 us
    ppermute x2, waiting for transfers between devices, exchange(): even = lax.ppermute(even, AXES, pairs(0))  1.85 us
  transfers between devices with their start and end apart: 9, of which 7 were waited for; matrix products, arithmetic and copies ran while one was open for 0% of the time, Pallas kernels for 9%

profile of v3, /device:TPU:16, one launch (start us, length us, event | category | flops | bytes accessed | tf_op | source)
XLA Modules:
  0.0 29.3 jit_solution(16726175854066394358)
XLA Ops:
  0.6 2.4 %collective-permute-start = (f32[32,128]{1,0:T(8,128)}, f32[32,128]{1,0:T(8,128)S(1)}, u32[]{:S(2)}, u32[]{:S(2)}) collective-permute-start(f32[32,128]{1,0:T(8,128)} %dual.1), channel_id=1, source_target_pairs={{0,16},{1,2},{2,1},{3,4},{4,3},{5,6},{6,5},{7,8},{8,7},{9,10},{10,... | collective-permute-start | bytes 49160 | tf_op jit(solution)/shard_map/ppermute | solution.py:309
  3.0 0.6 %collective-permute-start.1 = (f32[32,128]{1,0:T(8,128)}, f32[32,128]{1,0:T(8,128)S(1)}, u32[]{:S(2)}, u32[]{:S(2)}) collective-permute-start(f32[32,128]{1,0:T(8,128)} %dual.1), channel_id=1, source_target_pairs={{0,1},{1,0},{2,3},{3,2},{4,5},{5,4},{6,7},{7,6},{8,9},{9,8},{10,11... | collective-permute-start | bytes 49160 | tf_op jit(solution)/shard_map/ppermute | solution.py:310
  4.3 2.5 %prep.1 = (bf16[32,256,256]{2,1,0:T(8,128)(2,1)S(1)}, bf16[64,96]{1,0:T(8,128)(2,1)S(1)}, bf16[96,128]{1,0:T(8,128)(2,1)S(1)}, bf16[64,16]{1,0:T(8,128)(2,1)S(1)...) custom-call(f32[64,128,128]{2,1,0:T(8,128)} %tiles.1, ...), custom_call_target="tpu_custom_call" | custom-call | flops 4194304 | bytes 8388608 | tf_op jit(solution)/shard_map/prep/pallas_call | solution.py:358
  6.8 0.0 collective-permute-done.refs_11_
  6.9 0.1 collective-permute-done.1.refs_12_
  7.0 2.3 %shard_map.138 = (f32[16,128]{1,0:T(8,128)S(1)}, f32[96,128]{1,0:T(8,128)S(1)}) custom-call(bf16[32,256,256]{2,1,0:T(8,128)(2,1)S(1)} %get-tuple-element.27.refs_0_, bf16[64,96]{1,0:T(8,128)(2,1)S(1)} %get-tuple-element.28.refs_1_, bf16[96,128]{1,0:T(8,128)(2,1)S(1)} %get-tuple-element.29.refs_2_, bf16[64,16]{1,0:T(8,128)(2,1)S(1)} %get-tuple-element.30.refs_3_, ...), custom_call_target="tpu_custom_call" | custom-call | flops 8388608 | bytes 8388608 | tf_op jit(solution)/shard_map/pallas_call | solution.py:317
  9.3 0.1 collective-permute-start.2
  9.4 1.2 %collective-permute-done.2.other = f32[96,128]{1,0:T(8,128)S(1)} collective-permute-done((f32[96,128]{1,0:T(8,128)S(1)}, f32[96,128]{1,0:T(8,128)S(1)}, u32[]{:S(2)}, u32[]{:S(2)}) %collective-permute-start.2) | collective-permute-done | bytes 49184 | tf_op jit(solution)/shard_map/ppermute | solution.py:277
  10.6 1.3 %collective-permute-start.3 = (f32[64,128]{1,0:T(8,128)S(1)}, f32[64,128]{1,0:T(8,128)S(1)}, u32[]{:S(2)}, u32[]{:S(2)}) collective-permute-start(f32[64,128]{1,0:T(8,128)S(1)} %get-tuple-element.41), channel_id=1, source_target_pairs={{0,1},{1,2},{2,3},{3,4},{4,5},{5,6},{6,7},{7,8},{8,9},{9,10},{10,1... | collective-permute-start | bytes 98312 | tf_op jit(solution)/shard_map/ppermute | solution.py:400
  11.9 1.2 %collective-permute-start.4 = (f32[32,128]{1,0:T(8,128)S(1)}, f32[32,128]{1,0:T(8,128)S(1)}, u32[]{:S(2)}, u32[]{:S(2)}) collective-permute-start(f32[32,128]{1,0:T(8,128)S(1)} %get-tuple-element.42), channel_id=1, source_target_pairs={{0,2},{1,3},{2,4},{3,5},{4,6},{5,7},{6,8},{7,9},{8,10},{9,11},{10,... | collective-permute-start | bytes 49160 | tf_op jit(solution)/shard_map/ppermute | solution.py:401
  13.1 3.4 %collective-permute-done.4.far = f32[32,128]{1,0:T(8,128)S(1)} collective-permute-done((f32[32,128]{1,0:T(8,128)S(1)}, f32[32,128]{1,0:T(8,128)S(1)}, u32[]{:S(2)}, u32[]{:S(2)}) %collective-permute-start.4) | collective-permute-done | bytes 16416 | tf_op jit(solution)/shard_map/ppermute | solution.py:401
  16.6 0.0 collective-permute-done.3.near
  16.6 0.1 collective-permute-start.5
  16.7 1.2 %collective-permute-done.5.refs_12_ = f32[64,128]{1,0:T(8,128)S(1)} collective-permute-done((f32[64,128]{1,0:T(8,128)S(1)}, f32[64,128]{1,0:T(8,128)S(1)}, u32[]{:S(2)}, u32[]{:S(2)}) %collective-permute-start.5) | collective-permute-done | bytes 32800 | tf_op jit(solution)/shard_map/ppermute | solution.py:277
  17.9 2.3 %shard_map.141 = (f32[16,128]{1,0:T(8,128)}, f32[96,128]{1,0:T(8,128)S(1)}, f32[16,128]{1,0:T(8,128)}, f32[32,128]{1,0:T(8,128)S(1)}) custom-call(bf16[32,256,256]{2,1,0:T(8,128)(2,1)S(1)} %get-tuple-element.27.refs_0_, bf16[64,96]{1,0:T(8,128)(2,1)S(1)} %get-tuple-element.28.refs_1_, bf16[96,128]{1,0:T(8,128)(2,1)S(1)} %get-tuple-element.29.refs_2_, ...), custom_call_target="tpu_custom_call" | custom-call | flops 8388608 | bytes 8388608 | tf_op jit(solution)/shard_map/pallas_call | solution.py:317
  20.2 0.2 collective-permute-start.6
  20.4 1.1 %collective-permute-done.6.other = f32[96,128]{1,0:T(8,128)S(1)} collective-permute-done((f32[96,128]{1,0:T(8,128)S(1)}, f32[96,128]{1,0:T(8,128)S(1)}, u32[]{:S(2)}, u32[]{:S(2)}) %collective-permute-start.6) | collective-permute-done | bytes 49184 | tf_op jit(solution)/shard_map/ppermute | solution.py:277
  21.5 1.7 %collective-permute-start.8 = (f32[32,128]{1,0:T(8,128)S(1)}, f32[32,128]{1,0:T(8,128)S(1)}, u32[]{:S(2)}, u32[]{:S(2)}) collective-permute-start(f32[32,128]{1,0:T(8,128)S(1)} %get-tuple-element.47), channel_id=1, source_target_pairs={{0,1},{1,0},{2,3},{3,2},{4,5},{5,4},{6,7},{7,6},{8,9},{9,8},{10,11... | collective-permute-start | bytes 49160 | tf_op jit(solution)/shard_map/ppermute | solution.py:310
  23.2 0.4 %collective-permute-start.7 = (f32[32,128]{1,0:T(8,128)S(1)}, f32[32,128]{1,0:T(8,128)S(1)}, u32[]{:S(2)}, u32[]{:S(2)}) collective-permute-start(f32[32,128]{1,0:T(8,128)S(1)} %get-tuple-element.46), channel_id=1, source_target_pairs={{0,16},{1,2},{2,1},{3,4},{4,3},{5,6},{6,5},{7,8},{8,7},{9,10},{10,... | collective-permute-start | bytes 49160 | tf_op jit(solution)/shard_map/ppermute | solution.py:309
  23.6 1.7 %collective-permute-done.8 = f32[32,128]{1,0:T(8,128)S(1)} collective-permute-done((f32[32,128]{1,0:T(8,128)S(1)}, f32[32,128]{1,0:T(8,128)S(1)}, u32[]{:S(2)}, u32[]{:S(2)}) %collective-permute-start.8) | collective-permute-done | bytes 16416 | tf_op jit(solution)/shard_map/ppermute | solution.py:310
  25.3 3.4 %collective-permute-done.7 = f32[32,128]{1,0:T(8,128)S(1)} collective-permute-done((f32[32,128]{1,0:T(8,128)S(1)}, f32[32,128]{1,0:T(8,128)S(1)}, u32[]{:S(2)}, u32[]{:S(2)}) %collective-permute-start.7) | collective-permute-done | bytes 16416 | tf_op jit(solution)/shard_map/ppermute | solution.py:309
  28.7 0.6 %add_multiply_fusion = (f32[32,128]{1,0:T(8,128)}, f32[32,128]{1,0:T(8,128)}) fusion(f32[32,128]{1,0:T(8,128)S(1)} %get-tuple-element.49, f32[32,128]{1,0:T(8,128)S(1)} %get-tuple-element.45, f32[32,128]{1,0:T(8,128)S(1)} %collective-permute-done.8, f32[32,128]{1,0:T(8,128)S(1)} %collective-permute-done.7, pred[]{:T(512)S(6)} %lt.3, pred[]{:T(512)S(6)} %eq.3, ...), kind=kLoop, calls=%fused_computation | loop fusion | flops 36864 | bytes 98307 | tf_op jit(solution)/shard_map/div | solution.py:419
  (3 shorter events, 0.0 us)
Async XLA Ops:
  0.6 6.2 %collective-permute-start = (f32[32,128]{1,0:T(8,128)}, f32[32,128]{1,0:T(8,128)S(1)}, u32[]{:S(2)}, u32[]{:S(2)}) collective-permute-start(f32[32,128]{1,0:T(8,128)} %dual.1), channel_id=1, source_target_pairs={{0,16},{1,2},{2,1},{3,4},{4,3},{5,6},{6,5},{7,8},{8,7},{9,10},{10,... | collective-permute-start | bytes 49160 | tf_op jit(solution)/shard_map/ppermute | solution.py:309
  3.0 3.9 %collective-permute-start.1 = (f32[32,128]{1,0:T(8,128)}, f32[32,128]{1,0:T(8,128)S(1)}, u32[]{:S(2)}, u32[]{:S(2)}) collective-permute-start(f32[32,128]{1,0:T(8,128)} %dual.1), channel_id=1, source_target_pairs={{0,1},{1,0},{2,3},{3,2},{4,5},{5,4},{6,7},{7,6},{8,9},{9,8},{10,11... | collective-permute-start | bytes 49160 | tf_op jit(solution)/shard_map/ppermute | solution.py:310
  9.3 1.3 %collective-permute-start.2 = (f32[96,128]{1,0:T(8,128)S(1)}, f32[96,128]{1,0:T(8,128)S(1)}, u32[]{:S(2)}, u32[]{:S(2)}) collective-permute-start(f32[96,128]{1,0:T(8,128)S(1)} %get-tuple-element.39.window), channel_id=1, source_target_pairs={{0,16},{1,17},{2,18},{3,19},{4,20},{5,21},{6,22},{7,23},{8,24},{9,... | collective-permute-start | bytes 147464 | tf_op jit(solution)/shard_map/ppermute | solution.py:277
  10.6 6.0 %collective-permute-start.3 = (f32[64,128]{1,0:T(8,128)S(1)}, f32[64,128]{1,0:T(8,128)S(1)}, u32[]{:S(2)}, u32[]{:S(2)}) collective-permute-start(f32[64,128]{1,0:T(8,128)S(1)} %get-tuple-element.41), channel_id=1, source_target_pairs={{0,1},{1,2},{2,3},{3,4},{4,5},{5,6},{6,7},{7,8},{8,9},{9,10},{10,1... | collective-permute-start | bytes 98312 | tf_op jit(solution)/shard_map/ppermute | solution.py:400
  11.9 4.6 %collective-permute-start.4 = (f32[32,128]{1,0:T(8,128)S(1)}, f32[32,128]{1,0:T(8,128)S(1)}, u32[]{:S(2)}, u32[]{:S(2)}) collective-permute-start(f32[32,128]{1,0:T(8,128)S(1)} %get-tuple-element.42), channel_id=1, source_target_pairs={{0,2},{1,3},{2,4},{3,5},{4,6},{5,7},{6,8},{7,9},{8,10},{9,11},{10,... | collective-permute-start | bytes 49160 | tf_op jit(solution)/shard_map/ppermute | solution.py:401
  16.6 1.3 %collective-permute-start.5 = (f32[64,128]{1,0:T(8,128)S(1)}, f32[64,128]{1,0:T(8,128)S(1)}, u32[]{:S(2)}, u32[]{:S(2)}) collective-permute-start(f32[64,128]{1,0:T(8,128)S(1)} %shard_map.140.refs_11_), channel_id=1, source_target_pairs={{0,16},{1,17},{2,18},{3,19},{4,20},{5,21},{6,22},{7,23},{8,24},{9,... | collective-permute-start | bytes 98312 | tf_op jit(solution)/shard_map/ppermute | solution.py:277
  20.2 1.3 %collective-permute-start.6 = (f32[96,128]{1,0:T(8,128)S(1)}, f32[96,128]{1,0:T(8,128)S(1)}, u32[]{:S(2)}, u32[]{:S(2)}) collective-permute-start(f32[96,128]{1,0:T(8,128)S(1)} %get-tuple-element.44.window), channel_id=1, source_target_pairs={{0,16},{1,17},{2,18},{3,19},{4,20},{5,21},{6,22},{7,23},{8,24},{9,... | collective-permute-start | bytes 147464 | tf_op jit(solution)/shard_map/ppermute | solution.py:277
  21.5 3.8 %collective-permute-start.8 = (f32[32,128]{1,0:T(8,128)S(1)}, f32[32,128]{1,0:T(8,128)S(1)}, u32[]{:S(2)}, u32[]{:S(2)}) collective-permute-start(f32[32,128]{1,0:T(8,128)S(1)} %get-tuple-element.47), channel_id=1, source_target_pairs={{0,1},{1,0},{2,3},{3,2},{4,5},{5,4},{6,7},{7,6},{8,9},{9,8},{10,11... | collective-permute-start | bytes 49160 | tf_op jit(solution)/shard_map/ppermute | solution.py:310
  23.2 5.5 %collective-permute-start.7 = (f32[32,128]{1,0:T(8,128)S(1)}, f32[32,128]{1,0:T(8,128)S(1)}, u32[]{:S(2)}, u32[]{:S(2)}) collective-permute-start(f32[32,128]{1,0:T(8,128)S(1)} %get-tuple-element.46), channel_id=1, source_target_pairs={{0,16},{1,2},{2,1},{3,4},{4,3},{5,6},{6,5},{7,8},{8,7},{9,10},{10,... | collective-permute-start | bytes 49160 | tf_op jit(solution)/shard_map/ppermute | solution.py:309

commit v4 on v3

--- a/solution.py
+++ b/solution.py
@@ -14,6 +14,10 @@
 dual_step = 0.6
 f32 = jnp.float32
 bf16 = jnp.bfloat16
+
+
+def shares(total):
+    return total // 32 * 8, total * 3 // 64 * 8
 
 
 def split(value):
@@ -35,6 +39,8 @@
     dual,
     rhs,
     packed,
+    plain,
+    turned,
     row_pick,
     row_sum,
     col_pick,
@@ -54,7 +60,8 @@
     sems,
 ):
     total, size = tiles.shape[0], tiles.shape[1]
-    step = total // chunks
+    kept = held.shape[0]
+    step = kept // chunks
     small = []
     for source, target in (
         (rows, rows_in),
@@ -70,6 +77,10 @@
         copy = pltpu.make_async_copy(source, target, sems.at[chunks + len(small)])
         copy.start()
         small.append(copy)
+    direct = pltpu.make_async_copy(
+        tiles.at[pl.ds(kept, total - kept)], plain, sems.at[chunks + len(small)]
+    )
+    direct.start()
     copies = []
     for k in range(chunks):
         part = pl.ds(k * step, step)
@@ -96,53 +107,55 @@
         pick[...] = jnp.transpose(jnp.where(hit, 1.0, 0.0).astype(f32)).astype(bf16)
     low = jnp.zeros(classes.shape, f32)
     high = jnp.zeros(classes.shape, f32)
-    for k in range(lower_table.shape[0]):
-        low = jnp.where(classes_in[...] == k, lower_in[k], low)
-        high = jnp.where(classes_in[...] == k, upper_in[k], high)
+    for k in range(lower_table.shape[1]):
+        low = jnp.where(classes_in[...] == k, jnp.broadcast_to(lower_in[:, k : k + 1], low.shape), low)
+        high = jnp.where(classes_in[...] == k, jnp.broadcast_to(upper_in[:, k : k + 1], low.shape), high)
     lower[...] = low
     upper[...] = high
+    direct.wait()
+    for n in range(kept, total):
+        turned[n - kept] = jnp.transpose(plain[n - kept])
+        tile_high, tile_low = split(plain[n - kept])
+        packed[n, pl.ds(0, size)] = tile_high
+        packed[n, pl.ds(size, size)] = tile_low
     for k in range(chunks):
         copies[k].wait()
         for n in range(k * step, (k + 1) * step):
             tile_high, tile_low = split(held[n])
-            lanes = pl.ds(n % 2 * size, size)
-            packed[n // 2, pl.ds(0, size), lanes] = tile_high
-            packed[n // 2, pl.ds(size, size), lanes] = tile_low
-
-
-def products(packed, picked_high, picked_low, transposed):
-    total, size = picked_high.shape
+            packed[n, pl.ds(0, size)] = tile_high
+            packed[n, pl.ds(size, size)] = tile_low
+
+
+def packed_group(packed, high, low, q, transposed):
+    size = high.shape[1]
     row = lax.broadcasted_iota(jnp.int32, (8, size), 0)
     even = row % 2 == 0
-    both = jnp.concatenate([even, even], axis=0)
-    outs = []
-    for q in range(total // 8):
-        part = slice(8 * q, 8 * q + 8)
-        left = jnp.concatenate([picked_high[part], picked_low[part]], axis=0)
+    part = slice(8 * q, 8 * q + 8)
+    left = jnp.concatenate([high[part], low[part]], axis=0)
+    if transposed:
+        both = jnp.concatenate([even, even], axis=0)
+        zero = jnp.zeros_like(left)
+        left = jnp.concatenate(
+            [jnp.where(both, left, zero), jnp.where(both, zero, left)], axis=1
+        )
+    else:
+        left = jnp.concatenate([left, left], axis=1)
+    left = left.astype(bf16)
+    result = jnp.zeros((8, size), f32)
+    for j in range(4):
+        out = lax.dot_general(
+            left,
+            jnp.concatenate([packed[8 * q + 2 * j + k] for k in range(2)], axis=1),
+            (((1,), (1 if transposed else 0,)), ((), ())),
+            preferred_element_type=f32,
+        )
+        out = out[:8] + out[8:]
         if transposed:
-            zero = jnp.zeros_like(left)
-            left = jnp.concatenate(
-                [jnp.where(both, left, zero), jnp.where(both, zero, left)], axis=1
-            )
+            term = out[:, :size] + out[:, size:]
         else:
-            left = jnp.concatenate([left, left], axis=1)
-        left = left.astype(bf16)
-        result = jnp.zeros((8, size), f32)
-        for j in range(4):
-            out = lax.dot_general(
-                left,
-                packed[4 * q + j],
-                (((1,), (1 if transposed else 0,)), ((), ())),
-                preferred_element_type=f32,
-            )
-            out = out[:8] + out[8:]
-            if transposed:
-                term = out[:, :size] + out[:, size:]
-            else:
-                term = jnp.where(even, out[:, :size], out[:, size:])
-            result = jnp.where(row // 2 == j, term, result)
-        outs.append(result)
-    return jnp.concatenate(outs, axis=0)
+            term = jnp.where(even, out[:, :size], out[:, size:])
+        result = jnp.where(row // 2 == j, term, result)
+    return result
 
 
 def pick(selector, values):
@@ -152,20 +165,49 @@
     return out[:, :size], out[:, size:]
 
 
-def summed(selector, values):
-    both = jnp.concatenate(split(values), axis=0)
-    return jnp.dot(selector[...], both, preferred_element_type=f32)
-
-
-def iterate(state, view, primal, base):
-    packed, row_pick, row_sum, col_pick, col_sum, lower, upper, cost = state
+def interleaved(packed, extra, high, low, transposed, one):
+    groups = (packed.shape[0] - extra) // 8
+    results = []
+    done = 0
+    for q in range(groups):
+        results.append(packed_group(packed, high, low, q, transposed))
+        while done * groups < extra * (q + 1):
+            one(done)
+            done += 1
+    return jnp.concatenate(results, axis=0)
+
+
+def apply(packed, plain, picker, summer, values, rows, transposed, extra):
+    size = plain.shape[1]
+    skipped = plain.shape[0] - extra
+    high, low = pick(picker, values)
+    first = high.shape[0] - extra
+    lane = lax.broadcasted_iota(jnp.int32, (size, size), 1)
+    turned = [jnp.zeros((size, size), f32)]
+
+    def one(n):
+        terms = plain[skipped + n] * jnp.broadcast_to(rows[pl.ds(n, 1)], (size, size))
+        turned[0] = jnp.where(lane == n, jnp.sum(terms, axis=1, keepdims=True), turned[0])
+
+    if extra:
+        rows[pl.ds(0, extra)] = high[first:] + low[first:]
+    main = interleaved(packed, extra, high, low, transposed, one)
+    if extra:
+        main = jnp.concatenate([main, jnp.transpose(turned[0])[:extra]], axis=0)
+    both = jnp.concatenate(split(main), axis=0)
+    return jnp.dot(summer[...], both, preferred_element_type=f32)
+
+
+def iterate(state, view, primal, base, scratch):
+    packed, plain, turned, row_pick, row_sum, col_pick, col_sum, lower, upper, cost = state
     blocks = base.shape[0]
-    high, low = pick(row_pick, view)
-    adjoint = summed(col_sum, products(packed, high, low, False))
+    extra = shares(row_pick.shape[0])
+    adjoint = apply(packed, turned, row_pick, col_sum, view, scratch[0], False, extra[0])
     moved = primal[...] - primal_step * (cost[...] - adjoint)
     primal_next = jnp.minimum(jnp.maximum(moved, lower[...]), upper[...])
-    high, low = pick(col_pick, 2.0 * primal_next - primal[...])
-    window = summed(row_sum, products(packed, high, low, True)) * (-dual_step)
+    ahead = 2.0 * primal_next - primal[...]
+    window = apply(packed, plain, col_pick, row_sum, ahead, scratch[0], True, extra[1])
+    window = window * (-dual_step)
     first = (lax.axis_index("grp") == 0).astype(f32)
     own = window[blocks : 2 * blocks] + base * first
     window = jnp.concatenate([window[:blocks], own, window[2 * blocks :]], axis=0)
@@ -177,17 +219,18 @@
 
 
 def first_kernel(*refs):
-    state, (primal, dual, rhs, forth, reverse), (primal_out, window_out) = (
-        refs[:8],
-        refs[8:13],
-        refs[13:],
+    state, (primal, dual, rhs, forth, reverse), (primal_out, window_out), scratch = (
+        refs[:10],
+        refs[10:15],
+        refs[15:17],
+        refs[17:],
     )
     even = lax.rem(lax.axis_index("tm"), 2) == 0
     above = jnp.where(even, forth[...], reverse[...])
     below = jnp.where(even, reverse[...], forth[...])
     view = jnp.concatenate([above, dual[...], below], axis=0)
     primal_out[...], window_out[...] = iterate(
-        state, view, primal, dual[...] + dual_step * rhs[...]
+        state, view, primal, dual[...] + dual_step * rhs[...], scratch
     )
 
 
@@ -215,11 +258,13 @@
 
 
 def later_kernel(*refs):
-    state, (primal, rhs, total, sent, got), (primal_out, window_out, mean_out, dual_out) = (
-        refs[:8],
-        refs[8:13],
-        refs[13:],
-    )
+    state, (primal, rhs, total, sent, got), outs, scratch = (
+        refs[:10],
+        refs[10:15],
+        refs[15:19],
+        refs[19:],
+    )
+    primal_out, window_out, mean_out, dual_out = outs
     blocks = rhs.shape[0]
     rising = rises()
     side, part = (sent[pl.ds(k * blocks, blocks)] for k in range(2))
@@ -228,7 +273,7 @@
     above = jnp.where(rising, side, other)
     below = jnp.where(rising, other, side)
     view = jnp.concatenate([above, dual, below], axis=0)
-    primal_next, window = iterate(state, view, primal, dual + dual_step * rhs[...])
+    primal_next, window = iterate(state, view, primal, dual + dual_step * rhs[...], scratch)
     primal_out[...] = primal_next
     window_out[...] = window
     mean_out[...] = (primal[...] + primal_next) / ITERS
@@ -313,12 +358,13 @@
     def shape(count, kind=f32, width=size):
         return jax.ShapeDtypeStruct((count, width), kind)
 
-    def kernel(code, outs, args, limit=1 << 20, passes=0):
+    def kernel(code, outs, args, limit=1 << 20, passes=0, scratch=()):
         return pl.pallas_call(
             code,
             out_shape=tuple(outs),
             in_specs=vmem(len(args)),
             out_specs=tuple(vmem(len(outs))),
+            scratch_shapes=scratch,
             compiler_params=pltpu.CompilerParams(vmem_limit_bytes=limit),
             cost_estimate=pl.CostEstimate(
                 flops=4 * passes * total * size * size,
@@ -327,15 +373,17 @@
             ),
         )(*args)
 
-    chunks = 8
+    extra = max(shares(total))
+    kept = total - extra
+    chunks = kept // 8
     inputs = (
         tiles,
         tile_rows[None, :],
         tile_cols[None, :],
         tile_count,
         var_class,
-        lower_table,
-        upper_table,
+        lower_table[None, :],
+        upper_table[None, :],
         x_start,
         cost,
         y_start,
@@ -343,7 +391,9 @@
     )
     forth, reverse = exchange(y_start, y_start)
     outs = (
-        jax.ShapeDtypeStruct((total // 2, 2 * size, 2 * size), bf16),
+        jax.ShapeDtypeStruct((total, 2 * size, size), bf16),
+        jax.ShapeDtypeStruct((extra, size, size), f32),
+        jax.ShapeDtypeStruct((extra, size, size), f32),
         shape(total, bf16, 3 * rows),
         shape(3 * rows, bf16, 2 * total),
         shape(total, bf16, cols),
@@ -364,13 +414,13 @@
         ],
         out_specs=tuple(vmem(len(outs))),
         scratch_shapes=[
-            pltpu.VMEM(tiles.shape, f32),
+            pltpu.VMEM((kept, size, size), f32),
             pltpu.VMEM((1, total), jnp.int32),
             pltpu.VMEM((1, total), jnp.int32),
             pltpu.VMEM(var_class.shape, jnp.int32),
-            pltpu.SMEM(lower_table.shape, f32),
-            pltpu.SMEM(upper_table.shape, f32),
-            pltpu.SemaphoreType.DMA((chunks + 9,)),
+            pltpu.VMEM((1, lower_table.shape[0]), f32),
+            pltpu.VMEM((1, upper_table.shape[0]), f32),
+            pltpu.SemaphoreType.DMA((chunks + 10,)),
         ],
         compiler_params=pltpu.CompilerParams(vmem_limit_bytes=16 << 20),
         cost_estimate=pl.CostEstimate(
@@ -386,6 +436,7 @@
         )
     )
     state = (*selectors, lower, upper, cost)
+    scratch = [pltpu.VMEM((extra, size), f32)]
 
     primal_1, window = kernel(
         first_kernel,
@@ -393,6 +444,7 @@
         (*state, primal, dual, rhs, forth, reverse),
         limit=16 << 20,
         passes=2,
+        scratch=scratch,
     )
     window, near, far = kernel(
         fold_kernel, (shape(3 * rows), shape(2 * rows), shape(rows)), group_sum(window)
@@ -407,6 +459,7 @@
         (*state, primal_1, rhs, window, sent, got),
         limit=16 << 20,
         passes=2,
+        scratch=scratch,
     )
     own, forth, reverse = kernel(
         last_fold_kernel, (shape(rows),) * 3, group_sum(window)

time: 29.5 us -> 28.6 us (0.969)
  Pallas kernels: 7.15 us -> 6.38 us
    pallas_call x5, Pallas kernels: 4.65 us -> 3.89 us  [kernel(): pl.pallas_call(code, out_shape=tuple(outs), in_specs=vmem(len(args)), out...]
where the time goes in v4:
time: 28.6 us; the launch traced here: 28.5 us
  waiting for transfers between devices  12.2 us (43%)
  starting transfers between devices  7.97 us (28%)
  Pallas kernels  6.38 us (22%)
  between operations  1.35 us (5%)
  other arithmetic  0.62 us (2%)
    pallas_call x5, Pallas kernels, kernel(): pl.pallas_call(code, out_shape=tuple(outs), in_specs=vmem(len(args)), out...  3.89 us
    ppermute x3, waiting for transfers between devices, swap(): return lax.ppermute(value, AXES, route)  3.48 us
    ppermute x1, waiting for transfers between devices, body(): far = lax.ppermute(far, AXES, ring(2))  3.41 us
    ppermute x2, waiting for transfers between devices, exchange(): odd = lax.ppermute(odd, AXES, pairs(1))  3.41 us
    ppermute x2, starting transfers between devices, exchange(): odd = lax.ppermute(odd, AXES, pairs(1))  2.81 us
    pallas_call x1, Pallas kernels, body(): pl.pallas_call(functools.partial(prep_kernel, chunks), out_shape=outs, in...  2.5 us
    ppermute x2, starting transfers between devices, exchange(): even = lax.ppermute(even, AXES, pairs(0))  2.32 us
    ppermute x2, waiting for transfers between devices, exchange(): even = lax.ppermute(even, AXES, pairs(0))  1.85 us
  transfers between devices with their start and end apart: 9, of which 7 were waited for; matrix products, arithmetic and copies ran while one was open for 0% of the time, Pallas kernels for 9%

profile of v4, /device:TPU:16, one launch (start us, length us, event | category | flops | bytes accessed | tf_op | source)
XLA Modules:
  0.0 28.5 jit_solution(10494102535077850744)
XLA Ops:
  0.6 2.4 %collective-permute-start = (f32[32,128]{1,0:T(8,128)}, f32[32,128]{1,0:T(8,128)S(1)}, u32[]{:S(2)}, u32[]{:S(2)}) collective-permute-start(f32[32,128]{1,0:T(8,128)} %dual.1), channel_id=1, source_target_pairs={{0,16},{1,2},{2,1},{3,4},{4,3},{5,6},{6,5},{7,8},{8,7},{9,10},{10,... | collective-permute-start | bytes 49160 | tf_op jit(solution)/shard_map/ppermute | solution.py:354
  3.0 0.6 %collective-permute-start.1 = (f32[32,128]{1,0:T(8,128)}, f32[32,128]{1,0:T(8,128)S(1)}, u32[]{:S(2)}, u32[]{:S(2)}) collective-permute-start(f32[32,128]{1,0:T(8,128)} %dual.1), channel_id=1, source_target_pairs={{0,1},{1,0},{2,3},{3,2},{4,5},{5,4},{6,7},{7,6},{8,9},{9,8},{10,11... | collective-permute-start | bytes 49160 | tf_op jit(solution)/shard_map/ppermute | solution.py:355
  4.3 2.5 %prep.1 = (bf16[64,256,128]{2,1,0:T(8,128)(2,1)S(1)}, f32[24,128,128]{2,1,0:T(8,128)S(1)}, f32[24,128,128]{2,1,0:T(8,128)S(1)}, bf16[64,96]{1,0:T(8,128)(2,1)S(1...) custom-call(f32[64,128,128]{2,1,0:T(8,128)} %tiles.1, ...), custom_call_target="tpu_custom_call" | custom-call | flops 4194304 | bytes 8388608 | tf_op jit(solution)/shard_map/prep/pallas_call | solution.py:408
  6.8 0.0 collective-permute-done.refs_13_
  6.8 0.1 collective-permute-done.1.refs_14_
  7.0 1.8 %shard_map.138 = (f32[16,128]{1,0:T(8,128)S(1)}, f32[96,128]{1,0:T(8,128)S(1)}) custom-call(bf16[64,256,128]{2,1,0:T(8,128)(2,1)S(1)} %get-tuple-element.29.refs_0_, f32[24,128,128]{2,1,0:T(8,128)S(1)} %get-tuple-element.30.refs_1_, f32[24,128,128]{2,1,0:T(8,128)S(1)} %get-tuple-element.31.refs_2_, bf16[64,96]{1,0:T(8,128)(2,1)S(1)} %get-tuple-element.32.refs_3_, ...), custom_call_target="tpu_custom_call" | custom-call | flops 8388608 | bytes 8388608 | tf_op jit(solution)/shard_map/pallas_call | solution.py:362
  8.8 0.1 collective-permute-start.2
  8.9 1.2 %collective-permute-done.2.other = f32[96,128]{1,0:T(8,128)S(1)} collective-permute-done((f32[96,128]{1,0:T(8,128)S(1)}, f32[96,128]{1,0:T(8,128)S(1)}, u32[]{:S(2)}, u32[]{:S(2)}) %collective-permute-start.2) | collective-permute-done | bytes 49184 | tf_op jit(solution)/shard_map/ppermute | solution.py:322
  10.1 1.3 %collective-permute-start.3 = (f32[64,128]{1,0:T(8,128)S(1)}, f32[64,128]{1,0:T(8,128)S(1)}, u32[]{:S(2)}, u32[]{:S(2)}) collective-permute-start(f32[64,128]{1,0:T(8,128)S(1)} %get-tuple-element.45), channel_id=1, source_target_pairs={{0,1},{1,2},{2,3},{3,4},{4,5},{5,6},{6,7},{7,8},{8,9},{9,10},{10,1... | collective-permute-start | bytes 98312 | tf_op jit(solution)/shard_map/ppermute | solution.py:452
  11.4 1.2 %collective-permute-start.4 = (f32[32,128]{1,0:T(8,128)S(1)}, f32[32,128]{1,0:T(8,128)S(1)}, u32[]{:S(2)}, u32[]{:S(2)}) collective-permute-start(f32[32,128]{1,0:T(8,128)S(1)} %get-tuple-element.46), channel_id=1, source_target_pairs={{0,2},{1,3},{2,4},{3,5},{4,6},{5,7},{6,8},{7,9},{8,10},{9,11},{10,... | collective-permute-start | bytes 49160 | tf_op jit(solution)/shard_map/ppermute | solution.py:453
  12.7 3.4 %collective-permute-done.4.far = f32[32,128]{1,0:T(8,128)S(1)} collective-permute-done((f32[32,128]{1,0:T(8,128)S(1)}, f32[32,128]{1,0:T(8,128)S(1)}, u32[]{:S(2)}, u32[]{:S(2)}) %collective-permute-start.4) | collective-permute-done | bytes 16416 | tf_op jit(solution)/shard_map/ppermute | solution.py:453
  16.1 0.0 collective-permute-done.3.near
  16.1 0.1 collective-permute-start.5
  16.2 1.2 %collective-permute-done.5.refs_14_ = f32[64,128]{1,0:T(8,128)S(1)} collective-permute-done((f32[64,128]{1,0:T(8,128)S(1)}, f32[64,128]{1,0:T(8,128)S(1)}, u32[]{:S(2)}, u32[]{:S(2)}) %collective-permute-start.5) | collective-permute-done | bytes 32800 | tf_op jit(solution)/shard_map/ppermute | solution.py:322
  17.4 2.0 %shard_map.141 = (f32[16,128]{1,0:T(8,128)}, f32[96,128]{1,0:T(8,128)S(1)}, f32[16,128]{1,0:T(8,128)}, f32[32,128]{1,0:T(8,128)S(1)}) custom-call(bf16[64,256,128]{2,1,0:T(8,128)(2,1)S(1)} %get-tuple-element.29.refs_0_, f32[24,128,128]{2,1,0:T(8,128)S(1)} %get-tuple-element.30.refs_1_, f32[24,128,128]{2,1,0:T(8,128)S(1)} %get-tuple-element.31.refs_2_, ...), custom_call_target="tpu_custom_call" | custom-call | flops 8388608 | bytes 8388608 | tf_op jit(solution)/shard_map/pallas_call | solution.py:362
  19.4 0.2 collective-permute-start.6
  19.6 1.1 %collective-permute-done.6.other = f32[96,128]{1,0:T(8,128)S(1)} collective-permute-done((f32[96,128]{1,0:T(8,128)S(1)}, f32[96,128]{1,0:T(8,128)S(1)}, u32[]{:S(2)}, u32[]{:S(2)}) %collective-permute-start.6) | collective-permute-done | bytes 49184 | tf_op jit(solution)/shard_map/ppermute | solution.py:322
  20.6 1.7 %collective-permute-start.8 = (f32[32,128]{1,0:T(8,128)S(1)}, f32[32,128]{1,0:T(8,128)S(1)}, u32[]{:S(2)}, u32[]{:S(2)}) collective-permute-start(f32[32,128]{1,0:T(8,128)S(1)} %get-tuple-element.51), channel_id=1, source_target_pairs={{0,1},{1,0},{2,3},{3,2},{4,5},{5,4},{6,7},{7,6},{8,9},{9,8},{10,11... | collective-permute-start | bytes 49160 | tf_op jit(solution)/shard_map/ppermute | solution.py:355
  22.3 0.4 %collective-permute-start.7 = (f32[32,128]{1,0:T(8,128)S(1)}, f32[32,128]{1,0:T(8,128)S(1)}, u32[]{:S(2)}, u32[]{:S(2)}) collective-permute-start(f32[32,128]{1,0:T(8,128)S(1)} %get-tuple-element.50), channel_id=1, source_target_pairs={{0,16},{1,2},{2,1},{3,4},{4,3},{5,6},{6,5},{7,8},{8,7},{9,10},{10,... | collective-permute-start | bytes 49160 | tf_op jit(solution)/shard_map/ppermute | solution.py:354
  22.7 1.7 %collective-permute-done.8 = f32[32,128]{1,0:T(8,128)S(1)} collective-permute-done((f32[32,128]{1,0:T(8,128)S(1)}, f32[32,128]{1,0:T(8,128)S(1)}, u32[]{:S(2)}, u32[]{:S(2)}) %collective-permute-start.8) | collective-permute-done | bytes 16416 | tf_op jit(solution)/shard_map/ppermute | solution.py:355
  24.5 3.4 %collective-permute-done.7 = f32[32,128]{1,0:T(8,128)S(1)} collective-permute-done((f32[32,128]{1,0:T(8,128)S(1)}, f32[32,128]{1,0:T(8,128)S(1)}, u32[]{:S(2)}, u32[]{:S(2)}) %collective-permute-start.7) | collective-permute-done | bytes 16416 | tf_op jit(solution)/shard_map/ppermute | solution.py:354
  27.9 0.6 %add_multiply_fusion = (f32[32,128]{1,0:T(8,128)}, f32[32,128]{1,0:T(8,128)}) fusion(f32[32,128]{1,0:T(8,128)S(1)} %get-tuple-element.53, f32[32,128]{1,0:T(8,128)S(1)} %get-tuple-element.49, f32[32,128]{1,0:T(8,128)S(1)} %collective-permute-done.8, f32[32,128]{1,0:T(8,128)S(1)} %collective-permute-done.7, pred[]{:T(512)S(6)} %lt.3, pred[]{:T(512)S(6)} %eq.3, ...), kind=kLoop, calls=%fused_computation | loop fusion | flops 36864 | bytes 98307 | tf_op jit(solution)/shard_map/div | solution.py:472
  (3 shorter events, 0.0 us)
Async XLA Ops:
  0.6 6.2 %collective-permute-start = (f32[32,128]{1,0:T(8,128)}, f32[32,128]{1,0:T(8,128)S(1)}, u32[]{:S(2)}, u32[]{:S(2)}) collective-permute-start(f32[32,128]{1,0:T(8,128)} %dual.1), channel_id=1, source_target_pairs={{0,16},{1,2},{2,1},{3,4},{4,3},{5,6},{6,5},{7,8},{8,7},{9,10},{10,... | collective-permute-start | bytes 49160 | tf_op jit(solution)/shard_map/ppermute | solution.py:354
  3.0 3.9 %collective-permute-start.1 = (f32[32,128]{1,0:T(8,128)}, f32[32,128]{1,0:T(8,128)S(1)}, u32[]{:S(2)}, u32[]{:S(2)}) collective-permute-start(f32[32,128]{1,0:T(8,128)} %dual.1), channel_id=1, source_target_pairs={{0,1},{1,0},{2,3},{3,2},{4,5},{5,4},{6,7},{7,6},{8,9},{9,8},{10,11... | collective-permute-start | bytes 49160 | tf_op jit(solution)/shard_map/ppermute | solution.py:355
  8.8 1.3 %collective-permute-start.2 = (f32[96,128]{1,0:T(8,128)S(1)}, f32[96,128]{1,0:T(8,128)S(1)}, u32[]{:S(2)}, u32[]{:S(2)}) collective-permute-start(f32[96,128]{1,0:T(8,128)S(1)} %get-tuple-element.43.window), channel_id=1, source_target_pairs={{0,16},{1,17},{2,18},{3,19},{4,20},{5,21},{6,22},{7,23},{8,24},{9,... | collective-permute-start | bytes 147464 | tf_op jit(solution)/shard_map/ppermute | solution.py:322
  10.1 6.0 %collective-permute-start.3 = (f32[64,128]{1,0:T(8,128)S(1)}, f32[64,128]{1,0:T(8,128)S(1)}, u32[]{:S(2)}, u32[]{:S(2)}) collective-permute-start(f32[64,128]{1,0:T(8,128)S(1)} %get-tuple-element.45), channel_id=1, source_target_pairs={{0,1},{1,2},{2,3},{3,4},{4,5},{5,6},{6,7},{7,8},{8,9},{9,10},{10,1... | collective-permute-start | bytes 98312 | tf_op jit(solution)/shard_map/ppermute | solution.py:452
  11.4 4.6 %collective-permute-start.4 = (f32[32,128]{1,0:T(8,128)S(1)}, f32[32,128]{1,0:T(8,128)S(1)}, u32[]{:S(2)}, u32[]{:S(2)}) collective-permute-start(f32[32,128]{1,0:T(8,128)S(1)} %get-tuple-element.46), channel_id=1, source_target_pairs={{0,2},{1,3},{2,4},{3,5},{4,6},{5,7},{6,8},{7,9},{8,10},{9,11},{10,... | collective-permute-start | bytes 49160 | tf_op jit(solution)/shard_map/ppermute | solution.py:453
  16.1 1.3 %collective-permute-start.5 = (f32[64,128]{1,0:T(8,128)S(1)}, f32[64,128]{1,0:T(8,128)S(1)}, u32[]{:S(2)}, u32[]{:S(2)}) collective-permute-start(f32[64,128]{1,0:T(8,128)S(1)} %shard_map.140.refs_13_), channel_id=1, source_target_pairs={{0,16},{1,17},{2,18},{3,19},{4,20},{5,21},{6,22},{7,23},{8,24},{9,... | collective-permute-start | bytes 98312 | tf_op jit(solution)/shard_map/ppermute | solution.py:322
  19.4 1.2 %collective-permute-start.6 = (f32[96,128]{1,0:T(8,128)S(1)}, f32[96,128]{1,0:T(8,128)S(1)}, u32[]{:S(2)}, u32[]{:S(2)}) collective-permute-start(f32[96,128]{1,0:T(8,128)S(1)} %get-tuple-element.48.window), channel_id=1, source_target_pairs={{0,16},{1,17},{2,18},{3,19},{4,20},{5,21},{6,22},{7,23},{8,24},{9,... | collective-permute-start | bytes 147464 | tf_op jit(solution)/shard_map/ppermute | solution.py:322
  20.6 3.8 %collective-permute-start.8 = (f32[32,128]{1,0:T(8,128)S(1)}, f32[32,128]{1,0:T(8,128)S(1)}, u32[]{:S(2)}, u32[]{:S(2)}) collective-permute-start(f32[32,128]{1,0:T(8,128)S(1)} %get-tuple-element.51), channel_id=1, source_target_pairs={{0,1},{1,0},{2,3},{3,2},{4,5},{5,4},{6,7},{7,6},{8,9},{9,8},{10,11... | collective-permute-start | bytes 49160 | tf_op jit(solution)/shard_map/ppermute | solution.py:355
  22.3 5.5 %collective-permute-start.7 = (f32[32,128]{1,0:T(8,128)S(1)}, f32[32,128]{1,0:T(8,128)S(1)}, u32[]{:S(2)}, u32[]{:S(2)}) collective-permute-start(f32[32,128]{1,0:T(8,128)S(1)} %get-tuple-element.50), channel_id=1, source_target_pairs={{0,16},{1,2},{2,1},{3,4},{4,3},{5,6},{6,5},{7,8},{8,7},{9,10},{10,... | collective-permute-start | bytes 49160 | tf_op jit(solution)/shard_map/ppermute | solution.py:354

commit v5 on v4

--- a/solution.py
+++ b/solution.py
@@ -261,10 +261,10 @@
     state, (primal, rhs, total, sent, got), outs, scratch = (
         refs[:10],
         refs[10:15],
-        refs[15:19],
-        refs[19:],
-    )
-    primal_out, window_out, mean_out, dual_out = outs
+        refs[15:18],
+        refs[18:],
+    )
+    primal_out, window_out, dual_out = outs
     blocks = rhs.shape[0]
     rising = rises()
     side, part = (sent[pl.ds(k * blocks, blocks)] for k in range(2))
@@ -276,7 +276,6 @@
     primal_next, window = iterate(state, view, primal, dual + dual_step * rhs[...], scratch)
     primal_out[...] = primal_next
     window_out[...] = window
-    mean_out[...] = (primal[...] + primal_next) / ITERS
     dual_out[...] = dual
 
 
@@ -287,6 +286,11 @@
     even = lax.rem(lax.axis_index("tm"), 2) == 0
     forth_out[...] = jnp.where(even, total[:blocks], total[2 * blocks :])
     reverse_out[...] = jnp.where(even, total[2 * blocks :], total[:blocks])
+
+
+def emit_kernel(before, after, primal_out, mean_out):
+    primal_out[...] = after[...]
+    mean_out[...] = (before[...] + after[...]) / ITERS
 
 
 def vmem(count):
@@ -453,9 +457,9 @@
     far = lax.ppermute(far, AXES, ring(2))
     (sent,) = kernel(side_kernel, (shape(2 * rows),), (window, near, far))
     got = swap(sent, 1)
-    primal_2, window, primal_mean, dual_1 = kernel(
+    primal_2, window, dual_1 = kernel(
         later_kernel,
-        (shape(cols), shape(3 * rows), shape(cols), shape(rows)),
+        (shape(cols), shape(3 * rows), shape(rows)),
         (*state, primal_1, rhs, window, sent, got),
         limit=16 << 20,
         passes=2,
@@ -465,6 +469,9 @@
         last_fold_kernel, (shape(rows),) * 3, group_sum(window)
     )
     forth, reverse = exchange(forth, reverse)
+    primal_2, primal_mean = kernel(
+        emit_kernel, (shape(cols), shape(cols)), (primal_1, primal_2)
+    )
     even = lax.rem(tm, 2) == 0
     above = jnp.where(tm >= 1, jnp.where(even, forth, reverse), 0.0)
     below = jnp.where(tm + 1 < times, jnp.where(even, reverse, forth), 0.0)

time: 28.6 us -> 28.5 us (level)
  waiting for transfers between devices: 12.2 us -> 11.6 us
  Pallas kernels: 6.38 us -> 6.78 us
    ppermute x2, waiting for transfers between devices: 1.85 us -> 1.25 us  [exchange(): even = lax.ppermute(even, AXES, pairs(0))]
    pallas_call x5 -> x6, Pallas kernels: 3.89 us -> 4.28 us  [kernel(): pl.pallas_call(code, out_shape=tuple(outs), in_specs=vmem(len(args)), out...]
  transfers between devices with their start and end apart: 9 -> 9, of which waited for: 7 -> 7; matrix products, arithmetic and copies ran while one was open for 0% -> 0% of each run, Pallas kernels for 9% -> 11%
where the time goes in v5:
time: 28.5 us; the launch traced here: 28.3 us
  waiting for transfers between devices  11.6 us (41%)
  starting transfers between devices  8.03 us (28%)
  Pallas kernels  6.78 us (24%)
  between operations  1.36 us (5%)
  other arithmetic  0.62 us (2%)
    pallas_call x6, Pallas kernels, kernel(): pl.pallas_call(code, out_shape=tuple(outs), in_specs=vmem(len(args)), out...  4.28 us
    ppermute x3, waiting for transfers between devices, swap(): return lax.ppermute(value, AXES, route)  3.48 us
    ppermute x1, waiting for transfers between devices, body(): far = lax.ppermute(far, AXES, ring(2))  3.41 us
    ppermute x2, waiting for transfers between devices, exchange(): odd = lax.ppermute(odd, AXES, pairs(1))  3.41 us
    ppermute x2, starting transfers between devices, exchange(): odd = lax.ppermute(odd, AXES, pairs(1))  2.81 us
    pallas_call x1, Pallas kernels, body(): pl.pallas_call(functools.partial(prep_kernel, chunks), out_shape=outs, in...  2.5 us
    ppermute x2, starting transfers between devices, exchange(): even = lax.ppermute(even, AXES, pairs(0))  2.32 us
    ppermute x1, starting transfers between devices, body(): near = lax.ppermute(near, AXES, ring(1))  1.31 us
  transfers between devices with their start and end apart: 9, of which 7 were waited for; matrix products, arithmetic and copies ran while one was open for 0% of the time, Pallas kernels for 11%

profile of v5, /device:TPU:16, one launch (start us, length us, event | category | flops | bytes accessed | tf_op | source)
XLA Modules:
  0.0 28.3 jit_solution(4555855502900070665)
XLA Ops:
  0.6 2.4 %collective-permute-start = (f32[32,128]{1,0:T(8,128)}, f32[32,128]{1,0:T(8,128)S(1)}, u32[]{:S(2)}, u32[]{:S(2)}) collective-permute-start(f32[32,128]{1,0:T(8,128)} %dual.1), channel_id=1, source_target_pairs={{0,16},{1,2},{2,1},{3,4},{4,3},{5,6},{6,5},{7,8},{8,7},{9,10},{10,... | collective-permute-start | bytes 49160 | tf_op jit(solution)/shard_map/ppermute | solution.py:358
  3.0 0.6 %collective-permute-start.1 = (f32[32,128]{1,0:T(8,128)}, f32[32,128]{1,0:T(8,128)S(1)}, u32[]{:S(2)}, u32[]{:S(2)}) collective-permute-start(f32[32,128]{1,0:T(8,128)} %dual.1), channel_id=1, source_target_pairs={{0,1},{1,0},{2,3},{3,2},{4,5},{5,4},{6,7},{7,6},{8,9},{9,8},{10,11... | collective-permute-start | bytes 49160 | tf_op jit(solution)/shard_map/ppermute | solution.py:359
  4.3 2.5 %prep.1 = (bf16[64,256,128]{2,1,0:T(8,128)(2,1)S(1)}, f32[24,128,128]{2,1,0:T(8,128)S(1)}, f32[24,128,128]{2,1,0:T(8,128)S(1)}, bf16[64,96]{1,0:T(8,128)(2,1)S(1...) custom-call(f32[64,128,128]{2,1,0:T(8,128)} %tiles.1, ...), custom_call_target="tpu_custom_call" | custom-call | flops 4194304 | bytes 8388608 | tf_op jit(solution)/shard_map/prep/pallas_call | solution.py:412
  6.8 0.0 collective-permute-done.refs_13_
  6.8 0.1 collective-permute-done.1.refs_14_
  7.0 1.8 %shard_map.138 = (f32[16,128]{1,0:T(8,128)S(1)}, f32[96,128]{1,0:T(8,128)S(1)}) custom-call(bf16[64,256,128]{2,1,0:T(8,128)(2,1)S(1)} %get-tuple-element.30.refs_0_, f32[24,128,128]{2,1,0:T(8,128)S(1)} %get-tuple-element.31.refs_1_, f32[24,128,128]{2,1,0:T(8,128)S(1)} %get-tuple-element.32.refs_2_, bf16[64,96]{1,0:T(8,128)(2,1)S(1)} %get-tuple-element.33.refs_3_, ...), custom_call_target="tpu_custom_call" | custom-call | flops 8388608 | bytes 8388608 | tf_op jit(solution)/shard_map/pallas_call | solution.py:366
  8.8 0.1 collective-permute-start.2
  8.9 1.2 %collective-permute-done.2.other = f32[96,128]{1,0:T(8,128)S(1)} collective-permute-done((f32[96,128]{1,0:T(8,128)S(1)}, f32[96,128]{1,0:T(8,128)S(1)}, u32[]{:S(2)}, u32[]{:S(2)}) %collective-permute-start.2) | collective-permute-done | bytes 49184 | tf_op jit(solution)/shard_map/ppermute | solution.py:326
  10.1 1.3 %collective-permute-start.3 = (f32[64,128]{1,0:T(8,128)S(1)}, f32[64,128]{1,0:T(8,128)S(1)}, u32[]{:S(2)}, u32[]{:S(2)}) collective-permute-start(f32[64,128]{1,0:T(8,128)S(1)} %get-tuple-element.46), channel_id=1, source_target_pairs={{0,1},{1,2},{2,3},{3,4},{4,5},{5,6},{6,7},{7,8},{8,9},{9,10},{10,1... | collective-permute-start | bytes 98312 | tf_op jit(solution)/shard_map/ppermute | solution.py:456
  11.4 1.2 %collective-permute-start.4 = (f32[32,128]{1,0:T(8,128)S(1)}, f32[32,128]{1,0:T(8,128)S(1)}, u32[]{:S(2)}, u32[]{:S(2)}) collective-permute-start(f32[32,128]{1,0:T(8,128)S(1)} %get-tuple-element.47), channel_id=1, source_target_pairs={{0,2},{1,3},{2,4},{3,5},{4,6},{5,7},{6,8},{7,9},{8,10},{9,11},{10,... | collective-permute-start | bytes 49160 | tf_op jit(solution)/shard_map/ppermute | solution.py:457
  12.7 3.4 %collective-permute-done.4.far = f32[32,128]{1,0:T(8,128)S(1)} collective-permute-done((f32[32,128]{1,0:T(8,128)S(1)}, f32[32,128]{1,0:T(8,128)S(1)}, u32[]{:S(2)}, u32[]{:S(2)}) %collective-permute-start.4) | collective-permute-done | bytes 16416 | tf_op jit(solution)/shard_map/ppermute | solution.py:457
  16.1 0.0 collective-permute-done.3.near
  16.1 0.1 collective-permute-start.5
  16.2 1.2 %collective-permute-done.5.refs_14_ = f32[64,128]{1,0:T(8,128)S(1)} collective-permute-done((f32[64,128]{1,0:T(8,128)S(1)}, f32[64,128]{1,0:T(8,128)S(1)}, u32[]{:S(2)}, u32[]{:S(2)}) %collective-permute-start.5) | collective-permute-done | bytes 32800 | tf_op jit(solution)/shard_map/ppermute | solution.py:326
  17.4 1.8 %shard_map.141 = (f32[16,128]{1,0:T(8,128)S(1)}, f32[96,128]{1,0:T(8,128)S(1)}, f32[32,128]{1,0:T(8,128)S(1)}) custom-call(bf16[64,256,128]{2,1,0:T(8,128)(2,1)S(1)} %get-tuple-element.30.refs_0_, f32[24,128,128]{2,1,0:T(8,128)S(1)} %get-tuple-element.31.refs_1_, f32[24,128,128]{2,1,0:T(8,128)S(1)} %get-tuple-element.32.refs_2_, ...), custom_call_target="tpu_custom_call" | custom-call | flops 8388608 | bytes 8388608 | tf_op jit(solution)/shard_map/pallas_call | solution.py:366
  19.2 0.2 collective-permute-start.6
  19.4 1.1 %collective-permute-done.6.other = f32[96,128]{1,0:T(8,128)S(1)} collective-permute-done((f32[96,128]{1,0:T(8,128)S(1)}, f32[96,128]{1,0:T(8,128)S(1)}, u32[]{:S(2)}, u32[]{:S(2)}) %collective-permute-start.6) | collective-permute-done | bytes 49184 | tf_op jit(solution)/shard_map/ppermute | solution.py:326
  20.5 1.7 %collective-permute-start.8 = (f32[32,128]{1,0:T(8,128)S(1)}, f32[32,128]{1,0:T(8,128)S(1)}, u32[]{:S(2)}, u32[]{:S(2)}) collective-permute-start(f32[32,128]{1,0:T(8,128)S(1)} %get-tuple-element.53), channel_id=1, source_target_pairs={{0,1},{1,0},{2,3},{3,2},{4,5},{5,4},{6,7},{7,6},{8,9},{9,8},{10,11... | collective-permute-start | bytes 49160 | tf_op jit(solution)/shard_map/ppermute | solution.py:359
  22.2 0.4 %collective-permute-start.7 = (f32[32,128]{1,0:T(8,128)S(1)}, f32[32,128]{1,0:T(8,128)S(1)}, u32[]{:S(2)}, u32[]{:S(2)}) collective-permute-start(f32[32,128]{1,0:T(8,128)S(1)} %get-tuple-element.52), channel_id=1, source_target_pairs={{0,16},{1,2},{2,1},{3,4},{4,3},{5,6},{6,5},{7,8},{8,7},{9,10},{10,... | collective-permute-start | bytes 49160 | tf_op jit(solution)/shard_map/ppermute | solution.py:358
  22.6 0.6 %shard_map.142 = (f32[16,128]{1,0:T(8,128)}, f32[16,128]{1,0:T(8,128)}) custom-call(f32[16,128]{1,0:T(8,128)S(1)} %get-tuple-element.43.refs_10_.before, f32[16,128]{1,0:T(8,128)S(1)} %get-tuple-element.48.after), custom_call_target="tpu_custom_call" | custom-call | tf_op jit(solution)/shard_map/pallas_call | solution.py:366
  23.2 1.1 %collective-permute-done.8 = f32[32,128]{1,0:T(8,128)S(1)} collective-permute-done((f32[32,128]{1,0:T(8,128)S(1)}, f32[32,128]{1,0:T(8,128)S(1)}, u32[]{:S(2)}, u32[]{:S(2)}) %collective-permute-start.8) | collective-permute-done | bytes 16416 | tf_op jit(solution)/shard_map/ppermute | solution.py:359
  24.3 3.4 %collective-permute-done.7 = f32[32,128]{1,0:T(8,128)S(1)} collective-permute-done((f32[32,128]{1,0:T(8,128)S(1)}, f32[32,128]{1,0:T(8,128)S(1)}, u32[]{:S(2)}, u32[]{:S(2)}) %collective-permute-start.7) | collective-permute-done | bytes 16416 | tf_op jit(solution)/shard_map/ppermute | solution.py:358
  27.7 0.6 %add_multiply_fusion = (f32[32,128]{1,0:T(8,128)}, f32[32,128]{1,0:T(8,128)}) fusion(f32[32,128]{1,0:T(8,128)S(1)} %get-tuple-element.55, f32[32,128]{1,0:T(8,128)S(1)} %get-tuple-element.51, f32[32,128]{1,0:T(8,128)S(1)} %collective-permute-done.8, f32[32,128]{1,0:T(8,128)S(1)} %collective-permute-done.7, pred[]{:T(512)S(6)} %lt.3, pred[]{:T(512)S(6)} %eq.3, ...), kind=kLoop, calls=%fused_computation | loop fusion | flops 36864 | bytes 98307 | tf_op jit(solution)/shard_map/div | solution.py:479
  (3 shorter events, 0.0 us)
Async XLA Ops:
  0.6 6.2 %collective-permute-start = (f32[32,128]{1,0:T(8,128)}, f32[32,128]{1,0:T(8,128)S(1)}, u32[]{:S(2)}, u32[]{:S(2)}) collective-permute-start(f32[32,128]{1,0:T(8,128)} %dual.1), channel_id=1, source_target_pairs={{0,16},{1,2},{2,1},{3,4},{4,3},{5,6},{6,5},{7,8},{8,7},{9,10},{10,... | collective-permute-start | bytes 49160 | tf_op jit(solution)/shard_map/ppermute | solution.py:358
  3.0 3.9 %collective-permute-start.1 = (f32[32,128]{1,0:T(8,128)}, f32[32,128]{1,0:T(8,128)S(1)}, u32[]{:S(2)}, u32[]{:S(2)}) collective-permute-start(f32[32,128]{1,0:T(8,128)} %dual.1), channel_id=1, source_target_pairs={{0,1},{1,0},{2,3},{3,2},{4,5},{5,4},{6,7},{7,6},{8,9},{9,8},{10,11... | collective-permute-start | bytes 49160 | tf_op jit(solution)/shard_map/ppermute | solution.py:359
  8.8 1.3 %collective-permute-start.2 = (f32[96,128]{1,0:T(8,128)S(1)}, f32[96,128]{1,0:T(8,128)S(1)}, u32[]{:S(2)}, u32[]{:S(2)}) collective-permute-start(f32[96,128]{1,0:T(8,128)S(1)} %get-tuple-element.44.window), channel_id=1, source_target_pairs={{0,16},{1,17},{2,18},{3,19},{4,20},{5,21},{6,22},{7,23},{8,24},{9,... | collective-permute-start | bytes 147464 | tf_op jit(solution)/shard_map/ppermute | solution.py:326
  10.1 6.0 %collective-permute-start.3 = (f32[64,128]{1,0:T(8,128)S(1)}, f32[64,128]{1,0:T(8,128)S(1)}, u32[]{:S(2)}, u32[]{:S(2)}) collective-permute-start(f32[64,128]{1,0:T(8,128)S(1)} %get-tuple-element.46), channel_id=1, source_target_pairs={{0,1},{1,2},{2,3},{3,4},{4,5},{5,6},{6,7},{7,8},{8,9},{9,10},{10,1... | collective-permute-start | bytes 98312 | tf_op jit(solution)/shard_map/ppermute | solution.py:456
  11.4 4.6 %collective-permute-start.4 = (f32[32,128]{1,0:T(8,128)S(1)}, f32[32,128]{1,0:T(8,128)S(1)}, u32[]{:S(2)}, u32[]{:S(2)}) collective-permute-start(f32[32,128]{1,0:T(8,128)S(1)} %get-tuple-element.47), channel_id=1, source_target_pairs={{0,2},{1,3},{2,4},{3,5},{4,6},{5,7},{6,8},{7,9},{8,10},{9,11},{10,... | collective-permute-start | bytes 49160 | tf_op jit(solution)/shard_map/ppermute | solution.py:457
  16.1 1.3 %collective-permute-start.5 = (f32[64,128]{1,0:T(8,128)S(1)}, f32[64,128]{1,0:T(8,128)S(1)}, u32[]{:S(2)}, u32[]{:S(2)}) collective-permute-start(f32[64,128]{1,0:T(8,128)S(1)} %shard_map.140.refs_13_), channel_id=1, source_target_pairs={{0,16},{1,17},{2,18},{3,19},{4,20},{5,21},{6,22},{7,23},{8,24},{9,... | collective-permute-start | bytes 98312 | tf_op jit(solution)/shard_map/ppermute | solution.py:326
  19.2 1.3 %collective-permute-start.6 = (f32[96,128]{1,0:T(8,128)S(1)}, f32[96,128]{1,0:T(8,128)S(1)}, u32[]{:S(2)}, u32[]{:S(2)}) collective-permute-start(f32[96,128]{1,0:T(8,128)S(1)} %get-tuple-element.50.window), channel_id=1, source_target_pairs={{0,16},{1,17},{2,18},{3,19},{4,20},{5,21},{6,22},{7,23},{8,24},{9,... | collective-permute-start | bytes 147464 | tf_op jit(solution)/shard_map/ppermute | solution.py:326
  20.5 3.8 %collective-permute-start.8 = (f32[32,128]{1,0:T(8,128)S(1)}, f32[32,128]{1,0:T(8,128)S(1)}, u32[]{:S(2)}, u32[]{:S(2)}) collective-permute-start(f32[32,128]{1,0:T(8,128)S(1)} %get-tuple-element.53), channel_id=1, source_target_pairs={{0,1},{1,0},{2,3},{3,2},{4,5},{5,4},{6,7},{7,6},{8,9},{9,8},{10,11... | collective-permute-start | bytes 49160 | tf_op jit(solution)/shard_map/ppermute | solution.py:359
  22.2 5.5 %collective-permute-start.7 = (f32[32,128]{1,0:T(8,128)S(1)}, f32[32,128]{1,0:T(8,128)S(1)}, u32[]{:S(2)}, u32[]{:S(2)}) collective-permute-start(f32[32,128]{1,0:T(8,128)S(1)} %get-tuple-element.52), channel_id=1, source_target_pairs={{0,16},{1,2},{2,1},{3,4},{4,3},{5,6},{6,5},{7,8},{8,7},{9,10},{10,... | collective-permute-start | bytes 49160 | tf_op jit(solution)/shard_map/ppermute | solution.py:358

commit v6 on v5

--- a/solution.py
+++ b/solution.py
@@ -165,8 +165,8 @@
     return out[:, :size], out[:, size:]
 
 
-def interleaved(packed, extra, high, low, transposed, one):
-    groups = (packed.shape[0] - extra) // 8
+def interleaved(packed, used, extra, high, low, transposed, one):
+    groups = (used - extra) // 8
     results = []
     done = 0
     for q in range(groups):
@@ -177,7 +177,7 @@
     return jnp.concatenate(results, axis=0)
 
 
-def apply(packed, plain, picker, summer, values, rows, transposed, extra):
+def apply(packed, plain, picker, summer, values, rows, transposed, extra, used):
     size = plain.shape[1]
     skipped = plain.shape[0] - extra
     high, low = pick(picker, values)
@@ -191,22 +191,37 @@
 
     if extra:
         rows[pl.ds(0, extra)] = high[first:] + low[first:]
-    main = interleaved(packed, extra, high, low, transposed, one)
+    main = interleaved(packed, used, extra, high, low, transposed, one)
     if extra:
         main = jnp.concatenate([main, jnp.transpose(turned[0])[:extra]], axis=0)
+    if used < high.shape[0]:
+        blank = jnp.zeros((high.shape[0] - used, size), f32)
+        main = jnp.concatenate([main, blank], axis=0)
     both = jnp.concatenate(split(main), axis=0)
     return jnp.dot(summer[...], both, preferred_element_type=f32)
 
 
-def iterate(state, view, primal, base, scratch):
+def iterate(state, view, primal, base, scratch, emit):
+    *state, count = state
+    total = state[0].shape[0]
+
+    @pl.when(count[0] * 2 > total)
+    def _():
+        emit(*advance(state, view, primal, base, scratch, total, shares(total)))
+
+    @pl.when(count[0] * 2 <= total)
+    def _():
+        emit(*advance(state, view, primal, base, scratch, total // 2, (0, 0)))
+
+
+def advance(state, view, primal, base, scratch, used, extra):
     packed, plain, turned, row_pick, row_sum, col_pick, col_sum, lower, upper, cost = state
     blocks = base.shape[0]
-    extra = shares(row_pick.shape[0])
-    adjoint = apply(packed, turned, row_pick, col_sum, view, scratch[0], False, extra[0])
+    adjoint = apply(packed, turned, row_pick, col_sum, view, scratch[0], False, extra[0], used)
     moved = primal[...] - primal_step * (cost[...] - adjoint)
     primal_next = jnp.minimum(jnp.maximum(moved, lower[...]), upper[...])
     ahead = 2.0 * primal_next - primal[...]
-    window = apply(packed, plain, col_pick, row_sum, ahead, scratch[0], True, extra[1])
+    window = apply(packed, plain, col_pick, row_sum, ahead, scratch[0], True, extra[1], used)
     window = window * (-dual_step)
     first = (lax.axis_index("grp") == 0).astype(f32)
     own = window[blocks : 2 * blocks] + base * first
@@ -220,18 +235,21 @@
 
 def first_kernel(*refs):
     state, (primal, dual, rhs, forth, reverse), (primal_out, window_out), scratch = (
-        refs[:10],
-        refs[10:15],
-        refs[15:17],
-        refs[17:],
+        refs[:11],
+        refs[11:16],
+        refs[16:18],
+        refs[18:],
     )
     even = lax.rem(lax.axis_index("tm"), 2) == 0
     above = jnp.where(even, forth[...], reverse[...])
     below = jnp.where(even, reverse[...], forth[...])
     view = jnp.concatenate([above, dual[...], below], axis=0)
-    primal_out[...], window_out[...] = iterate(
-        state, view, primal, dual[...] + dual_step * rhs[...], scratch
-    )
+
+    def emit(primal_next, window):
+        primal_out[...] = primal_next
+        window_out[...] = window
+
+    iterate(state, view, primal, dual[...] + dual_step * rhs[...], scratch, emit)
 
 
 def fold_kernel(window, other, summed_out, near_out, far_out):
@@ -259,10 +277,10 @@
 
 def later_kernel(*refs):
     state, (primal, rhs, total, sent, got), outs, scratch = (
-        refs[:10],
-        refs[10:15],
-        refs[15:18],
-        refs[18:],
+        refs[:11],
+        refs[11:16],
+        refs[16:19],
+        refs[19:],
     )
     primal_out, window_out, dual_out = outs
     blocks = rhs.shape[0]
@@ -273,10 +291,13 @@
     above = jnp.where(rising, side, other)
     below = jnp.where(rising, other, side)
     view = jnp.concatenate([above, dual, below], axis=0)
-    primal_next, window = iterate(state, view, primal, dual + dual_step * rhs[...], scratch)
-    primal_out[...] = primal_next
-    window_out[...] = window
     dual_out[...] = dual
+
+    def emit(primal_next, window):
+        primal_out[...] = primal_next
+        window_out[...] = window
+
+    iterate(state, view, primal, dual + dual_step * rhs[...], scratch, emit)
 
 
 def last_fold_kernel(window, other, own_out, forth_out, reverse_out):
@@ -366,7 +387,10 @@
         return pl.pallas_call(
             code,
             out_shape=tuple(outs),
-            in_specs=vmem(len(args)),
+            in_specs=[
+                pl.BlockSpec(memory_space=pltpu.SMEM if value is tile_count else pltpu.VMEM)
+                for value in args
+            ],
             out_specs=tuple(vmem(len(outs))),
             scratch_shapes=scratch,
             compiler_params=pltpu.CompilerParams(vmem_limit_bytes=limit),
@@ -439,7 +463,7 @@
             for value in inputs
         )
     )
-    state = (*selectors, lower, upper, cost)
+    state = (*selectors, lower, upper, cost, tile_count)
     scratch = [pltpu.VMEM((extra, size), f32)]
 
     primal_1, window = kernel(
@@ -465,13 +489,9 @@
         passes=2,
         scratch=scratch,
     )
-    own, forth, reverse = kernel(
-        last_fold_kernel, (shape(rows),) * 3, group_sum(window)
-    )
+    own, forth, reverse = kernel(last_fold_kernel, (shape(rows),) * 3, group_sum(window))
     forth, reverse = exchange(forth, reverse)
-    primal_2, primal_mean = kernel(
-        emit_kernel, (shape(cols), shape(cols)), (primal_1, primal_2)
-    )
+    primal_2, primal_mean = kernel(emit_kernel, (shape(cols), shape(cols)), (primal_1, primal_2))
     even = lax.rem(tm, 2) == 0
     above = jnp.where(tm >= 1, jnp.where(even, forth, reverse), 0.0)
     below = jnp.where(tm + 1 < times, jnp.where(even, reverse, forth), 0.0)

time: 28.5 us -> 27.9 us (0.979)
  Pallas kernels: 6.78 us -> 6.13 us
    pallas_call x6, Pallas kernels: 4.28 us -> 3.63 us  [kernel(): pl.pallas_call(code, out_shape=tuple(outs), in_specs=[pl.BlockSpec(memory...]
where the time goes in v6:
time: 27.9 us; the launch traced here: 27.7 us
  waiting for transfers between devices  11.6 us (42%)
  starting transfers between devices  8.04 us (29%)
  Pallas kernels  6.13 us (22%)
  between operations  1.36 us (5%)
  other arithmetic  0.62 us (2%)
    pallas_call x6, Pallas kernels, kernel(): pl.pallas_call(code, out_shape=tuple(outs), in_specs=[pl.BlockSpec(memory...  3.63 us
    ppermute x3, waiting for transfers between devices, swap(): return lax.ppermute(value, AXES, route)  3.48 us
    ppermute x1, waiting for transfers between devices, body(): far = lax.ppermute(far, AXES, ring(2))  3.42 us
    ppermute x2, waiting for transfers between devices, exchange(): odd = lax.ppermute(odd, AXES, pairs(1))  3.41 us
    ppermute x2, starting transfers between devices, exchange(): odd = lax.ppermute(odd, AXES, pairs(1))  2.81 us
    pallas_call x1, Pallas kernels, body(): pl.pallas_call(functools.partial(prep_kernel, chunks), out_shape=outs, in...  2.5 us
    ppermute x2, starting transfers between devices, exchange(): even = lax.ppermute(even, AXES, pairs(0))  2.32 us
    ppermute x1, starting transfers between devices, body(): near = lax.ppermute(near, AXES, ring(1))  1.32 us
  transfers between devices with their start and end apart: 9, of which 7 were waited for; matrix products, arithmetic and copies ran while one was open for 0% of the time, Pallas kernels for 11%

profile of v6, /device:TPU:16, one launch (start us, length us, event | category | flops | bytes accessed | tf_op | source)
XLA Modules:
  0.0 27.7 jit_solution(6528480428813469991)
XLA Ops:
  0.6 2.4 %collective-permute-start = (f32[32,128]{1,0:T(8,128)}, f32[32,128]{1,0:T(8,128)S(1)}, u32[]{:S(2)}, u32[]{:S(2)}) collective-permute-start(f32[32,128]{1,0:T(8,128)} %dual.1), channel_id=1, source_target_pairs={{0,16},{1,2},{2,1},{3,4},{4,3},{5,6},{6,5},{7,8},{8,7},{9,10},{10,... | collective-permute-start | bytes 49160 | tf_op jit(solution)/shard_map/ppermute | solution.py:379
  3.0 0.6 %collective-permute-start.1 = (f32[32,128]{1,0:T(8,128)}, f32[32,128]{1,0:T(8,128)S(1)}, u32[]{:S(2)}, u32[]{:S(2)}) collective-permute-start(f32[32,128]{1,0:T(8,128)} %dual.1), channel_id=1, source_target_pairs={{0,1},{1,0},{2,3},{3,2},{4,5},{5,4},{6,7},{7,6},{8,9},{9,8},{10,11... | collective-permute-start | bytes 49160 | tf_op jit(solution)/shard_map/ppermute | solution.py:380
  4.3 2.5 %prep.1 = (bf16[64,256,128]{2,1,0:T(8,128)(2,1)S(1)}, f32[24,128,128]{2,1,0:T(8,128)S(1)}, f32[24,128,128]{2,1,0:T(8,128)S(1)}, bf16[64,96]{1,0:T(8,128)(2,1)S(1...) custom-call(f32[64,128,128]{2,1,0:T(8,128)} %tiles.1, ...), custom_call_target="tpu_custom_call" | custom-call | flops 4194304 | bytes 8388608 | tf_op jit(solution)/shard_map/prep/pallas_call | solution.py:436
  6.8 0.0 collective-permute-done.refs_14_
  6.8 0.1 collective-permute-done.1.refs_15_
  7.0 1.5 %shard_map.138 = (f32[16,128]{1,0:T(8,128)S(1)}, f32[96,128]{1,0:T(8,128)S(1)}) custom-call(bf16[64,256,128]{2,1,0:T(8,128)(2,1)S(1)} %get-tuple-element.30.refs_0_, f32[24,128,128]{2,1,0:T(8,128)S(1)} %get-tuple-element.31.refs_1_, f32[24,128,128]{2,1,0:T(8,128)S(1)} %get-tuple-element.32.refs_2_, bf16[64,96]{1,0:T(8,128)(2,1)S(1)} %get-tuple-element.33.refs_3_, ...), custom_call_target="tpu_custom_call" | custom-call | flops 8388608 | bytes 8388608 | tf_op jit(solution)/shard_map/pallas_call | solution.py:387
  8.5 0.1 collective-permute-start.2
  8.6 1.2 %collective-permute-done.2.other = f32[96,128]{1,0:T(8,128)S(1)} collective-permute-done((f32[96,128]{1,0:T(8,128)S(1)}, f32[96,128]{1,0:T(8,128)S(1)}, u32[]{:S(2)}, u32[]{:S(2)}) %collective-permute-start.2) | collective-permute-done | bytes 49184 | tf_op jit(solution)/shard_map/ppermute | solution.py:347
  9.8 1.3 %collective-permute-start.3 = (f32[64,128]{1,0:T(8,128)S(1)}, f32[64,128]{1,0:T(8,128)S(1)}, u32[]{:S(2)}, u32[]{:S(2)}) collective-permute-start(f32[64,128]{1,0:T(8,128)S(1)} %get-tuple-element.46), channel_id=1, source_target_pairs={{0,1},{1,2},{2,3},{3,4},{4,5},{5,6},{6,7},{7,8},{8,9},{9,10},{10,1... | collective-permute-start | bytes 98312 | tf_op jit(solution)/shard_map/ppermute | solution.py:480
  11.1 1.2 %collective-permute-start.4 = (f32[32,128]{1,0:T(8,128)S(1)}, f32[32,128]{1,0:T(8,128)S(1)}, u32[]{:S(2)}, u32[]{:S(2)}) collective-permute-start(f32[32,128]{1,0:T(8,128)S(1)} %get-tuple-element.47), channel_id=1, source_target_pairs={{0,2},{1,3},{2,4},{3,5},{4,6},{5,7},{6,8},{7,9},{8,10},{9,11},{10,... | collective-permute-start | bytes 49160 | tf_op jit(solution)/shard_map/ppermute | solution.py:481
  12.3 3.4 %collective-permute-done.4.far = f32[32,128]{1,0:T(8,128)S(1)} collective-permute-done((f32[32,128]{1,0:T(8,128)S(1)}, f32[32,128]{1,0:T(8,128)S(1)}, u32[]{:S(2)}, u32[]{:S(2)}) %collective-permute-start.4) | collective-permute-done | bytes 16416 | tf_op jit(solution)/shard_map/ppermute | solution.py:481
  15.8 0.0 collective-permute-done.3.near
  15.8 0.1 collective-permute-start.5
  15.9 1.2 %collective-permute-done.5.refs_15_ = f32[64,128]{1,0:T(8,128)S(1)} collective-permute-done((f32[64,128]{1,0:T(8,128)S(1)}, f32[64,128]{1,0:T(8,128)S(1)}, u32[]{:S(2)}, u32[]{:S(2)}) %collective-permute-start.5) | collective-permute-done | bytes 32800 | tf_op jit(solution)/shard_map/ppermute | solution.py:347
  17.1 1.5 %shard_map.141 = (f32[16,128]{1,0:T(8,128)S(1)}, f32[96,128]{1,0:T(8,128)S(1)}, f32[32,128]{1,0:T(8,128)S(1)}) custom-call(bf16[64,256,128]{2,1,0:T(8,128)(2,1)S(1)} %get-tuple-element.30.refs_0_, f32[24,128,128]{2,1,0:T(8,128)S(1)} %get-tuple-element.31.refs_1_, f32[24,128,128]{2,1,0:T(8,128)S(1)} %get-tuple-element.32.refs_2_, ...), custom_call_target="tpu_custom_call" | custom-call | flops 8388608 | bytes 8388608 | tf_op jit(solution)/shard_map/pallas_call | solution.py:387
  18.6 0.2 collective-permute-start.6
  18.8 1.1 %collective-permute-done.6.other = f32[96,128]{1,0:T(8,128)S(1)} collective-permute-done((f32[96,128]{1,0:T(8,128)S(1)}, f32[96,128]{1,0:T(8,128)S(1)}, u32[]{:S(2)}, u32[]{:S(2)}) %collective-permute-start.6) | collective-permute-done | bytes 49184 | tf_op jit(solution)/shard_map/ppermute | solution.py:347
  19.9 1.7 %collective-permute-start.8 = (f32[32,128]{1,0:T(8,128)S(1)}, f32[32,128]{1,0:T(8,128)S(1)}, u32[]{:S(2)}, u32[]{:S(2)}) collective-permute-start(f32[32,128]{1,0:T(8,128)S(1)} %get-tuple-element.53), channel_id=1, source_target_pairs={{0,1},{1,0},{2,3},{3,2},{4,5},{5,4},{6,7},{7,6},{8,9},{9,8},{10,11... | collective-permute-start | bytes 49160 | tf_op jit(solution)/shard_map/ppermute | solution.py:380
  21.5 0.4 %collective-permute-start.7 = (f32[32,128]{1,0:T(8,128)S(1)}, f32[32,128]{1,0:T(8,128)S(1)}, u32[]{:S(2)}, u32[]{:S(2)}) collective-permute-start(f32[32,128]{1,0:T(8,128)S(1)} %get-tuple-element.52), channel_id=1, source_target_pairs={{0,16},{1,2},{2,1},{3,4},{4,3},{5,6},{6,5},{7,8},{8,7},{9,10},{10,... | collective-permute-start | bytes 49160 | tf_op jit(solution)/shard_map/ppermute | solution.py:379
  22.0 0.6 %shard_map.142 = (f32[16,128]{1,0:T(8,128)}, f32[16,128]{1,0:T(8,128)}) custom-call(f32[16,128]{1,0:T(8,128)S(1)} %get-tuple-element.43.refs_11_.before, f32[16,128]{1,0:T(8,128)S(1)} %get-tuple-element.48.after), custom_call_target="tpu_custom_call" | custom-call | tf_op jit(solution)/shard_map/pallas_call | solution.py:387
  22.6 1.1 %collective-permute-done.8 = f32[32,128]{1,0:T(8,128)S(1)} collective-permute-done((f32[32,128]{1,0:T(8,128)S(1)}, f32[32,128]{1,0:T(8,128)S(1)}, u32[]{:S(2)}, u32[]{:S(2)}) %collective-permute-start.8) | collective-permute-done | bytes 16416 | tf_op jit(solution)/shard_map/ppermute | solution.py:380
  23.7 3.4 %collective-permute-done.7 = f32[32,128]{1,0:T(8,128)S(1)} collective-permute-done((f32[32,128]{1,0:T(8,128)S(1)}, f32[32,128]{1,0:T(8,128)S(1)}, u32[]{:S(2)}, u32[]{:S(2)}) %collective-permute-start.7) | collective-permute-done | bytes 16416 | tf_op jit(solution)/shard_map/ppermute | solution.py:379
  27.1 0.6 %add_multiply_fusion = (f32[32,128]{1,0:T(8,128)}, f32[32,128]{1,0:T(8,128)}) fusion(f32[32,128]{1,0:T(8,128)S(1)} %get-tuple-element.55, f32[32,128]{1,0:T(8,128)S(1)} %get-tuple-element.51, f32[32,128]{1,0:T(8,128)S(1)} %collective-permute-done.8, f32[32,128]{1,0:T(8,128)S(1)} %collective-permute-done.7, pred[]{:T(512)S(6)} %lt.3, pred[]{:T(512)S(6)} %eq.3, ...), kind=kLoop, calls=%fused_computation | loop fusion | flops 36864 | bytes 98307 | tf_op jit(solution)/shard_map/div | solution.py:499
  (3 shorter events, 0.0 us)
Async XLA Ops:
  0.6 6.2 %collective-permute-start = (f32[32,128]{1,0:T(8,128)}, f32[32,128]{1,0:T(8,128)S(1)}, u32[]{:S(2)}, u32[]{:S(2)}) collective-permute-start(f32[32,128]{1,0:T(8,128)} %dual.1), channel_id=1, source_target_pairs={{0,16},{1,2},{2,1},{3,4},{4,3},{5,6},{6,5},{7,8},{8,7},{9,10},{10,... | collective-permute-start | bytes 49160 | tf_op jit(solution)/shard_map/ppermute | solution.py:379
  3.0 3.9 %collective-permute-start.1 = (f32[32,128]{1,0:T(8,128)}, f32[32,128]{1,0:T(8,128)S(1)}, u32[]{:S(2)}, u32[]{:S(2)}) collective-permute-start(f32[32,128]{1,0:T(8,128)} %dual.1), channel_id=1, source_target_pairs={{0,1},{1,0},{2,3},{3,2},{4,5},{5,4},{6,7},{7,6},{8,9},{9,8},{10,11... | collective-permute-start | bytes 49160 | tf_op jit(solution)/shard_map/ppermute | solution.py:380
  8.5 1.3 %collective-permute-start.2 = (f32[96,128]{1,0:T(8,128)S(1)}, f32[96,128]{1,0:T(8,128)S(1)}, u32[]{:S(2)}, u32[]{:S(2)}) collective-permute-start(f32[96,128]{1,0:T(8,128)S(1)} %get-tuple-element.44.window), channel_id=1, source_target_pairs={{0,16},{1,17},{2,18},{3,19},{4,20},{5,21},{6,22},{7,23},{8,24},{9,... | collective-permute-start | bytes 147464 | tf_op jit(solution)/shard_map/ppermute | solution.py:347
  9.8 6.0 %collective-permute-start.3 = (f32[64,128]{1,0:T(8,128)S(1)}, f32[64,128]{1,0:T(8,128)S(1)}, u32[]{:S(2)}, u32[]{:S(2)}) collective-permute-start(f32[64,128]{1,0:T(8,128)S(1)} %get-tuple-element.46), channel_id=1, source_target_pairs={{0,1},{1,2},{2,3},{3,4},{4,5},{5,6},{6,7},{7,8},{8,9},{9,10},{10,1... | collective-permute-start | bytes 98312 | tf_op jit(solution)/shard_map/ppermute | solution.py:480
  11.1 4.6 %collective-permute-start.4 = (f32[32,128]{1,0:T(8,128)S(1)}, f32[32,128]{1,0:T(8,128)S(1)}, u32[]{:S(2)}, u32[]{:S(2)}) collective-permute-start(f32[32,128]{1,0:T(8,128)S(1)} %get-tuple-element.47), channel_id=1, source_target_pairs={{0,2},{1,3},{2,4},{3,5},{4,6},{5,7},{6,8},{7,9},{8,10},{9,11},{10,... | collective-permute-start | bytes 49160 | tf_op jit(solution)/shard_map/ppermute | solution.py:481
  15.8 1.3 %collective-permute-start.5 = (f32[64,128]{1,0:T(8,128)S(1)}, f32[64,128]{1,0:T(8,128)S(1)}, u32[]{:S(2)}, u32[]{:S(2)}) collective-permute-start(f32[64,128]{1,0:T(8,128)S(1)} %shard_map.140.refs_14_), channel_id=1, source_target_pairs={{0,16},{1,17},{2,18},{3,19},{4,20},{5,21},{6,22},{7,23},{8,24},{9,... | collective-permute-start | bytes 98312 | tf_op jit(solution)/shard_map/ppermute | solution.py:347
  18.6 1.3 %collective-permute-start.6 = (f32[96,128]{1,0:T(8,128)S(1)}, f32[96,128]{1,0:T(8,128)S(1)}, u32[]{:S(2)}, u32[]{:S(2)}) collective-permute-start(f32[96,128]{1,0:T(8,128)S(1)} %get-tuple-element.50.window), channel_id=1, source_target_pairs={{0,16},{1,17},{2,18},{3,19},{4,20},{5,21},{6,22},{7,23},{8,24},{9,... | collective-permute-start | bytes 147464 | tf_op jit(solution)/shard_map/ppermute | solution.py:347
  19.9 3.8 %collective-permute-start.8 = (f32[32,128]{1,0:T(8,128)S(1)}, f32[32,128]{1,0:T(8,128)S(1)}, u32[]{:S(2)}, u32[]{:S(2)}) collective-permute-start(f32[32,128]{1,0:T(8,128)S(1)} %get-tuple-element.53), channel_id=1, source_target_pairs={{0,1},{1,0},{2,3},{3,2},{4,5},{5,4},{6,7},{7,6},{8,9},{9,8},{10,11... | collective-permute-start | bytes 49160 | tf_op jit(solution)/shard_map/ppermute | solution.py:380
  21.5 5.5 %collective-permute-start.7 = (f32[32,128]{1,0:T(8,128)S(1)}, f32[32,128]{1,0:T(8,128)S(1)}, u32[]{:S(2)}, u32[]{:S(2)}) collective-permute-start(f32[32,128]{1,0:T(8,128)S(1)} %get-tuple-element.52), channel_id=1, source_target_pairs={{0,16},{1,2},{2,1},{3,4},{4,3},{5,6},{6,5},{7,8},{8,7},{9,10},{10,... | collective-permute-start | bytes 49160 | tf_op jit(solution)/shard_map/ppermute | solution.py:379

commit v7 on v6

--- a/solution.py
+++ b/solution.py
@@ -80,12 +80,16 @@
     direct = pltpu.make_async_copy(
         tiles.at[pl.ds(kept, total - kept)], plain, sems.at[chunks + len(small)]
     )
-    direct.start()
+    more = count[0] * 2 > total
+    pl.when(more)(direct.start)
     copies = []
     for k in range(chunks):
         part = pl.ds(k * step, step)
         copy = pltpu.make_async_copy(tiles.at[part], held.at[part], sems.at[k])
-        copy.start()
+        if 2 * k * step < total:
+            copy.start()
+        else:
+            pl.when(more)(copy.start)
         copies.append(copy)
     for copy in small:
         copy.wait()
@@ -112,18 +116,30 @@
         high = jnp.where(classes_in[...] == k, jnp.broadcast_to(upper_in[:, k : k + 1], low.shape), high)
     lower[...] = low
     upper[...] = high
-    direct.wait()
-    for n in range(kept, total):
-        turned[n - kept] = jnp.transpose(plain[n - kept])
-        tile_high, tile_low = split(plain[n - kept])
+
+    def store(n, tile):
+        tile_high, tile_low = split(tile)
         packed[n, pl.ds(0, size)] = tile_high
         packed[n, pl.ds(size, size)] = tile_low
-    for k in range(chunks):
+
+    def finish(k):
         copies[k].wait()
         for n in range(k * step, (k + 1) * step):
-            tile_high, tile_low = split(held[n])
-            packed[n, pl.ds(0, size)] = tile_high
-            packed[n, pl.ds(size, size)] = tile_low
+            store(n, held[n])
+
+    for k in range(chunks):
+        if 2 * k * step < total:
+            finish(k)
+
+    @pl.when(more)
+    def _():
+        direct.wait()
+        for n in range(kept, total):
+            turned[n - kept] = jnp.transpose(plain[n - kept])
+            store(n, plain[n - kept])
+        for k in range(chunks):
+            if 2 * k * step >= total:
+                finish(k)
 
 
 def packed_group(packed, high, low, q, transposed):
@@ -489,9 +505,13 @@
         passes=2,
         scratch=scratch,
     )
-    own, forth, reverse = kernel(last_fold_kernel, (shape(rows),) * 3, group_sum(window))
+    own, forth, reverse = kernel(
+        last_fold_kernel, (shape(rows),) * 3, group_sum(window)
+    )
     forth, reverse = exchange(forth, reverse)
-    primal_2, primal_mean = kernel(emit_kernel, (shape(cols), shape(cols)), (primal_1, primal_2))
+    primal_2, primal_mean = kernel(
+        emit_kernel, (shape(cols), shape(cols)), (primal_1, primal_2)
+    )
     even = lax.rem(tm, 2) == 0
     above = jnp.where(tm >= 1, jnp.where(even, forth, reverse), 0.0)
     below = jnp.where(tm + 1 < times, jnp.where(even, reverse, forth), 0.0)

time: 27.9 us -> 27.8 us (level)
  the two profiles are of different devices: /device:TPU:16 before, /device:TPU:24 now
where the time goes in v7:
time: 27.8 us; the launch traced here: 27.6 us
  waiting for transfers between devices  12.4 us (45%)
  Pallas kernels  7.23 us (26%)
  starting transfers between devices  6.04 us (22%)
  between operations  1.37 us (5%)
  other arithmetic  0.62 us (2%)
    ppermute x1, waiting for transfers between devices, body(): far = lax.ppermute(far, AXES, ring(2))  4.63 us
    pallas_call x6, Pallas kernels, kernel(): pl.pallas_call(code, out_shape=tuple(outs), in_specs=[pl.BlockSpec(memory...  4.33 us
    ppermute x3, waiting for transfers between devices, swap(): return lax.ppermute(value, AXES, route)  3.63 us
    ppermute x2, starting transfers between devices, exchange(): odd = lax.ppermute(odd, AXES, pairs(1))  3.25 us
    pallas_call x1, Pallas kernels, body(): pl.pallas_call(functools.partial(prep_kernel, chunks), out_shape=outs, in...  2.91 us
    ppermute x2, waiting for transfers between devices, exchange(): odd = lax.ppermute(odd, AXES, pairs(1))  2.24 us
    ppermute x2, waiting for transfers between devices, exchange(): even = lax.ppermute(even, AXES, pairs(0))  1.85 us
    ppermute x1, starting transfers between devices, body(): near = lax.ppermute(near, AXES, ring(1))  1.43 us
  transfers between devices with their start and end apart: 9, of which 6 were waited for; matrix products, arithmetic and copies ran while one was open for 0% of the time, Pallas kernels for 13%

profile of v7, /device:TPU:24, one launch (start us, length us, event | category | flops | bytes accessed | tf_op | source)
XLA Modules:
  0.0 27.6 jit_solution(4585886320035389461)
XLA Ops:
  0.6 2.4 %collective-permute-start = (f32[32,128]{1,0:T(8,128)}, f32[32,128]{1,0:T(8,128)S(1)}, u32[]{:S(2)}, u32[]{:S(2)}) collective-permute-start(f32[32,128]{1,0:T(8,128)} %dual.1), channel_id=1, source_target_pairs={{0,16},{1,2},{2,1},{3,4},{4,3},{5,6},{6,5},{7,8},{8,7},{9,10},{10,... | collective-permute-start | bytes 49160 | tf_op jit(solution)/shard_map/ppermute | solution.py:395
  3.0 0.6 %collective-permute-start.1 = (f32[32,128]{1,0:T(8,128)}, f32[32,128]{1,0:T(8,128)S(1)}, u32[]{:S(2)}, u32[]{:S(2)}) collective-permute-start(f32[32,128]{1,0:T(8,128)} %dual.1), channel_id=1, source_target_pairs={{0,1},{1,0},{2,3},{3,2},{4,5},{5,4},{6,7},{7,6},{8,9},{9,8},{10,11... | collective-permute-start | bytes 49160 | tf_op jit(solution)/shard_map/ppermute | solution.py:396
  4.3 2.9 %prep.1 = (bf16[64,256,128]{2,1,0:T(8,128)(2,1)S(1)}, f32[24,128,128]{2,1,0:T(8,128)S(1)}, f32[24,128,128]{2,1,0:T(8,128)S(1)}, bf16[64,96]{1,0:T(8,128)(2,1)S(1...) custom-call(f32[64,128,128]{2,1,0:T(8,128)} %tiles.1, ...), custom_call_target="tpu_custom_call" | custom-call | flops 4194304 | bytes 8388608 | tf_op jit(solution)/shard_map/prep/pallas_call | solution.py:452
  7.3 0.0 collective-permute-done.refs_14_
  7.3 0.0 collective-permute-done.1.refs_15_
  7.3 1.8 %shard_map.138 = (f32[16,128]{1,0:T(8,128)S(1)}, f32[96,128]{1,0:T(8,128)S(1)}) custom-call(bf16[64,256,128]{2,1,0:T(8,128)(2,1)S(1)} %get-tuple-element.30.refs_0_, f32[24,128,128]{2,1,0:T(8,128)S(1)} %get-tuple-element.31.refs_1_, f32[24,128,128]{2,1,0:T(8,128)S(1)} %get-tuple-element.32.refs_2_, bf16[64,96]{1,0:T(8,128)(2,1)S(1)} %get-tuple-element.33.refs_3_, ...), custom_call_target="tpu_custom_call" | custom-call | flops 8388608 | bytes 8388608 | tf_op jit(solution)/shard_map/pallas_call | solution.py:403
  9.1 0.1 collective-permute-start.2
  9.2 1.2 %collective-permute-done.2.other = f32[96,128]{1,0:T(8,128)S(1)} collective-permute-done((f32[96,128]{1,0:T(8,128)S(1)}, f32[96,128]{1,0:T(8,128)S(1)}, u32[]{:S(2)}, u32[]{:S(2)}) %collective-permute-start.2) | collective-permute-done | bytes 49184 | tf_op jit(solution)/shard_map/ppermute | solution.py:363
  10.4 1.4 %collective-permute-start.3 = (f32[64,128]{1,0:T(8,128)S(1)}, f32[64,128]{1,0:T(8,128)S(1)}, u32[]{:S(2)}, u32[]{:S(2)}) collective-permute-start(f32[64,128]{1,0:T(8,128)S(1)} %get-tuple-element.46), channel_id=1, source_target_pairs={{0,1},{1,2},{2,3},{3,4},{4,5},{5,6},{6,7},{7,8},{8,9},{9,10},{10,1... | collective-permute-start | bytes 98312 | tf_op jit(solution)/shard_map/ppermute | solution.py:496
  11.9 0.0 collective-permute-start.4
  11.9 4.6 %collective-permute-done.4.far = f32[32,128]{1,0:T(8,128)S(1)} collective-permute-done((f32[32,128]{1,0:T(8,128)S(1)}, f32[32,128]{1,0:T(8,128)S(1)}, u32[]{:S(2)}, u32[]{:S(2)}) %collective-permute-start.4) | collective-permute-done | bytes 16416 | tf_op jit(solution)/shard_map/ppermute | solution.py:497
  16.5 0.0 collective-permute-done.3.near
  16.5 0.1 collective-permute-start.5
  16.6 1.2 %collective-permute-done.5.refs_15_ = f32[64,128]{1,0:T(8,128)S(1)} collective-permute-done((f32[64,128]{1,0:T(8,128)S(1)}, f32[64,128]{1,0:T(8,128)S(1)}, u32[]{:S(2)}, u32[]{:S(2)}) %collective-permute-start.5) | collective-permute-done | bytes 32800 | tf_op jit(solution)/shard_map/ppermute | solution.py:363
  17.8 1.8 %shard_map.141 = (f32[16,128]{1,0:T(8,128)S(1)}, f32[96,128]{1,0:T(8,128)S(1)}, f32[32,128]{1,0:T(8,128)S(1)}) custom-call(bf16[64,256,128]{2,1,0:T(8,128)(2,1)S(1)} %get-tuple-element.30.refs_0_, f32[24,128,128]{2,1,0:T(8,128)S(1)} %get-tuple-element.31.refs_1_, f32[24,128,128]{2,1,0:T(8,128)S(1)} %get-tuple-element.32.refs_2_, ...), custom_call_target="tpu_custom_call" | custom-call | flops 8388608 | bytes 8388608 | tf_op jit(solution)/shard_map/pallas_call | solution.py:403
  19.7 0.1 collective-permute-start.6
  19.7 1.2 %collective-permute-done.6.other = f32[96,128]{1,0:T(8,128)S(1)} collective-permute-done((f32[96,128]{1,0:T(8,128)S(1)}, f32[96,128]{1,0:T(8,128)S(1)}, u32[]{:S(2)}, u32[]{:S(2)}) %collective-permute-start.6) | collective-permute-done | bytes 49184 | tf_op jit(solution)/shard_map/ppermute | solution.py:363
  21.0 0.5 %collective-permute-start.8 = (f32[32,128]{1,0:T(8,128)S(1)}, f32[32,128]{1,0:T(8,128)S(1)}, u32[]{:S(2)}, u32[]{:S(2)}) collective-permute-start(f32[32,128]{1,0:T(8,128)S(1)} %get-tuple-element.53), channel_id=1, source_target_pairs={{0,1},{1,0},{2,3},{3,2},{4,5},{5,4},{6,7},{7,6},{8,9},{9,8},{10,11... | collective-permute-start | bytes 49160 | tf_op jit(solution)/shard_map/ppermute | solution.py:396
  21.5 0.8 %collective-permute-start.7 = (f32[32,128]{1,0:T(8,128)S(1)}, f32[32,128]{1,0:T(8,128)S(1)}, u32[]{:S(2)}, u32[]{:S(2)}) collective-permute-start(f32[32,128]{1,0:T(8,128)S(1)} %get-tuple-element.52), channel_id=1, source_target_pairs={{0,16},{1,2},{2,1},{3,4},{4,3},{5,6},{6,5},{7,8},{8,7},{9,10},{10,... | collective-permute-start | bytes 49160 | tf_op jit(solution)/shard_map/ppermute | solution.py:395
  22.3 0.6 %shard_map.142 = (f32[16,128]{1,0:T(8,128)}, f32[16,128]{1,0:T(8,128)}) custom-call(f32[16,128]{1,0:T(8,128)S(1)} %get-tuple-element.43.refs_11_.before, f32[16,128]{1,0:T(8,128)S(1)} %get-tuple-element.48.after), custom_call_target="tpu_custom_call" | custom-call | tf_op jit(solution)/shard_map/pallas_call | solution.py:403
  22.9 1.8 %collective-permute-done.8 = f32[32,128]{1,0:T(8,128)S(1)} collective-permute-done((f32[32,128]{1,0:T(8,128)S(1)}, f32[32,128]{1,0:T(8,128)S(1)}, u32[]{:S(2)}, u32[]{:S(2)}) %collective-permute-start.8) | collective-permute-done | bytes 16416 | tf_op jit(solution)/shard_map/ppermute | solution.py:396
  24.8 2.2 %collective-permute-done.7 = f32[32,128]{1,0:T(8,128)S(1)} collective-permute-done((f32[32,128]{1,0:T(8,128)S(1)}, f32[32,128]{1,0:T(8,128)S(1)}, u32[]{:S(2)}, u32[]{:S(2)}) %collective-permute-start.7) | collective-permute-done | bytes 16416 | tf_op jit(solution)/shard_map/ppermute | solution.py:395
  27.0 0.6 %add_multiply_fusion = (f32[32,128]{1,0:T(8,128)}, f32[32,128]{1,0:T(8,128)}) fusion(f32[32,128]{1,0:T(8,128)S(1)} %get-tuple-element.55, f32[32,128]{1,0:T(8,128)S(1)} %get-tuple-element.51, f32[32,128]{1,0:T(8,128)S(1)} %collective-permute-done.8, f32[32,128]{1,0:T(8,128)S(1)} %collective-permute-done.7, pred[]{:T(512)S(6)} %lt.3, pred[]{:T(512)S(6)} %eq.3, ...), kind=kLoop, calls=%fused_computation | loop fusion | flops 36864 | bytes 98307 | tf_op jit(solution)/shard_map/div | solution.py:519
  (3 shorter events, 0.0 us)
Async XLA Ops:
  0.6 6.6 %collective-permute-start = (f32[32,128]{1,0:T(8,128)}, f32[32,128]{1,0:T(8,128)S(1)}, u32[]{:S(2)}, u32[]{:S(2)}) collective-permute-start(f32[32,128]{1,0:T(8,128)} %dual.1), channel_id=1, source_target_pairs={{0,16},{1,2},{2,1},{3,4},{4,3},{5,6},{6,5},{7,8},{8,7},{9,10},{10,... | collective-permute-start | bytes 49160 | tf_op jit(solution)/shard_map/ppermute | solution.py:395
  3.0 4.2 %collective-permute-start.1 = (f32[32,128]{1,0:T(8,128)}, f32[32,128]{1,0:T(8,128)S(1)}, u32[]{:S(2)}, u32[]{:S(2)}) collective-permute-start(f32[32,128]{1,0:T(8,128)} %dual.1), channel_id=1, source_target_pairs={{0,1},{1,0},{2,3},{3,2},{4,5},{5,4},{6,7},{7,6},{8,9},{9,8},{10,11... | collective-permute-start | bytes 49160 | tf_op jit(solution)/shard_map/ppermute | solution.py:396
  9.1 1.3 %collective-permute-start.2 = (f32[96,128]{1,0:T(8,128)S(1)}, f32[96,128]{1,0:T(8,128)S(1)}, u32[]{:S(2)}, u32[]{:S(2)}) collective-permute-start(f32[96,128]{1,0:T(8,128)S(1)} %get-tuple-element.44.window), channel_id=1, source_target_pairs={{0,16},{1,17},{2,18},{3,19},{4,20},{5,21},{6,22},{7,23},{8,24},{9,... | collective-permute-start | bytes 147464 | tf_op jit(solution)/shard_map/ppermute | solution.py:363
  10.4 6.1 %collective-permute-start.3 = (f32[64,128]{1,0:T(8,128)S(1)}, f32[64,128]{1,0:T(8,128)S(1)}, u32[]{:S(2)}, u32[]{:S(2)}) collective-permute-start(f32[64,128]{1,0:T(8,128)S(1)} %get-tuple-element.46), channel_id=1, source_target_pairs={{0,1},{1,2},{2,3},{3,4},{4,5},{5,6},{6,7},{7,8},{8,9},{9,10},{10,1... | collective-permute-start | bytes 98312 | tf_op jit(solution)/shard_map/ppermute | solution.py:496
  11.9 4.6 %collective-permute-start.4 = (f32[32,128]{1,0:T(8,128)S(1)}, f32[32,128]{1,0:T(8,128)S(1)}, u32[]{:S(2)}, u32[]{:S(2)}) collective-permute-start(f32[32,128]{1,0:T(8,128)S(1)} %get-tuple-element.47), channel_id=1, source_target_pairs={{0,2},{1,3},{2,4},{3,5},{4,6},{5,7},{6,8},{7,9},{8,10},{9,11},{10,... | collective-permute-start | bytes 49160 | tf_op jit(solution)/shard_map/ppermute | solution.py:497
  16.5 1.3 %collective-permute-start.5 = (f32[64,128]{1,0:T(8,128)S(1)}, f32[64,128]{1,0:T(8,128)S(1)}, u32[]{:S(2)}, u32[]{:S(2)}) collective-permute-start(f32[64,128]{1,0:T(8,128)S(1)} %shard_map.140.refs_14_), channel_id=1, source_target_pairs={{0,16},{1,17},{2,18},{3,19},{4,20},{5,21},{6,22},{7,23},{8,24},{9,... | collective-permute-start | bytes 98312 | tf_op jit(solution)/shard_map/ppermute | solution.py:363
  19.7 1.3 %collective-permute-start.6 = (f32[96,128]{1,0:T(8,128)S(1)}, f32[96,128]{1,0:T(8,128)S(1)}, u32[]{:S(2)}, u32[]{:S(2)}) collective-permute-start(f32[96,128]{1,0:T(8,128)S(1)} %get-tuple-element.50.window), channel_id=1, source_target_pairs={{0,16},{1,17},{2,18},{3,19},{4,20},{5,21},{6,22},{7,23},{8,24},{9,... | collective-permute-start | bytes 147464 | tf_op jit(solution)/shard_map/ppermute | solution.py:363
  21.0 3.8 %collective-permute-start.8 = (f32[32,128]{1,0:T(8,128)S(1)}, f32[32,128]{1,0:T(8,128)S(1)}, u32[]{:S(2)}, u32[]{:S(2)}) collective-permute-start(f32[32,128]{1,0:T(8,128)S(1)} %get-tuple-element.53), channel_id=1, source_target_pairs={{0,1},{1,0},{2,3},{3,2},{4,5},{5,4},{6,7},{7,6},{8,9},{9,8},{10,11... | collective-permute-start | bytes 49160 | tf_op jit(solution)/shard_map/ppermute | solution.py:396
  21.5 5.5 %collective-permute-start.7 = (f32[32,128]{1,0:T(8,128)S(1)}, f32[32,128]{1,0:T(8,128)S(1)}, u32[]{:S(2)}, u32[]{:S(2)}) collective-permute-start(f32[32,128]{1,0:T(8,128)S(1)} %get-tuple-element.52), channel_id=1, source_target_pairs={{0,16},{1,2},{2,1},{3,4},{4,3},{5,6},{6,5},{7,8},{8,7},{9,10},{10,... | collective-permute-start | bytes 49160 | tf_op jit(solution)/shard_map/ppermute | solution.py:395
